TPU v7x, 256 devices: a whole 4x4x8 slice. The times are simulated.
256 devices in a mesh: dp: 8 (over y, core), ctx: 32 (over x, z).
Axes of the slice: x: 4, y: 4, z: 8, core: 2. Of those that a mesh axis runs over, the one named last changes fastest.
Arguments:
- queries: bfloat16 [8, 8192, 2560], P('dp', 'ctx'), may hold values from -120 to 120
- global_keys: bfloat16 [8, 8192, 512], P('dp', 'ctx'), may hold values from -5 to 5
- global_values: bfloat16 [8, 8192, 512], P('dp', 'ctx'), may hold values from -6 to 6
- out_grad: bfloat16 [8, 8192, 2560], P('dp', 'ctx'), may hold values from -6 to 6
- query_gain: float32 [2560], replicated, may hold values from 0.5 to 1.5
- doc_start: int32 [8, 64], P('dp', 'ctx'), may hold values from 0 to 63, as said below
Outputs:
- attn_out: bfloat16 [8, 8192, 2560], P('dp', 'ctx')
- query_grad: bfloat16 [8, 8192, 2560], P('dp', 'ctx')
- key_grad: bfloat16 [8, 8192, 512], P('dp', 'ctx')
- value_grad: bfloat16 [8, 8192, 512], P('dp', 'ctx')
- gain_grad: float32 [2560], replicated
Inputs may be any that keep to these rules, and one draw needn't show every extreme that they name: doc_start[g, b] is the first block of block b's document: it is at most b and at least b - 6, never falls along b, and equals b where a document begins; every slab has a document of exactly 7 blocks.
All inputs are finite; a program needn't handle non-finite values.
Results may differ from a plain program's by a relative error of at most 0.017.
The roundings to bfloat16 on the way count: a program that leaves them out, or rounds other values in their place, can miss the bound.
Values may be sent and summed in bfloat16 or wider, within the bound.
No kernel may reach another device: no remote copies, remote signals or barrier semaphores. Data moves between devices by JAX's collectives and lax.ppermute only.
A program may use at most 64 MiB of HBM per device.

v0:
```python
import math

import jax
import jax.numpy as jnp
from jax import lax
from jax.sharding import PartitionSpec as P

HD = 128
BLOCK = 128
REACH = 4


def shifted(value, axis, steps):
    count = lax.axis_size(axis)
    first, last = (max(0, -steps), min(count, count - steps))
    return lax.ppermute(value, axis, [(source, source + steps) for source in range(first, last)])


def head_group(inputs, allowed, factor):
    query_part, key_part, value_part, grad_part = inputs
    scores = (
        jnp.einsum("tgd,wd->gtw", query_part, key_part, preferred_element_type=jnp.float32) * factor
    )
    scores = jnp.where(allowed[None], scores, -jnp.inf)
    row_max = jnp.max(scores, axis=-1, keepdims=True)
    log_total = row_max + jnp.log(jnp.sum(jnp.exp(scores - row_max), axis=-1, keepdims=True))
    weights = jnp.exp(scores - log_total)
    weights_low = weights.astype(jnp.bfloat16)
    result = jnp.einsum(
        "gtw,wd->tgd", weights_low, value_part, preferred_element_type=jnp.float32
    ).astype(jnp.bfloat16)
    inner_sum = jnp.einsum("tgd,tgd->gt", grad_part, result, preferred_element_type=jnp.float32)
    dweights = jnp.einsum("tgd,wd->gtw", grad_part, value_part, preferred_element_type=jnp.float32)
    dscore_low = (weights * (dweights - inner_sum[..., None])).astype(jnp.bfloat16)
    dquery = (
        jnp.einsum("gtw,wd->tgd", dscore_low, key_part, preferred_element_type=jnp.float32) * factor
    )
    dkey = (
        jnp.einsum("gtw,tgd->wd", dscore_low, query_part, preferred_element_type=jnp.float32)
        * factor
    )
    dvalue = jnp.einsum("gtw,tgd->wd", weights_low, grad_part, preferred_element_type=jnp.float32)
    return (result, dquery, dkey, dvalue)


def local(queries, global_keys, global_values, out_grad, query_gain, doc_start):
    row_count = queries.shape[1]
    reach = REACH
    width = reach * row_count
    device = lax.axis_index("ctx")
    query_rows = queries[0]
    key_rows = global_keys[0]
    value_rows = global_values[0]
    grad_rows = out_grad[0]
    kv_count = key_rows.shape[1] // HD
    group_size = query_rows.shape[1] // (kv_count * HD)
    factor = 1.0 / math.sqrt(HD)
    scaled = (query_rows.astype(jnp.float32) * query_gain).astype(jnp.bfloat16)
    key_list = [key_rows]
    value_list = [value_rows]
    for distance in range(1, reach):
        far_keys, far_values = shifted((key_rows, value_rows), "ctx", distance)
        key_list.insert(0, far_keys)
        value_list.insert(0, far_values)
    window_keys = jnp.concatenate(key_list, axis=0)
    window_values = jnp.concatenate(value_list, axis=0)
    first_device = device - (reach - 1)
    query_pos = device * row_count + jnp.arange(row_count, dtype=jnp.int32)
    key_pos = first_device * row_count + jnp.arange(width, dtype=jnp.int32)
    begins = jnp.repeat(doc_start[0], BLOCK) * BLOCK
    allowed = (key_pos[None, :] <= query_pos[:, None]) & (key_pos[None, :] >= begins[:, None])
    query_four = scaled.reshape(row_count, kv_count, group_size, HD).transpose(1, 0, 2, 3)
    grad_four = grad_rows.reshape(row_count, kv_count, group_size, HD).transpose(1, 0, 2, 3)
    key_three = window_keys.reshape(width, kv_count, HD).transpose(1, 0, 2)
    value_three = window_values.reshape(width, kv_count, HD).transpose(1, 0, 2)
    results, dqueries, dkeys, dvalues = lax.map(
        lambda inputs: head_group(inputs, allowed, factor),
        (query_four, key_three, value_three, grad_four),
    )
    attn_out = results.transpose(1, 0, 2, 3).reshape(row_count, -1)
    dscaled = dqueries.transpose(1, 0, 2, 3).reshape(row_count, -1)

    def by_offset(partial_value):
        return partial_value.reshape(kv_count, reach, row_count, HD)[:, ::-1]

    key_offsets = by_offset(dkeys)
    value_offsets = by_offset(dvalues)
    key_total = key_offsets[:, 0]
    value_total = value_offsets[:, 0]
    for distance in range(1, reach):
        got_keys, got_values = shifted(
            (key_offsets[:, distance], value_offsets[:, distance]), "ctx", -distance
        )
        key_total = key_total + got_keys
        value_total = value_total + got_values
    key_grad = key_total.transpose(1, 0, 2).reshape(row_count, -1).astype(jnp.bfloat16)
    value_grad = value_total.transpose(1, 0, 2).reshape(row_count, -1).astype(jnp.bfloat16)
    query_grad = (dscaled * query_gain).astype(jnp.bfloat16)
    gain_term = jnp.sum(dscaled * query_rows.astype(jnp.float32), axis=0)
    gain_grad = lax.psum(gain_term, ("dp", "ctx"))
    return (attn_out[None], query_grad[None], key_grad[None], value_grad[None], gain_grad)


def solution(mesh):
    return jax.shard_map(
        local,
        mesh=mesh,
        in_specs=(
            P("dp", "ctx", None),
            P("dp", "ctx", None),
            P("dp", "ctx", None),
            P("dp", "ctx", None),
            P(),
            P("dp", "ctx"),
        ),
        out_specs=(
            P("dp", "ctx", None),
            P("dp", "ctx", None),
            P("dp", "ctx", None),
            P("dp", "ctx", None),
            P(),
        ),
        check_vma=False,
    )
```

profile of v0, /device:TPU:22, one launch (start us, length us, event | category | flops | bytes accessed | tf_op | source)
XLA Modules:
  0.0 340.2 jit_solution(1276972712751430127)
XLA Ops:
  1.7 3.8 %collective-permute-start.5 = (bf16[256,512]{0,1:T(8,128)(2,1)S(1)}, bf16[256,512]{0,1:T(8,128)(2,1)}, u32[]{:S(2)}, u32[]{:S(2)}) collective-permute-start(bf16[256,512]{0,1:T(8,128)(2,1)S(1)} %bitcast.227), channel_id=1, source_target_pairs={{0,1},{1,2},{2,3},{3,4},{4,5},{5,6},{6,7},{7,8},{8,9},{9,10},{10,1... | collective-permute-start | bytes 786440 | tf_op jit(solution)/shard_map/ppermute | solution.py:16
  5.6 5.2 %collective-permute-start.4 = (bf16[256,512]{0,1:T(8,128)(2,1)S(1)}, bf16[256,512]{0,1:T(8,128)(2,1)}, u32[]{:S(2)}, u32[]{:S(2)}) collective-permute-start(bf16[256,512]{0,1:T(8,128)(2,1)S(1)} %bitcast.228), channel_id=1, source_target_pairs={{0,2},{1,3},{2,4},{3,5},{4,6},{5,7},{6,8},{7,9},{8,10},{9,11},{10,... | collective-permute-start | bytes 786440 | tf_op jit(solution)/shard_map/ppermute | solution.py:16
  10.7 5.9 %collective-permute-start.3 = (bf16[256,512]{0,1:T(8,128)(2,1)S(1)}, bf16[256,512]{0,1:T(8,128)(2,1)}, u32[]{:S(2)}, u32[]{:S(2)}) collective-permute-start(bf16[256,512]{0,1:T(8,128)(2,1)S(1)} %bitcast.229), channel_id=1, source_target_pairs={{0,3},{1,4},{2,5},{3,6},{4,7},{5,8},{6,9},{7,10},{8,11},{9,12},{10... | collective-permute-start | bytes 786440 | tf_op jit(solution)/shard_map/ppermute | solution.py:16
  16.7 2.9 collective-permute-start.2
  25.7 25.4 %collective-permute-done.2 = bf16[256,512]{1,0:T(8,128)(2,1)S(1)} collective-permute-done((bf16[256,512]{1,0:T(8,128)(2,1)}, bf16[256,512]{1,0:T(8,128)(2,1)S(1)}, u32[]{:S(2)}, u32[]{:S(2)}) %collective-permute-start.2) | collective-permute-done | bytes 262176 | tf_op jit(solution)/shard_map/ppermute | solution.py:16
  51.1 16.0 %collective-permute-start = (bf16[256,512]{1,0:T(8,128)(2,1)S(1)}, bf16[256,512]{1,0:T(8,128)(2,1)}, u32[]{:S(2)}, u32[]{:S(2)}) collective-permute-start(bf16[256,512]{1,0:T(8,128)(2,1)S(1)} %bitcast.240), channel_id=1, source_target_pairs={{0,3},{1,4},{2,5},{3,6},{4,7},{5,8},{6,9},{7,10},{8,11},{9,12},{10... | collective-permute-start | bytes 786440 | tf_op jit(solution)/shard_map/ppermute | solution.py:16
  67.2 2.5 copy.42
  74.3 3.7 %collective-permute-done = bf16[256,512]{1,0:T(8,128)(2,1)} collective-permute-done((bf16[256,512]{1,0:T(8,128)(2,1)S(1)}, bf16[256,512]{1,0:T(8,128)(2,1)}, u32[]{:S(2)}, u32[]{:S(2)}) %collective-permute-start) | collective-permute-done | bytes 262176 | tf_op jit(solution)/shard_map/ppermute | solution.py:16
  80.2 68.0 %while.17 = (s32[]{:T(128)}, bf16[4,256,5,128]{1,3,2,0:T(8,128)(2,1)}, f32[4,256,5,128]{1,3,2,0:T(8,128)}, f32[4,1024,128]{2,1,0:T(8,128)}, f32[4,1024,128]{2,1,...) while((s32[]{:T(128)}, ...), condition=%wide.region_3.4_spmd.clone, body=%wide.region_0.3_spmd.clone.sunk | while | flops 2042689024 | bytes 49229988 | solution.py:76
  87.5 3.1 fusion.75
  90.6 2.6 fusion.72
  104.5 3.1 fusion.75
  107.6 2.6 fusion.72
  121.5 3.1 fusion.75
  124.6 2.6 fusion.72
  138.5 3.1 fusion.75
  141.7 2.6 fusion.72
  151.8 4.7 %collective-permute-start.11 = (f32[4,256,128]{2,0,1:T(4,128)S(1)}, f32[4,256,128]{2,0,1:T(4,128)S(1)}, u32[]{:S(2)}, u32[]{:S(2)}) collective-permute-start(f32[4,256,128]{2,0,1:T(4,128)S(1)} %bitcast.237), channel_id=1, source_target_pairs={{3,0},{4,1},{5,2},{6,3},{7,4},{8,5},{9,6},{10,7},{11,8},{12,9},{13... | collective-permute-start | bytes 1572872 | tf_op jit(solution)/shard_map/ppermute | solution.py:16
  158.4 3.8 %collective-permute-start.10 = (f32[4,256,128]{2,0,1:T(4,128)S(1)}, f32[4,256,128]{2,0,1:T(4,128)}, u32[]{:S(2)}, u32[]{:S(2)}) collective-permute-start(f32[4,256,128]{2,0,1:T(4,128)S(1)} %bitcast.235), channel_id=1, source_target_pairs={{2,0},{3,1},{4,2},{5,3},{6,4},{7,5},{8,6},{9,7},{10,8},{11,9},{12,... | collective-permute-start | bytes 1572872 | tf_op jit(solution)/shard_map/ppermute | solution.py:16
  165.4 5.2 %collective-permute-start.8 = (f32[4,256,128]{2,0,1:T(4,128)}, f32[4,256,128]{2,0,1:T(4,128)}, u32[]{:S(2)}, u32[]{:S(2)}) collective-permute-start(f32[4,256,128]{2,0,1:T(4,128)} %bitcast.171), channel_id=1, source_target_pairs={{3,0},{4,1},{5,2},{6,3},{7,4},{8,5},{9,6},{10,7},{11,8},{12,9},{13... | collective-permute-start | bytes 1572872 | tf_op jit(solution)/shard_map/ppermute | solution.py:16
  170.6 5.6 %collective-permute-start.6 = (f32[4,256,128]{2,0,1:T(4,128)}, f32[4,256,128]{2,0,1:T(4,128)}, u32[]{:S(2)}, u32[]{:S(2)}) collective-permute-start(f32[4,256,128]{2,0,1:T(4,128)} %bitcast.173), channel_id=1, source_target_pairs={{1,0},{2,1},{3,2},{4,3},{5,4},{6,5},{7,6},{8,7},{9,8},{10,9},{11,1... | collective-permute-start | bytes 1572872 | tf_op jit(solution)/shard_map/ppermute | solution.py:16
  176.2 15.0 %collective-permute-done.11 = f32[4,256,128]{2,0,1:T(4,128)S(1)} collective-permute-done((f32[4,256,128]{2,0,1:T(4,128)S(1)}, f32[4,256,128]{2,0,1:T(4,128)S(1)}, u32[]{:S(2)}, u32[]{:S(2)}) %collective-permute-start.11) | collective-permute-done | bytes 524320 | tf_op jit(solution)/shard_map/ppermute | solution.py:16
  191.2 5.3 %collective-permute-start.7 = (f32[4,256,128]{2,0,1:T(4,128)S(1)}, f32[4,256,128]{2,0,1:T(4,128)}, u32[]{:S(2)}, u32[]{:S(2)}) collective-permute-start(f32[4,256,128]{2,0,1:T(4,128)S(1)} %bitcast.236), channel_id=1, source_target_pairs={{2,0},{3,1},{4,2},{5,3},{6,4},{7,5},{8,6},{9,7},{10,8},{11,9},{12,... | collective-permute-start | bytes 1572872 | tf_op jit(solution)/shard_map/ppermute | solution.py:16
  201.0 133.8 %psum.7 = f32[2560]{0:T(1024)} all-reduce(f32[2560]{0:T(1024)S(1)} %reduce_sum.21), channel_id=1, replica_groups=mesh['dp'=8,'ctx'=32] {'dp','ctx'}, use_global_device_ids=true, to_apply=%region_5.6 | all-reduce | flops 2560 | bytes 20480 | tf_op jit(solution)/shard_map/psum | solution.py:100
  (122 shorter events, 77.3 us)
Async XLA Ops:
  1.7 70.3 %collective-permute-start.5 = (bf16[256,512]{0,1:T(8,128)(2,1)S(1)}, bf16[256,512]{0,1:T(8,128)(2,1)}, u32[]{:S(2)}, u32[]{:S(2)}) collective-permute-start(bf16[256,512]{0,1:T(8,128)(2,1)S(1)} %bitcast.227), channel_id=1, source_target_pairs={{0,1},{1,2},{2,3},{3,4},{4,5},{5,6},{6,7},{7,8},{8,9},{9,10},{10,1... | collective-permute-start | bytes 786440 | tf_op jit(solution)/shard_map/ppermute | solution.py:16
  5.6 66.5 %collective-permute-start.4 = (bf16[256,512]{0,1:T(8,128)(2,1)S(1)}, bf16[256,512]{0,1:T(8,128)(2,1)}, u32[]{:S(2)}, u32[]{:S(2)}) collective-permute-start(bf16[256,512]{0,1:T(8,128)(2,1)S(1)} %bitcast.228), channel_id=1, source_target_pairs={{0,2},{1,3},{2,4},{3,5},{4,6},{5,7},{6,8},{7,9},{8,10},{9,11},{10,... | collective-permute-start | bytes 786440 | tf_op jit(solution)/shard_map/ppermute | solution.py:16
  10.7 61.3 %collective-permute-start.3 = (bf16[256,512]{0,1:T(8,128)(2,1)S(1)}, bf16[256,512]{0,1:T(8,128)(2,1)}, u32[]{:S(2)}, u32[]{:S(2)}) collective-permute-start(bf16[256,512]{0,1:T(8,128)(2,1)S(1)} %bitcast.229), channel_id=1, source_target_pairs={{0,3},{1,4},{2,5},{3,6},{4,7},{5,8},{6,9},{7,10},{8,11},{9,12},{10... | collective-permute-start | bytes 786440 | tf_op jit(solution)/shard_map/ppermute | solution.py:16
  16.7 34.4 %collective-permute-start.2 = (bf16[256,512]{1,0:T(8,128)(2,1)}, bf16[256,512]{1,0:T(8,128)(2,1)S(1)}, u32[]{:S(2)}, u32[]{:S(2)}) collective-permute-start(bf16[256,512]{1,0:T(8,128)(2,1)} %bitcast.238), channel_id=1, source_target_pairs={{0,1},{1,2},{2,3},{3,4},{4,5},{5,6},{6,7},{7,8},{8,9},{9,10},{10,1... | collective-permute-start | bytes 786440 | tf_op jit(solution)/shard_map/ppermute | solution.py:16
  19.6 51.2 %collective-permute-start.1 = (bf16[256,512]{1,0:T(8,128)(2,1)}, bf16[256,512]{1,0:T(8,128)(2,1)}, u32[]{:S(2)}, u32[]{:S(2)}) collective-permute-start(bf16[256,512]{1,0:T(8,128)(2,1)} %bitcast.239), channel_id=1, source_target_pairs={{0,2},{1,3},{2,4},{3,5},{4,6},{5,7},{6,8},{7,9},{8,10},{9,11},{10,... | collective-permute-start | bytes 786440 | tf_op jit(solution)/shard_map/ppermute | solution.py:16
  23.9 45.8 %copy-start = (f32[1,256,2560]{1,2,0:T(8,128)}, f32[1,256,2560]{1,2,0:T(8,128)S(1)}, u32[]{:S(2)}) copy-start(f32[1,256,2560]{1,2,0:T(8,128)S(1)} %copy.41) | copy-start | bytes 7864324
  23.9 1.8 copy-start.10
  23.9 27.2 %copy-start.7 = (bf16[1,256,512]{2,1,0:T(8,128)(2,1)S(1)}, bf16[1,256,512]{2,1,0:T(8,128)(2,1)}, u32[]{:S(2)}) copy-start(bf16[1,256,512]{2,1,0:T(8,128)(2,1)} %param.10) | copy-start | bytes 786436
  51.1 16.0 %copy-start.8 = (bf16[256,512]{1,0:T(8,128)(2,1)}, bf16[256,512]{1,0:T(8,128)(2,1)S(1)}, u32[]{:S(2)}) copy-start(bf16[256,512]{1,0:T(8,128)(2,1)S(1)} %collective-permute-done.2) | copy-start | bytes 786436
  51.1 26.9 %collective-permute-start = (bf16[256,512]{1,0:T(8,128)(2,1)S(1)}, bf16[256,512]{1,0:T(8,128)(2,1)}, u32[]{:S(2)}, u32[]{:S(2)}) collective-permute-start(bf16[256,512]{1,0:T(8,128)(2,1)S(1)} %bitcast.240), channel_id=1, source_target_pairs={{0,3},{1,4},{2,5},{3,6},{4,7},{5,8},{6,9},{7,10},{8,11},{9,12},{10... | collective-permute-start | bytes 786440 | tf_op jit(solution)/shard_map/ppermute | solution.py:16
  70.8 9.4 %copy-start.2 = (bf16[4,256,5,128]{1,3,2,0:T(8,128)(2,1)S(1)}, bf16[4,256,5,128]{1,3,2,0:T(8,128)(2,1)}, u32[]{:S(2)}) copy-start(bf16[4,256,5,128]{1,3,2,0:T(8,128)(2,1)} %fusion.35) | copy-start | bytes 3932164
  84.0 1.2 copy-start.5
  101.0 1.2 copy-start.5
  149.9 12.3 %copy-start.3 = (f32[4,256,5,128]{1,3,2,0:T(8,128)S(1)}, f32[4,256,5,128]{1,3,2,0:T(8,128)}, u32[]{:S(2)}) copy-start(f32[4,256,5,128]{1,3,2,0:T(8,128)} %get-tuple-element.61) | copy-start | bytes 7864324
  149.9 12.3 %copy-start.9 = (f32[2560]{0:T(1024)S(1)}, f32[2560]{0:T(1024)}, u32[]{:S(2)}) copy-start(f32[2560]{0:T(1024)} %param.12) | copy-start | bytes 30724
  151.4 11.2 %copy-start.4 = (f32[4,1024,128]{2,1,0:T(8,128)S(1)}, f32[4,1024,128]{2,1,0:T(8,128)}, u32[]{:S(2)}) copy-start(f32[4,1024,128]{2,1,0:T(8,128)} %get-tuple-element.62) | copy-start | bytes 6291460
  151.8 39.4 %collective-permute-start.11 = (f32[4,256,128]{2,0,1:T(4,128)S(1)}, f32[4,256,128]{2,0,1:T(4,128)S(1)}, u32[]{:S(2)}, u32[]{:S(2)}) collective-permute-start(f32[4,256,128]{2,0,1:T(4,128)S(1)} %bitcast.237), channel_id=1, source_target_pairs={{3,0},{4,1},{5,2},{6,3},{7,4},{8,5},{9,6},{10,7},{11,8},{12,9},{13... | collective-permute-start | bytes 1572872 | tf_op jit(solution)/shard_map/ppermute | solution.py:16
  156.5 178.3 %collective-permute-start.9 = (f32[4,256,128]{2,0,1:T(4,128)}, f32[4,256,128]{2,0,1:T(4,128)}, u32[]{:S(2)}, u32[]{:S(2)}) collective-permute-start(f32[4,256,128]{2,0,1:T(4,128)} %bitcast.170), channel_id=1, source_target_pairs={{1,0},{2,1},{3,2},{4,3},{5,4},{6,5},{7,6},{8,7},{9,8},{10,9},{11,1... | collective-permute-start | bytes 1572872 | tf_op jit(solution)/shard_map/ppermute | solution.py:16
  158.4 176.4 %collective-permute-start.10 = (f32[4,256,128]{2,0,1:T(4,128)S(1)}, f32[4,256,128]{2,0,1:T(4,128)}, u32[]{:S(2)}, u32[]{:S(2)}) collective-permute-start(f32[4,256,128]{2,0,1:T(4,128)S(1)} %bitcast.235), channel_id=1, source_target_pairs={{2,0},{3,1},{4,2},{5,3},{6,4},{7,5},{8,6},{9,7},{10,8},{11,9},{12,... | collective-permute-start | bytes 1572872 | tf_op jit(solution)/shard_map/ppermute | solution.py:16
  162.8 33.7 %copy-start.1 = (f32[1,256,2560]{1,2,0:T(8,128)S(1)}, f32[1,256,2560]{1,2,0:T(8,128)}, u32[]{:S(2)}) copy-start(f32[1,256,2560]{1,2,0:T(8,128)} %copy-done) | copy-start | bytes 7864324
  165.4 172.1 %collective-permute-start.8 = (f32[4,256,128]{2,0,1:T(4,128)}, f32[4,256,128]{2,0,1:T(4,128)}, u32[]{:S(2)}, u32[]{:S(2)}) collective-permute-start(f32[4,256,128]{2,0,1:T(4,128)} %bitcast.171), channel_id=1, source_target_pairs={{3,0},{4,1},{5,2},{6,3},{7,4},{8,5},{9,6},{10,7},{11,8},{12,9},{13... | collective-permute-start | bytes 1572872 | tf_op jit(solution)/shard_map/ppermute | solution.py:16
  170.6 166.9 %collective-permute-start.6 = (f32[4,256,128]{2,0,1:T(4,128)}, f32[4,256,128]{2,0,1:T(4,128)}, u32[]{:S(2)}, u32[]{:S(2)}) collective-permute-start(f32[4,256,128]{2,0,1:T(4,128)} %bitcast.173), channel_id=1, source_target_pairs={{1,0},{2,1},{3,2},{4,3},{5,4},{6,5},{7,6},{8,7},{9,8},{10,9},{11,1... | collective-permute-start | bytes 1572872 | tf_op jit(solution)/shard_map/ppermute | solution.py:16
  191.2 5.3 %copy-start.6 = (f32[4,256,128]{2,0,1:T(4,128)}, f32[4,256,128]{2,0,1:T(4,128)S(1)}, u32[]{:S(2)}) copy-start(f32[4,256,128]{2,0,1:T(4,128)S(1)} %collective-permute-done.11) | copy-start | bytes 1572868
  191.2 146.3 %collective-permute-start.7 = (f32[4,256,128]{2,0,1:T(4,128)S(1)}, f32[4,256,128]{2,0,1:T(4,128)}, u32[]{:S(2)}, u32[]{:S(2)}) collective-permute-start(f32[4,256,128]{2,0,1:T(4,128)S(1)} %bitcast.236), channel_id=1, source_target_pairs={{2,0},{3,1},{4,2},{5,3},{6,4},{7,5},{8,6},{9,7},{10,8},{11,9},{12,... | collective-permute-start | bytes 1572872 | tf_op jit(solution)/shard_map/ppermute | solution.py:16
  (2 other events, 2.5 us)
where the time goes:
time: 345 us; the launch traced here: 340 us
  blocking collectives  134 us (39%)
  starting transfers between devices  62.2 us (18%)
  matrix products  55.5 us (16%)
  waiting for transfers between devices  44.1 us (13%)
  local copies, waits for them, and re-layouts  27.5 us (8%)
  other arithmetic  15.8 us (5%)
    psum x1, blocking collectives, local(): gain_grad = lax.psum(gain_term, ('dp', 'ctx'))  134 us
    ppermute x12, starting transfers between devices, shifted(): lax.ppermute(value, axis, [(source, source + steps) for source in range(f...  62.2 us
    ppermute x12, waiting for transfers between devices, shifted(): lax.ppermute(value, axis, [(source, source + steps) for source in range(f...  44.1 us
    dot_general x4, matrix products, head_group(): jnp.einsum('gtw,tgd->wd', weights_low, grad_part, preferred_element_type=...  12.5 us
    unnamed x31, local copies, waits for them, and re-layouts  12.2 us
    dot_general x4, matrix products, head_group(): jnp.einsum('tgd,wd->gtw', grad_part, value_part, preferred_element_type=j...  10.4 us
    dot_general x4, matrix products, head_group(): jnp.einsum('gtw,wd->tgd', dscore_low, key_part, preferred_element_type=jn...  9.25 us
    dot_general x4, matrix products, head_group(): jnp.einsum('gtw,wd->tgd', weights_low, value_part, preferred_element_type...  8.8 us
  transfers between devices with their start and end apart: 12, of which 3 were waited for; matrix products, arithmetic and copies ran while one was open for 6% of the time, Pallas kernels for 0%

commit v1 on v0

v1 whole, which is shorter than its diff:
```python
import functools
import math

import jax
import jax.numpy as jnp
from jax import lax
from jax.experimental import pallas as pl
from jax.experimental.pallas import tpu as pltpu
from jax.sharding import PartitionSpec as P

HD = 128
BLOCK = 128
REACH = 4
LOG2E = 1.4426950408889634


def shifted(value, axis, steps):
    count = lax.axis_size(axis)
    first, last = (max(0, -steps), min(count, count - steps))
    return lax.ppermute(value, axis, [(source, source + steps) for source in range(first, last)])


def all_sum(value, axis):
    count = lax.axis_size(axis)
    step = 1
    while step < count:
        value = value + lax.ppermute(value, axis, [(i, i ^ step) for i in range(count)])
        step *= 2
    return value


def dot(a, b, dims=((1,), (0,))):
    return lax.dot_general(a, b, (dims, ((), ())), preferred_element_type=jnp.float32)


def probs_kernel(group, rows, lo, q_ref, g_ref, gain_ref, *refs):
    k_refs, (p_ref, *dv_refs) = refs[:REACH], refs[REACH : 2 * REACH + 1]
    bias, k_all, p_low, g_all = refs[2 * REACH + 1 :]
    width = REACH * rows

    @pl.when(pl.program_id(0) == 0)
    def _():
        key = lax.broadcasted_iota(jnp.int32, (width, rows), 0)
        query = lax.broadcasted_iota(jnp.int32, (width, rows), 1)
        begin = jnp.where(query < BLOCK, lo[0], lo[1])
        allowed = (key >= begin) & (key <= query + (width - rows))
        bias[...] = jnp.where(allowed, 0.0, -jnp.inf)

    for j in range(REACH):
        k_all[j * rows : (j + 1) * rows, :] = k_refs[j][...]
    for g in range(group):
        cols = slice(g * HD, (g + 1) * HD)
        g_all[g * rows : (g + 1) * rows, :] = g_ref[:, cols]
        scaled = (q_ref[:, cols].astype(jnp.float32) * gain_ref[:, cols]).astype(jnp.bfloat16)
        raw = dot(k_all[...], scaled, ((1,), (1,))) + bias[...]
        top = jnp.max(raw, axis=0, keepdims=True)
        e = jnp.exp2((raw - top) * (LOG2E / math.sqrt(HD)))
        probs = e * (1.0 / jnp.sum(e, axis=0, keepdims=True))
        p_ref[g] = probs
        p_low[:, g * rows : (g + 1) * rows] = probs.astype(jnp.bfloat16)
    dv = dot(p_low[...], g_all[...])
    for j in range(REACH):
        dv_refs[j][...] = dv[j * rows : (j + 1) * rows, :]


def grads_kernel(group, rows, q_ref, g_ref, gain_ref, p_ref, *refs):
    k_refs, v_refs = refs[:REACH], refs[REACH : 2 * REACH]
    o_ref, dq_ref, gain_out, *dk_refs = refs[2 * REACH : 3 * REACH + 3]
    k_t, v_t, v_all, ds_all, q_all = refs[3 * REACH + 3 :]
    factor = 1.0 / math.sqrt(HD)
    for j in range(REACH):
        part = slice(j * rows, (j + 1) * rows)
        v_all[part, :] = v_refs[j][...]
        k_t[:, part] = k_refs[j][...].T
        v_t[:, part] = v_refs[j][...].T
    for g in range(group):
        cols = slice(g * HD, (g + 1) * HD)
        q32 = q_ref[:, cols].astype(jnp.float32)
        gain = gain_ref[:, cols]
        q_all[g * rows : (g + 1) * rows, :] = (q32 * gain).astype(jnp.bfloat16)
        probs = p_ref[g]
        out_t = dot(v_t[...], probs.astype(jnp.bfloat16)).astype(jnp.bfloat16)
        o_ref[:, cols] = out_t.T
        g_t = g_ref[:, cols].T
        delta = jnp.sum(g_t.astype(jnp.float32) * out_t.astype(jnp.float32), axis=0, keepdims=True)
        ds = (probs * (dot(v_all[...], g_t) - delta)).astype(jnp.bfloat16)
        ds_all[:, g * rows : (g + 1) * rows] = ds
        dscaled = (dot(k_t[...], ds) * factor).T
        dq_ref[:, cols] = (dscaled * gain).astype(jnp.bfloat16)
        gain_out[:, cols] = jnp.sum(dscaled * q32, axis=0, keepdims=True)
    dk = dot(ds_all[...], q_all[...]) * factor
    for j in range(REACH):
        dk_refs[j][...] = dk[j * rows : (j + 1) * rows, :]


def attention_probs(lo, queries, out_grad, gain, keys):
    rows, channels = queries.shape
    kv_channels = keys[0].shape[1]
    kv_count = kv_channels // HD
    group = channels // kv_channels
    width = REACH * rows
    wide = pl.BlockSpec((rows, group * HD), lambda c, lo: (0, c))
    thin = pl.BlockSpec((rows, HD), lambda c, lo: (0, c))
    return pl.pallas_call(
        functools.partial(probs_kernel, group, rows),
        out_shape=[jax.ShapeDtypeStruct((kv_count * group, width, rows), jnp.float32)]
        + [jax.ShapeDtypeStruct((rows, kv_channels), jnp.float32)] * REACH,
        grid_spec=pltpu.PrefetchScalarGridSpec(
            num_scalar_prefetch=1,
            grid=(kv_count,),
            in_specs=[wide, wide, pl.BlockSpec((1, group * HD), lambda c, lo: (0, c))]
            + [thin] * REACH,
            out_specs=[pl.BlockSpec((group, width, rows), lambda c, lo: (c, 0, 0))] + [thin] * REACH,
            scratch_shapes=[
                pltpu.VMEM((width, rows), jnp.float32),
                pltpu.VMEM((width, HD), jnp.bfloat16),
                pltpu.VMEM((width, group * rows), jnp.bfloat16),
                pltpu.VMEM((group * rows, HD), jnp.bfloat16),
            ],
        ),
        cost_estimate=pl.CostEstimate(
            flops=4 * kv_count * group * width * rows * HD,
            bytes_accessed=4 * kv_count * group * width * rows,
            transcendentals=kv_count * group * width * rows,
        ),
        name="probs",
    )(lo, queries, out_grad, gain, *keys)


def attention_grads(queries, out_grad, gain, probs, keys, values):
    rows, channels = queries.shape
    kv_channels = keys[0].shape[1]
    kv_count = kv_channels // HD
    group = channels // kv_channels
    width = REACH * rows
    wide = pl.BlockSpec((rows, group * HD), lambda c: (0, c))
    line = pl.BlockSpec((1, group * HD), lambda c: (0, c))
    thin = pl.BlockSpec((rows, HD), lambda c: (0, c))
    return pl.pallas_call(
        functools.partial(grads_kernel, group, rows),
        out_shape=[jax.ShapeDtypeStruct((rows, channels), jnp.bfloat16)] * 2
        + [jax.ShapeDtypeStruct((1, channels), jnp.float32)]
        + [jax.ShapeDtypeStruct((rows, kv_channels), jnp.float32)] * REACH,
        grid=(kv_count,),
        in_specs=[wide, wide, line, pl.BlockSpec((group, width, rows), lambda c: (c, 0, 0))]
        + [thin] * (2 * REACH),
        out_specs=[wide, wide, line] + [thin] * REACH,
        scratch_shapes=[
            pltpu.VMEM((HD, width), jnp.bfloat16),
            pltpu.VMEM((HD, width), jnp.bfloat16),
            pltpu.VMEM((width, HD), jnp.bfloat16),
            pltpu.VMEM((width, group * rows), jnp.bfloat16),
            pltpu.VMEM((group * rows, HD), jnp.bfloat16),
        ],
        cost_estimate=pl.CostEstimate(
            flops=8 * kv_count * group * width * rows * HD,
            bytes_accessed=4 * kv_count * group * width * rows,
            transcendentals=0,
        ),
        name="grads",
    )(queries, out_grad, gain, probs, *keys, *values)


def local(queries, global_keys, global_values, out_grad, query_gain, doc_start):
    rows = queries.shape[1]
    device = lax.axis_index("ctx")
    q, do = queries[0], out_grad[0]
    gain = query_gain[None]
    keys, values = [global_keys[0]], [global_values[0]]
    for _ in range(1, REACH):
        keys.insert(0, shifted(keys[0], "ctx", 1))
    for _ in range(1, REACH):
        values.insert(0, shifted(values[0], "ctx", 1))
    lo = doc_start[0] * BLOCK - (device - (REACH - 1)) * rows
    probs, *dv = attention_probs(lo, q, do, gain, keys)
    attn_out, query_grad, gain_term, *dk = attention_grads(q, do, gain, probs, keys, values)
    value_total = dv[0]
    for part in dv[1:]:
        value_total = shifted(value_total, "ctx", -1) + part
    key_total = dk[0]
    for part in dk[1:]:
        key_total = shifted(key_total, "ctx", -1) + part
    gain_grad = all_sum(all_sum(gain_term[0], "dp"), "ctx")
    return (
        attn_out[None],
        query_grad[None],
        key_total.astype(jnp.bfloat16)[None],
        value_total.astype(jnp.bfloat16)[None],
        gain_grad,
    )


def solution(mesh):
    rows = P("dp", "ctx", None)
    return jax.shard_map(
        local,
        mesh=mesh,
        in_specs=(rows, rows, rows, rows, P(), P("dp", "ctx")),
        out_specs=(rows, rows, rows, rows, P()),
        check_vma=False,
    )
```

time: 345 us -> 171 us (0.50); the launches traced: 340 us -> 171 us
  blocking collectives: 134 us -> 0 us
  matrix products: 55.5 us -> 0 us
  Pallas kernels: 0 us -> 34.7 us
  waiting for transfers between devices: 44.1 us -> 72.3 us
  local copies, waits for them, and re-layouts: 27.5 us -> 2.76 us
  other arithmetic: 15.8 us -> 4.8 us
  starting transfers between devices: 62.2 us -> 55.2 us
    psum x1 -> x0, blocking collectives: 134 us -> none  [local(): gain_grad = lax.psum(gain_term, ('dp', 'ctx'))]
    dot_general x24 -> x0, matrix products: 55.5 us -> none  [the longest x4 12.5 us: head_group(): jnp.einsum('gtw,tgd->wd', weights_low, grad_part, preferred_element_type=...]
    pallas_call x0 -> x2, Pallas kernels: none -> 34.7 us  [the longest x1 19.1 us: attention_grads(): pl.pallas_call(functools.partial(grads_kernel, group, rows), out_shape=[j...]
    ppermute x0 -> x8, waiting for transfers between devices: none -> 29 us  [all_sum(): lax.ppermute(value, axis, [(i, i ^ step) for i in range(count)])]
    ppermute x12, starting transfers between devices: 62.2 us -> 49.3 us  [shifted(): lax.ppermute(value, axis, [(source, source + steps) for source in range(f...]
    unnamed x31 -> x26, local copies, waits for them, and re-layouts: 12.2 us -> 1.44 us
    ppermute x0 -> x8, starting transfers between devices: none -> 5.94 us  [all_sum(): lax.ppermute(value, axis, [(i, i ^ step) for i in range(count)])]
    transpose x3 -> x0, other arithmetic: 5.09 us -> none  [the longest x1 2.22 us: local(): key_three = window_keys.reshape(width, kv_count, HD).transpose(1, 0, 2)]
  transfers between devices with their start and end apart: 12 -> 20, of which waited for: 3 -> 17; matrix products, arithmetic and copies ran while one was open for 6% -> 3% of each run, Pallas kernels for 0% -> 9%
where the time goes in v1:
time: 171 us
  waiting for transfers between devices  72.3 us (42%)
  starting transfers between devices  55.2 us (32%)
  Pallas kernels  34.7 us (20%)
  other arithmetic  4.8 us (3%)
  local copies, waits for them, and re-layouts  2.76 us (2%)
    ppermute x12, starting transfers between devices, shifted(): lax.ppermute(value, axis, [(source, source + steps) for source in range(f...  49.3 us
    ppermute x12, waiting for transfers between devices, shifted(): lax.ppermute(value, axis, [(source, source + steps) for source in range(f...  43.3 us
    ppermute x8, waiting for transfers between devices, all_sum(): lax.ppermute(value, axis, [(i, i ^ step) for i in range(count)])  29 us
    pallas_call x1, Pallas kernels, attention_grads(): pl.pallas_call(functools.partial(grads_kernel, group, rows), out_shape=[j...  19.1 us
    pallas_call x1, Pallas kernels, attention_probs(): pl.pallas_call(functools.partial(probs_kernel, group, rows), out_shape=[j...  15.7 us
    ppermute x8, starting transfers between devices, all_sum(): lax.ppermute(value, axis, [(i, i ^ step) for i in range(count)])  5.94 us
  transfers between devices with their start and end apart: 20, of which 17 were waited for; matrix products, arithmetic and copies ran while one was open for 3% of the time, Pallas kernels for 9%

profile of v1, /device:TPU:22, one launch (start us, length us, event | category | flops | bytes accessed | tf_op | source)
XLA Modules:
  0.0 170.6 jit_solution(1842890710871884623)
XLA Ops:
  0.6 3.8 %collective-permute-start = (bf16[256,512]{1,0:T(8,128)(2,1)}, bf16[256,512]{1,0:T(8,128)(2,1)S(1)}, u32[]{:S(2)}, u32[]{:S(2)}) collective-permute-start(bf16[256,512]{1,0:T(8,128)(2,1)} %bitcast.16), channel_id=1, source_target_pairs={{0,1},{1,2},{2,3},{3,4},{4,5},{5,6},{6,7},{7,8},{8,9},{9,10},{10,1... | collective-permute-start | bytes 786440 | tf_op jit(solution)/shard_map/ppermute | solution.py:20
  4.5 3.8 %collective-permute-start.3 = (bf16[256,512]{1,0:T(8,128)(2,1)}, bf16[256,512]{1,0:T(8,128)(2,1)S(1)}, u32[]{:S(2)}, u32[]{:S(2)}) collective-permute-start(bf16[256,512]{1,0:T(8,128)(2,1)} %bitcast.19), channel_id=1, source_target_pairs={{0,1},{1,2},{2,3},{3,4},{4,5},{5,6},{6,7},{7,8},{8,9},{9,10},{10,1... | collective-permute-start | bytes 786440 | tf_op jit(solution)/shard_map/ppermute | solution.py:20
  8.3 7.7 %collective-permute-done.refs_2_ = bf16[256,512]{1,0:T(8,128)(2,1)S(1)} collective-permute-done((bf16[256,512]{1,0:T(8,128)(2,1)}, bf16[256,512]{1,0:T(8,128)(2,1)S(1)}, u32[]{:S(2)}, u32[]{:S(2)}) %collective-permute-start) | collective-permute-done | bytes 262176 | tf_op jit(solution)/shard_map/ppermute | solution.py:20
  17.9 2.8 %collective-permute-done.3.refs_6_ = bf16[256,512]{1,0:T(8,128)(2,1)S(1)} collective-permute-done((bf16[256,512]{1,0:T(8,128)(2,1)}, bf16[256,512]{1,0:T(8,128)(2,1)S(1)}, u32[]{:S(2)}, u32[]{:S(2)}) %collective-permute-start.3) | collective-permute-done | bytes 262176 | tf_op jit(solution)/shard_map/ppermute | solution.py:20
  22.7 3.9 %collective-permute-done.1.refs_1_ = bf16[256,512]{1,0:T(8,128)(2,1)S(1)} collective-permute-done((bf16[256,512]{1,0:T(8,128)(2,1)S(1)}, bf16[256,512]{1,0:T(8,128)(2,1)S(1)}, u32[]{:S(2)}, u32[]{:S(2)}) %collective-permute-start.1) | collective-permute-done | bytes 262176 | tf_op jit(solution)/shard_map/ppermute | solution.py:20
  28.6 5.2 %collective-permute-done.4.refs_5_ = bf16[256,512]{1,0:T(8,128)(2,1)S(1)} collective-permute-done((bf16[256,512]{1,0:T(8,128)(2,1)S(1)}, bf16[256,512]{1,0:T(8,128)(2,1)S(1)}, u32[]{:S(2)}, u32[]{:S(2)}) %collective-permute-start.4) | collective-permute-done | bytes 262176 | tf_op jit(solution)/shard_map/ppermute | solution.py:20
  39.2 15.7 %probs.1 = (f32[20,1024,256]{2,1,0:T(8,128)}, f32[256,512]{1,0:T(8,128)}, f32[256,512]{1,0:T(8,128)}, f32[256,512]{1,0:T(8,128)}, f32[256,512]{1,0:T(8,128)}) custom-call(s32[2]{0:T(128)} %subtract_bitcast_fusion.lo, bf16[256,2560]{1,0:T(8,128)(2,1)} %bitcast.12, bf16[256,2560]{1,0:T(8,128)(2,1)} %bitcast.14, f32[1,2560]{1,0:T(1,128)} %broadcast_in_dim.15.gain_ref, ...), custom_call_target="tpu_custom_call" | custom-call | flops 2684354560 | bytes 20971520 | tf_op jit(solution)/shard_map/probs/pallas_call | solution.py:104
  55.6 19.1 %grads.1 = (bf16[256,2560]{1,0:T(8,128)(2,1)}, bf16[256,2560]{1,0:T(8,128)(2,1)}, f32[1,2560]{1,0:T(1,128)}, f32[256,512]{1,0:T(8,128)}, f32[256,512]{1,0:T(8,12...) custom-call(bf16[256,2560]{1,0:T(8,128)(2,1)} %bitcast.13, bf16[256,2560]{1,0:T(8,128)(2,1)} %bitcast.15, ...), custom_call_target="tpu_custom_call" | custom-call | flops 5368709120 | bytes 20971520 | tf_op jit(solution)/shard_map/grads/pallas_call | solution.py:139
  74.7 5.8 %collective-permute-start.6 = (f32[256,512]{1,0:T(8,128)}, f32[256,512]{1,0:T(8,128)S(1)}, u32[]{:S(2)}, u32[]{:S(2)}) collective-permute-start(f32[256,512]{1,0:T(8,128)} %get-tuple-element.20), channel_id=1, source_target_pairs={{1,0},{2,1},{3,2},{4,3},{5,4},{6,5},{7,6},{8,7},{9,8},{10,9},{11,1... | collective-permute-start | bytes 1572872 | tf_op jit(solution)/shard_map/ppermute | solution.py:20
  82.5 10.7 %collective-permute-done.6 = f32[256,512]{1,0:T(8,128)S(1)} collective-permute-done((f32[256,512]{1,0:T(8,128)}, f32[256,512]{1,0:T(8,128)S(1)}, u32[]{:S(2)}, u32[]{:S(2)}) %collective-permute-start.6) | collective-permute-done | bytes 524320 | tf_op jit(solution)/shard_map/ppermute | solution.py:20
  94.3 6.4 %collective-permute-start.7 = (f32[256,512]{1,0:T(8,128)S(1)}, f32[256,512]{1,0:T(8,128)S(1)}, u32[]{:S(2)}, u32[]{:S(2)}) collective-permute-start(f32[256,512]{1,0:T(8,128)S(1)} %add.43), channel_id=1, source_target_pairs={{1,0},{2,1},{3,2},{4,3},{5,4},{6,5},{7,6},{8,7},{9,8},{10,9},{11,1... | collective-permute-start | bytes 1572872 | tf_op jit(solution)/shard_map/ppermute | solution.py:20
  100.7 3.5 %collective-permute-done.9 = f32[256,512]{1,0:T(8,128)S(1)} collective-permute-done((f32[256,512]{1,0:T(8,128)S(1)}, f32[256,512]{1,0:T(8,128)S(1)}, u32[]{:S(2)}, u32[]{:S(2)}) %collective-permute-start.9) | collective-permute-done | bytes 524320 | tf_op jit(solution)/shard_map/ppermute | solution.py:20
  104.3 6.6 %collective-permute-start.10 = (f32[256,512]{1,0:T(8,128)S(1)}, f32[256,512]{1,0:T(8,128)S(1)}, u32[]{:S(2)}, u32[]{:S(2)}) collective-permute-start(f32[256,512]{1,0:T(8,128)S(1)} %add.46), channel_id=1, source_target_pairs={{1,0},{2,1},{3,2},{4,3},{5,4},{6,5},{7,6},{8,7},{9,8},{10,9},{11,1... | collective-permute-start | bytes 1572872 | tf_op jit(solution)/shard_map/ppermute | solution.py:20
  111.0 4.5 %collective-permute-done.7 = f32[256,512]{1,0:T(8,128)S(1)} collective-permute-done((f32[256,512]{1,0:T(8,128)S(1)}, f32[256,512]{1,0:T(8,128)S(1)}, u32[]{:S(2)}, u32[]{:S(2)}) %collective-permute-start.7) | collective-permute-done | bytes 524320 | tf_op jit(solution)/shard_map/ppermute | solution.py:20
  115.6 6.6 %collective-permute-start.8 = (f32[256,512]{1,0:T(8,128)S(1)}, f32[256,512]{1,0:T(8,128)S(1)}, u32[]{:S(2)}, u32[]{:S(2)}) collective-permute-start(f32[256,512]{1,0:T(8,128)S(1)} %add.44), channel_id=1, source_target_pairs={{1,0},{2,1},{3,2},{4,3},{5,4},{6,5},{7,6},{8,7},{9,8},{10,9},{11,1... | collective-permute-start | bytes 1572872 | tf_op jit(solution)/shard_map/ppermute | solution.py:20
  122.2 4.5 %collective-permute-done.10 = f32[256,512]{1,0:T(8,128)S(1)} collective-permute-done((f32[256,512]{1,0:T(8,128)S(1)}, f32[256,512]{1,0:T(8,128)S(1)}, u32[]{:S(2)}, u32[]{:S(2)}) %collective-permute-start.10) | collective-permute-done | bytes 524320 | tf_op jit(solution)/shard_map/ppermute | solution.py:20
  126.8 6.6 %collective-permute-start.11 = (f32[256,512]{1,0:T(8,128)S(1)}, f32[256,512]{1,0:T(8,128)S(1)}, u32[]{:S(2)}, u32[]{:S(2)}) collective-permute-start(f32[256,512]{1,0:T(8,128)S(1)} %add.47), channel_id=1, source_target_pairs={{1,0},{2,1},{3,2},{4,3},{5,4},{6,5},{7,6},{8,7},{9,8},{10,9},{11,1... | collective-permute-start | bytes 1572872 | tf_op jit(solution)/shard_map/ppermute | solution.py:20
  138.8 4.9 %collective-permute-done.14 = f32[2560]{0:T(1024)S(1)} collective-permute-done((f32[2560]{0:T(1024)S(1)}, f32[2560]{0:T(1024)S(1)}, u32[]{:S(2)}, u32[]{:S(2)}) %collective-permute-start.14) | collective-permute-done | bytes 10272 | tf_op jit(solution)/shard_map/ppermute | solution.py:27
  143.7 3.7 %collective-permute-done.15 = f32[2560]{0:T(1024)S(1)} collective-permute-done((f32[2560]{0:T(1024)S(1)}, f32[2560]{0:T(1024)S(1)}, u32[]{:S(2)}, u32[]{:S(2)}) %collective-permute-start.15) | collective-permute-done | bytes 10272 | tf_op jit(solution)/shard_map/ppermute | solution.py:27
  147.4 4.6 %collective-permute-done.16 = f32[2560]{0:T(1024)S(1)} collective-permute-done((f32[2560]{0:T(1024)S(1)}, f32[2560]{0:T(1024)S(1)}, u32[]{:S(2)}, u32[]{:S(2)}) %collective-permute-start.16) | collective-permute-done | bytes 10272 | tf_op jit(solution)/shard_map/ppermute | solution.py:27
  152.0 2.5 %collective-permute-start.17 = (f32[2560]{0:T(1024)S(1)}, f32[2560]{0:T(1024)S(1)}, u32[]{:S(2)}, u32[]{:S(2)}) collective-permute-start(f32[2560]{0:T(1024)S(1)} %add.53), channel_id=1, source_target_pairs={{0,4},{1,5},{2,6},{3,7},{4,0},{5,1},{6,2},{7,3},{8,12},{9,13},{10,... | collective-permute-start | bytes 30728 | tf_op jit(solution)/shard_map/ppermute | solution.py:27
  154.5 5.1 %collective-permute-done.17 = f32[2560]{0:T(1024)S(1)} collective-permute-done((f32[2560]{0:T(1024)S(1)}, f32[2560]{0:T(1024)S(1)}, u32[]{:S(2)}, u32[]{:S(2)}) %collective-permute-start.17) | collective-permute-done | bytes 10272 | tf_op jit(solution)/shard_map/ppermute | solution.py:27
  160.2 3.1 %collective-permute-done.18 = f32[2560]{0:T(1024)S(1)} collective-permute-done((f32[2560]{0:T(1024)S(1)}, f32[2560]{0:T(1024)S(1)}, u32[]{:S(2)}, u32[]{:S(2)}) %collective-permute-start.18) | collective-permute-done | bytes 10272 | tf_op jit(solution)/shard_map/ppermute | solution.py:27
  164.4 4.0 %collective-permute-done.19 = f32[2560]{0:T(1024)S(1)} collective-permute-done((f32[2560]{0:T(1024)S(1)}, f32[2560]{0:T(1024)S(1)}, u32[]{:S(2)}, u32[]{:S(2)}) %collective-permute-start.19) | collective-permute-done | bytes 10272 | tf_op jit(solution)/shard_map/ppermute | solution.py:27
  (61 shorter events, 24.5 us)
Async XLA Ops:
  0.6 15.4 %collective-permute-start = (bf16[256,512]{1,0:T(8,128)(2,1)}, bf16[256,512]{1,0:T(8,128)(2,1)S(1)}, u32[]{:S(2)}, u32[]{:S(2)}) collective-permute-start(bf16[256,512]{1,0:T(8,128)(2,1)} %bitcast.16), channel_id=1, source_target_pairs={{0,1},{1,2},{2,3},{3,4},{4,5},{5,6},{6,7},{7,8},{8,9},{9,10},{10,1... | collective-permute-start | bytes 786440 | tf_op jit(solution)/shard_map/ppermute | solution.py:20
  4.5 16.3 %collective-permute-start.3 = (bf16[256,512]{1,0:T(8,128)(2,1)}, bf16[256,512]{1,0:T(8,128)(2,1)S(1)}, u32[]{:S(2)}, u32[]{:S(2)}) collective-permute-start(bf16[256,512]{1,0:T(8,128)(2,1)} %bitcast.19), channel_id=1, source_target_pairs={{0,1},{1,2},{2,3},{3,4},{4,5},{5,6},{6,7},{7,8},{8,9},{9,10},{10,1... | collective-permute-start | bytes 786440 | tf_op jit(solution)/shard_map/ppermute | solution.py:20
  16.0 10.6 %collective-permute-start.1 = (bf16[256,512]{1,0:T(8,128)(2,1)S(1)}, bf16[256,512]{1,0:T(8,128)(2,1)S(1)}, u32[]{:S(2)}, u32[]{:S(2)}) collective-permute-start(bf16[256,512]{1,0:T(8,128)(2,1)S(1)} %collective-permute-done.refs_2_), channel_id=1, source_target_pairs={{0,1},{1,2},{2,3},{3,4},{4,5},{5,6},{6,7},{7,8},{8,9},{9,10},{10,1... | collective-permute-start | bytes 786440 | tf_op jit(solution)/shard_map/ppermute | solution.py:20
  20.8 34.1 %copy-start.6 = (bf16[256,512]{1,0:T(8,128)(2,1)}, bf16[256,512]{1,0:T(8,128)(2,1)S(1)}, u32[]{:S(2)}) copy-start(bf16[256,512]{1,0:T(8,128)(2,1)S(1)} %collective-permute-done.3.refs_6_) | copy-start | bytes 786436
  20.8 12.9 %collective-permute-start.4 = (bf16[256,512]{1,0:T(8,128)(2,1)S(1)}, bf16[256,512]{1,0:T(8,128)(2,1)S(1)}, u32[]{:S(2)}, u32[]{:S(2)}) collective-permute-start(bf16[256,512]{1,0:T(8,128)(2,1)S(1)} %collective-permute-done.3.refs_6_), channel_id=1, source_target_pairs={{0,1},{1,2},{2,3},{3,4},{4,5},{5,6},{6,7},{7,8},{8,9},{9,10},{10,1... | collective-permute-start | bytes 786440 | tf_op jit(solution)/shard_map/ppermute | solution.py:20
  26.6 11.9 %collective-permute-start.2 = (bf16[256,512]{1,0:T(8,128)(2,1)S(1)}, bf16[256,512]{1,0:T(8,128)(2,1)S(1)}, u32[]{:S(2)}, u32[]{:S(2)}) collective-permute-start(bf16[256,512]{1,0:T(8,128)(2,1)S(1)} %collective-permute-done.1.refs_1_), channel_id=1, source_target_pairs={{0,1},{1,2},{2,3},{3,4},{4,5},{5,6},{6,7},{7,8},{8,9},{9,10},{10,1... | collective-permute-start | bytes 786440 | tf_op jit(solution)/shard_map/ppermute | solution.py:20
  33.7 21.1 %collective-permute-start.5 = (bf16[256,512]{1,0:T(8,128)(2,1)S(1)}, bf16[256,512]{1,0:T(8,128)(2,1)S(1)}, u32[]{:S(2)}, u32[]{:S(2)}) collective-permute-start(bf16[256,512]{1,0:T(8,128)(2,1)S(1)} %collective-permute-done.4.refs_5_), channel_id=1, source_target_pairs={{0,1},{1,2},{2,3},{3,4},{4,5},{5,6},{6,7},{7,8},{8,9},{9,10},{10,1... | collective-permute-start | bytes 786440 | tf_op jit(solution)/shard_map/ppermute | solution.py:20
  74.7 29.6 %copy-start.2 = (f32[256,512]{1,0:T(8,128)S(1)}, f32[256,512]{1,0:T(8,128)}, u32[]{:S(2)}) copy-start(f32[256,512]{1,0:T(8,128)} %get-tuple-element.25) | copy-start | bytes 1572868
  74.7 18.4 %collective-permute-start.6 = (f32[256,512]{1,0:T(8,128)}, f32[256,512]{1,0:T(8,128)S(1)}, u32[]{:S(2)}, u32[]{:S(2)}) collective-permute-start(f32[256,512]{1,0:T(8,128)} %get-tuple-element.20), channel_id=1, source_target_pairs={{1,0},{2,1},{3,2},{4,3},{5,4},{6,5},{7,6},{8,7},{9,8},{10,9},{11,1... | collective-permute-start | bytes 1572872 | tf_op jit(solution)/shard_map/ppermute | solution.py:20
  80.5 23.7 %collective-permute-start.9 = (f32[256,512]{1,0:T(8,128)S(1)}, f32[256,512]{1,0:T(8,128)S(1)}, u32[]{:S(2)}, u32[]{:S(2)}) collective-permute-start(f32[256,512]{1,0:T(8,128)S(1)} %copy-done.12), channel_id=1, source_target_pairs={{1,0},{2,1},{3,2},{4,3},{5,4},{6,5},{7,6},{8,7},{9,8},{10,9},{11,1... | collective-permute-start | bytes 1572872 | tf_op jit(solution)/shard_map/ppermute | solution.py:20
  94.3 21.2 %collective-permute-start.7 = (f32[256,512]{1,0:T(8,128)S(1)}, f32[256,512]{1,0:T(8,128)S(1)}, u32[]{:S(2)}, u32[]{:S(2)}) collective-permute-start(f32[256,512]{1,0:T(8,128)S(1)} %add.43), channel_id=1, source_target_pairs={{1,0},{2,1},{3,2},{4,3},{5,4},{6,5},{7,6},{8,7},{9,8},{10,9},{11,1... | collective-permute-start | bytes 1572872 | tf_op jit(solution)/shard_map/ppermute | solution.py:20
  104.3 22.4 %collective-permute-start.10 = (f32[256,512]{1,0:T(8,128)S(1)}, f32[256,512]{1,0:T(8,128)S(1)}, u32[]{:S(2)}, u32[]{:S(2)}) collective-permute-start(f32[256,512]{1,0:T(8,128)S(1)} %add.46), channel_id=1, source_target_pairs={{1,0},{2,1},{3,2},{4,3},{5,4},{6,5},{7,6},{8,7},{9,8},{10,9},{11,1... | collective-permute-start | bytes 1572872 | tf_op jit(solution)/shard_map/ppermute | solution.py:20
  115.6 53.5 %copy-start.4 = (f32[256,512]{1,0:T(8,128)S(1)}, f32[256,512]{1,0:T(8,128)}, u32[]{:S(2)}) copy-start(f32[256,512]{1,0:T(8,128)} %get-tuple-element.23) | copy-start | bytes 1572868
  115.6 53.5 %collective-permute-start.8 = (f32[256,512]{1,0:T(8,128)S(1)}, f32[256,512]{1,0:T(8,128)S(1)}, u32[]{:S(2)}, u32[]{:S(2)}) collective-permute-start(f32[256,512]{1,0:T(8,128)S(1)} %add.44), channel_id=1, source_target_pairs={{1,0},{2,1},{3,2},{4,3},{5,4},{6,5},{7,6},{8,7},{9,8},{10,9},{11,1... | collective-permute-start | bytes 1572872 | tf_op jit(solution)/shard_map/ppermute | solution.py:20
  126.7 43.1 %copy-start.3 = (f32[256,512]{1,0:T(8,128)S(1)}, f32[256,512]{1,0:T(8,128)}, u32[]{:S(2)}) copy-start(f32[256,512]{1,0:T(8,128)} %get-tuple-element.27) | copy-start | bytes 1572868
  126.8 43.1 %collective-permute-start.11 = (f32[256,512]{1,0:T(8,128)S(1)}, f32[256,512]{1,0:T(8,128)S(1)}, u32[]{:S(2)}, u32[]{:S(2)}) collective-permute-start(f32[256,512]{1,0:T(8,128)S(1)} %add.47), channel_id=1, source_target_pairs={{1,0},{2,1},{3,2},{4,3},{5,4},{6,5},{7,6},{8,7},{9,8},{10,9},{11,1... | collective-permute-start | bytes 1572872 | tf_op jit(solution)/shard_map/ppermute | solution.py:20
  133.5 1.3 collective-permute-start.12
  134.8 3.7 %collective-permute-start.13 = (f32[2560]{0:T(1024)S(1)}, f32[2560]{0:T(1024)S(1)}, u32[]{:S(2)}, u32[]{:S(2)}) collective-permute-start(f32[2560]{0:T(1024)S(1)} %add.49), channel_id=1, source_target_pairs={{0,64},{32,96},{64,0},{96,32},{128,192},{160,224},{192,128},{224,1... | collective-permute-start | bytes 30728 | tf_op jit(solution)/shard_map/ppermute | solution.py:27
  138.5 5.2 %collective-permute-start.14 = (f32[2560]{0:T(1024)S(1)}, f32[2560]{0:T(1024)S(1)}, u32[]{:S(2)}, u32[]{:S(2)}) collective-permute-start(f32[2560]{0:T(1024)S(1)} %add.50), channel_id=1, source_target_pairs={{0,128},{32,160},{64,192},{96,224},{128,0},{160,32},{192,64},{224,... | collective-permute-start | bytes 30728 | tf_op jit(solution)/shard_map/ppermute | solution.py:27
  143.7 3.7 %collective-permute-start.15 = (f32[2560]{0:T(1024)S(1)}, f32[2560]{0:T(1024)S(1)}, u32[]{:S(2)}, u32[]{:S(2)}) collective-permute-start(f32[2560]{0:T(1024)S(1)} %add.51), channel_id=1, source_target_pairs={{0,1},{1,0},{2,3},{3,2},{4,5},{5,4},{6,7},{7,6},{8,9},{9,8},{10,11... | collective-permute-start | bytes 30728 | tf_op jit(solution)/shard_map/ppermute | solution.py:27
  147.4 4.6 %collective-permute-start.16 = (f32[2560]{0:T(1024)S(1)}, f32[2560]{0:T(1024)S(1)}, u32[]{:S(2)}, u32[]{:S(2)}) collective-permute-start(f32[2560]{0:T(1024)S(1)} %add.52), channel_id=1, source_target_pairs={{0,2},{1,3},{2,0},{3,1},{4,6},{5,7},{6,4},{7,5},{8,10},{9,11},{10,... | collective-permute-start | bytes 30728 | tf_op jit(solution)/shard_map/ppermute | solution.py:27
  152.0 7.6 %collective-permute-start.17 = (f32[2560]{0:T(1024)S(1)}, f32[2560]{0:T(1024)S(1)}, u32[]{:S(2)}, u32[]{:S(2)}) collective-permute-start(f32[2560]{0:T(1024)S(1)} %add.53), channel_id=1, source_target_pairs={{0,4},{1,5},{2,6},{3,7},{4,0},{5,1},{6,2},{7,3},{8,12},{9,13},{10,... | collective-permute-start | bytes 30728 | tf_op jit(solution)/shard_map/ppermute | solution.py:27
  159.6 3.7 %collective-permute-start.18 = (f32[2560]{0:T(1024)S(1)}, f32[2560]{0:T(1024)S(1)}, u32[]{:S(2)}, u32[]{:S(2)}) collective-permute-start(f32[2560]{0:T(1024)S(1)} %add.54), channel_id=1, source_target_pairs={{0,8},{1,9},{2,10},{3,11},{4,12},{5,13},{6,14},{7,15},{8,0},{9,1},... | collective-permute-start | bytes 30728 | tf_op jit(solution)/shard_map/ppermute | solution.py:27
  163.3 5.2 %collective-permute-start.19 = (f32[2560]{0:T(1024)S(1)}, f32[2560]{0:T(1024)S(1)}, u32[]{:S(2)}, u32[]{:S(2)}) collective-permute-start(f32[2560]{0:T(1024)S(1)} %add.55), channel_id=1, source_target_pairs={{0,16},{1,17},{2,18},{3,19},{4,20},{5,21},{6,22},{7,23},{8,24},{9,... | collective-permute-start | bytes 30728 | tf_op jit(solution)/shard_map/ppermute | solution.py:27
  (9 other events, 144.6 us)

commit v2 on v1

--- a/solution.py
+++ b/solution.py
@@ -8,25 +8,46 @@
 from jax.experimental.pallas import tpu as pltpu
 from jax.sharding import PartitionSpec as P
 
+
 HD = 128
 BLOCK = 128
 REACH = 4
 LOG2E = 1.4426950408889634
-
-
-def shifted(value, axis, steps):
-    count = lax.axis_size(axis)
+SCALE_STEPS = 64.0
+SCALE_ROWS = 16
+CODE_MAX = 32767.0
+CODE_ROWS = HD + SCALE_ROWS
+
+
+def shifted(value, steps):
+    count = lax.axis_size("ctx")
     first, last = (max(0, -steps), min(count, count - steps))
-    return lax.ppermute(value, axis, [(source, source + steps) for source in range(first, last)])
-
-
-def all_sum(value, axis):
-    count = lax.axis_size(axis)
-    step = 1
-    while step < count:
-        value = value + lax.ppermute(value, axis, [(i, i ^ step) for i in range(count)])
-        step *= 2
-    return value
+    pairs = [(source, source + steps) for source in range(first, last)]
+    return lax.ppermute(value, "ctx", pairs)
+
+
+def exchange(value, axis, first, second):
+    count = math.prod(lax.axis_size(a) for a in axis)
+    one, two, three = (
+        lax.ppermute(value, axis, [(i, i ^ bits) for i in range(count)])
+        for bits in (first, second, first | second)
+    )
+    return (value + one) + (two + three)
+
+
+def encode(value):
+    top = jnp.maximum(jnp.max(jnp.abs(value), axis=0, keepdims=True), 2.0**-100)
+    level = jnp.ceil(jnp.log2(top) * SCALE_STEPS)
+    coded = jnp.round(value * (jnp.exp2(level * (-1.0 / SCALE_STEPS)) * CODE_MAX))
+    level = jnp.broadcast_to(level, (SCALE_ROWS, value.shape[1]))
+    return tuple(v.astype(jnp.int32).astype(jnp.int16) for v in (coded, level))
+
+
+def decode(coded, level):
+    level = level.astype(jnp.int32).astype(jnp.float32)[:1]
+    return coded.astype(jnp.int32).astype(jnp.float32) * (
+        jnp.exp2(level * (1.0 / SCALE_STEPS)) * (1.0 / CODE_MAX)
+    )
 
 
 def dot(a, b, dims=((1,), (0,))):
@@ -59,12 +80,14 @@
         p_ref[g] = probs
         p_low[:, g * rows : (g + 1) * rows] = probs.astype(jnp.bfloat16)
     dv = dot(p_low[...], g_all[...])
-    for j in range(REACH):
-        dv_refs[j][...] = dv[j * rows : (j + 1) * rows, :]
-
-
-def grads_kernel(group, rows, q_ref, g_ref, gain_ref, p_ref, *refs):
+    dv_refs[0][:HD, :], dv_refs[0][HD:, :] = encode(dv[:rows, :].T)
+    for j in range(1, REACH):
+        dv_refs[j][...] = dv[j * rows : (j + 1) * rows, :].T
+
+
+def grads_kernel(group, rows, skip, q_ref, g_ref, gain_ref, p_ref, *refs):
     k_refs, v_refs = refs[:REACH], refs[REACH : 2 * REACH]
+    refs = refs[: 2 * REACH] + refs[2 * REACH + skip :]
     o_ref, dq_ref, gain_out, *dk_refs = refs[2 * REACH : 3 * REACH + 3]
     k_t, v_t, v_all, ds_all, q_all = refs[3 * REACH + 3 :]
     factor = 1.0 / math.sqrt(HD)
@@ -89,8 +112,35 @@
         dq_ref[:, cols] = (dscaled * gain).astype(jnp.bfloat16)
         gain_out[:, cols] = jnp.sum(dscaled * q32, axis=0, keepdims=True)
     dk = dot(ds_all[...], q_all[...]) * factor
-    for j in range(REACH):
-        dk_refs[j][...] = dk[j * rows : (j + 1) * rows, :]
+    dk_refs[0][:HD, :], dk_refs[0][HD:, :] = encode(dk[:rows, :].T)
+    for j in range(1, REACH):
+        dk_refs[j][...] = dk[j * rows : (j + 1) * rows, :].T
+
+
+def hop_kernel(kv_count, last, message, part, out):
+    for c in range(kv_count):
+        at, here = c * CODE_ROWS, slice(c * HD, (c + 1) * HD)
+        total = part[here, :] + decode(
+            message[at : at + HD, :], message[at + HD : at + CODE_ROWS, :]
+        )
+        if last:
+            out[:, here] = total.T.astype(jnp.bfloat16)
+        else:
+            out[at : at + HD, :], out[at + HD : at + CODE_ROWS, :] = encode(total)
+
+
+def hop(message, part, last):
+    kv_channels, rows = part.shape
+    shape = jax.ShapeDtypeStruct((rows, kv_channels), jnp.bfloat16) if last else message
+    return pl.pallas_call(
+        functools.partial(hop_kernel, kv_channels // HD, last),
+        out_shape=jax.ShapeDtypeStruct(shape.shape, shape.dtype),
+        compiler_params=pltpu.CompilerParams(vmem_limit_bytes=16 * 2**20),
+        cost_estimate=pl.CostEstimate(
+            flops=10 * part.size, bytes_accessed=8 * part.size, transcendentals=0
+        ),
+        name="last_hop" if last else "hop",
+    )(message, part)
 
 
 def attention_probs(lo, queries, out_grad, gain, keys):
@@ -101,16 +151,20 @@
     width = REACH * rows
     wide = pl.BlockSpec((rows, group * HD), lambda c, lo: (0, c))
     thin = pl.BlockSpec((rows, HD), lambda c, lo: (0, c))
+    code = pl.BlockSpec((CODE_ROWS, rows), lambda c, lo: (c, 0))
+    part = pl.BlockSpec((HD, rows), lambda c, lo: (c, 0))
     return pl.pallas_call(
         functools.partial(probs_kernel, group, rows),
         out_shape=[jax.ShapeDtypeStruct((kv_count * group, width, rows), jnp.float32)]
-        + [jax.ShapeDtypeStruct((rows, kv_channels), jnp.float32)] * REACH,
+        + [jax.ShapeDtypeStruct((kv_count * CODE_ROWS, rows), jnp.int16)]
+        + [jax.ShapeDtypeStruct((kv_channels, rows), jnp.float32)] * (REACH - 1),
         grid_spec=pltpu.PrefetchScalarGridSpec(
             num_scalar_prefetch=1,
             grid=(kv_count,),
             in_specs=[wide, wide, pl.BlockSpec((1, group * HD), lambda c, lo: (0, c))]
             + [thin] * REACH,
-            out_specs=[pl.BlockSpec((group, width, rows), lambda c, lo: (c, 0, 0))] + [thin] * REACH,
+            out_specs=[pl.BlockSpec((group, width, rows), lambda c, lo: (c, 0, 0)), code]
+            + [part] * (REACH - 1),
             scratch_shapes=[
                 pltpu.VMEM((width, rows), jnp.float32),
                 pltpu.VMEM((width, HD), jnp.bfloat16),
@@ -127,24 +181,30 @@
     )(lo, queries, out_grad, gain, *keys)
 
 
-def attention_grads(queries, out_grad, gain, probs, keys, values):
+def attention_grads(first, count, before, queries, out_grad, gain, probs, keys, values):
     rows, channels = queries.shape
     kv_channels = keys[0].shape[1]
     kv_count = kv_channels // HD
     group = channels // kv_channels
     width = REACH * rows
-    wide = pl.BlockSpec((rows, group * HD), lambda c: (0, c))
-    line = pl.BlockSpec((1, group * HD), lambda c: (0, c))
-    thin = pl.BlockSpec((rows, HD), lambda c: (0, c))
+    wide = pl.BlockSpec((rows, group * HD), lambda c: (0, c + first))
+    line = pl.BlockSpec((1, group * HD), lambda c: (0, c + first))
+    thin = pl.BlockSpec((rows, HD), lambda c: (0, c + first))
+    code = pl.BlockSpec((CODE_ROWS, rows), lambda c: (c + first, 0))
+    part = pl.BlockSpec((HD, rows), lambda c: (c + first, 0))
+    n_in = 4 + 2 * REACH
     return pl.pallas_call(
-        functools.partial(grads_kernel, group, rows),
+        functools.partial(grads_kernel, group, rows, len(before)),
         out_shape=[jax.ShapeDtypeStruct((rows, channels), jnp.bfloat16)] * 2
         + [jax.ShapeDtypeStruct((1, channels), jnp.float32)]
-        + [jax.ShapeDtypeStruct((rows, kv_channels), jnp.float32)] * REACH,
-        grid=(kv_count,),
-        in_specs=[wide, wide, line, pl.BlockSpec((group, width, rows), lambda c: (c, 0, 0))]
-        + [thin] * (2 * REACH),
-        out_specs=[wide, wide, line] + [thin] * REACH,
+        + [jax.ShapeDtypeStruct((kv_count * CODE_ROWS, rows), jnp.int16)]
+        + [jax.ShapeDtypeStruct((kv_channels, rows), jnp.float32)] * (REACH - 1),
+        grid=(count,),
+        in_specs=[wide, wide, line]
+        + [pl.BlockSpec((group, width, rows), lambda c: (c + first, 0, 0))]
+        + [thin] * (2 * REACH)
+        + [pl.BlockSpec(memory_space=pl.ANY)] * len(before),
+        out_specs=[wide, wide, line, code] + [part] * (REACH - 1),
         scratch_shapes=[
             pltpu.VMEM((HD, width), jnp.bfloat16),
             pltpu.VMEM((HD, width), jnp.bfloat16),
@@ -152,40 +212,58 @@
             pltpu.VMEM((width, group * rows), jnp.bfloat16),
             pltpu.VMEM((group * rows, HD), jnp.bfloat16),
         ],
+        input_output_aliases={n_in + i: i for i in range(len(before))},
         cost_estimate=pl.CostEstimate(
-            flops=8 * kv_count * group * width * rows * HD,
-            bytes_accessed=4 * kv_count * group * width * rows,
+            flops=8 * count * group * width * rows * HD,
+            bytes_accessed=4 * count * group * width * rows,
             transcendentals=0,
         ),
-        name="grads",
-    )(queries, out_grad, gain, probs, *keys, *values)
-
-
-def local(queries, global_keys, global_values, out_grad, query_gain, doc_start):
+    )(queries, out_grad, gain, probs, *keys, *values, *before)
+
+
+def step(queries, global_keys, global_values, out_grad, query_gain, doc_start):
     rows = queries.shape[1]
     device = lax.axis_index("ctx")
     q, do = queries[0], out_grad[0]
     gain = query_gain[None]
+    together = lax.optimization_barrier
     keys, values = [global_keys[0]], [global_values[0]]
     for _ in range(1, REACH):
-        keys.insert(0, shifted(keys[0], "ctx", 1))
-    for _ in range(1, REACH):
-        values.insert(0, shifted(values[0], "ctx", 1))
+        keys.insert(0, shifted(keys[0], 1))
+    for _ in range(1, REACH - 1):
+        values.insert(0, shifted(values[0], 1))
+    keys[0], values[0] = together((keys[0], values[0]))
+    values.insert(0, shifted(values[0], 1))
     lo = doc_start[0] * BLOCK - (device - (REACH - 1)) * rows
-    probs, *dv = attention_probs(lo, q, do, gain, keys)
-    attn_out, query_grad, gain_term, *dk = attention_grads(q, do, gain, probs, keys, values)
-    value_total = dv[0]
-    for part in dv[1:]:
-        value_total = shifted(value_total, "ctx", -1) + part
-    key_total = dk[0]
-    for part in dk[1:]:
-        key_total = shifted(key_total, "ctx", -1) + part
-    gain_grad = all_sum(all_sum(gain_term[0], "dp"), "ctx")
+    half = keys[0].shape[1] // HD // 2
+
+    probs, dv_sum, *dv = attention_probs(lo, q, do, gain, keys)
+    moved = shifted(dv_sum, -1)
+    early = attention_grads(0, half, [], q, do, gain, probs, keys, values)
+    moved, gain = together((moved, gain))
+    moved = shifted(hop(moved, dv[0], False), -1)
+    attn_out, query_grad, gain_term, dk_sum, *dk = attention_grads(
+        half, half, early, q, do, gain, probs, keys, values
+    )
+    moved, dk_sum = together((moved, dk_sum))
+    dk_moved = shifted(dk_sum, -1)
+    moved = shifted(hop(moved, dv[1], False), -1)
+    both = ("dp", "ctx")
+    total = exchange(gain_term[0], both, 64, 128)
+    total = exchange(total, both, 8, 16)
+    dk_moved, moved, total = together((dk_moved, moved, total))
+    dk_moved = shifted(hop(dk_moved, dk[0], False), -1)
+    value_grad = hop(moved, dv[2], True)
+    total = exchange(total, both, 1, 2)
+    dk_moved, total = together((dk_moved, total))
+    dk_moved = shifted(hop(dk_moved, dk[1], False), -1)
+    gain_grad = exchange(total, both, 4, 32)
+    key_grad = hop(dk_moved, dk[2], True)
     return (
         attn_out[None],
         query_grad[None],
-        key_total.astype(jnp.bfloat16)[None],
-        value_total.astype(jnp.bfloat16)[None],
+        key_grad[None],
+        value_grad[None],
         gain_grad,
     )
 
@@ -193,7 +271,7 @@
 def solution(mesh):
     rows = P("dp", "ctx", None)
     return jax.shard_map(
-        local,
+        step,
         mesh=mesh,
         in_specs=(rows, rows, rows, rows, P(), P("dp", "ctx")),
         out_specs=(rows, rows, rows, rows, P()),

time: 171 us -> 143 us (0.84)
  waiting for transfers between devices: 72.3 us -> 33.4 us
  Pallas kernels: 34.7 us -> 41.1 us
  starting transfers between devices: 55.2 us -> 60 us
  other arithmetic: 4.8 us -> 2.67 us
    ppermute x20 -> x24, waiting for transfers between devices: 72.3 us -> 33.4 us  [the longest x12 28.6 us: shifted(): return lax.ppermute(value, 'ctx', pairs)]
    pallas_call x1 -> x8, Pallas kernels: 19.1 us -> 25 us  [the longest x2 22.6 us: attention_grads(): pl.pallas_call(functools.partial(grads_kernel, group, rows, len(before)),...]
    ppermute x20 -> x24, starting transfers between devices: 55.2 us -> 60 us  [the longest x12 41 us: shifted(): return lax.ppermute(value, 'ctx', pairs)]
  transfers between devices with their start and end apart: 20 -> 24, of which waited for: 17 -> 16; matrix products, arithmetic and copies ran while one was open for 3% -> 3% of each run, Pallas kernels for 9% -> 17%
where the time goes in v2:
time: 143 us; the launch traced here: 142 us
  starting transfers between devices  60 us (42%)
  Pallas kernels  41.1 us (29%)
  waiting for transfers between devices  33.4 us (23%)
  local copies, waits for them, and re-layouts  3.8 us (3%)
  other arithmetic  2.67 us (2%)
    ppermute x12, starting transfers between devices, shifted(): return lax.ppermute(value, 'ctx', pairs)  41 us
    ppermute x12, waiting for transfers between devices, shifted(): return lax.ppermute(value, 'ctx', pairs)  28.6 us
    pallas_call x2, Pallas kernels, attention_grads(): pl.pallas_call(functools.partial(grads_kernel, group, rows, len(before)),...  22.6 us
    ppermute x12, starting transfers between devices, exchange(): lax.ppermute(value, axis, [(i, i ^ bits) for i in range(count)])  18.9 us
    pallas_call x1, Pallas kernels, attention_probs(): pl.pallas_call(functools.partial(probs_kernel, group, rows), out_shape=[j...  16.1 us
    ppermute x12, waiting for transfers between devices, exchange(): lax.ppermute(value, axis, [(i, i ^ bits) for i in range(count)])  4.88 us
  transfers between devices with their start and end apart: 24, of which 16 were waited for; matrix products, arithmetic and copies ran while one was open for 3% of the time, Pallas kernels for 17%

profile of v2, /device:TPU:22, one launch (start us, length us, event | category | flops | bytes accessed | tf_op | source)
XLA Modules:
  0.0 141.9 jit_solution(11119426951822242849)
XLA Ops:
  0.6 3.8 %collective-permute-start = (bf16[256,512]{1,0:T(8,128)(2,1)}, bf16[256,512]{1,0:T(8,128)(2,1)S(1)}, u32[]{:S(2)}, u32[]{:S(2)}) collective-permute-start(bf16[256,512]{1,0:T(8,128)(2,1)} %bitcast.18), channel_id=1, source_target_pairs={{0,1},{1,2},{2,3},{3,4},{4,5},{5,6},{6,7},{7,8},{8,9},{9,10},{10,1... | collective-permute-start | bytes 786440 | tf_op jit(solution)/shard_map/ppermute | solution.py:26
  4.5 3.8 %collective-permute-start.3 = (bf16[256,512]{1,0:T(8,128)(2,1)}, bf16[256,512]{1,0:T(8,128)(2,1)S(1)}, u32[]{:S(2)}, u32[]{:S(2)}) collective-permute-start(bf16[256,512]{1,0:T(8,128)(2,1)} %bitcast.22), channel_id=1, source_target_pairs={{0,1},{1,2},{2,3},{3,4},{4,5},{5,6},{6,7},{7,8},{8,9},{9,10},{10,1... | collective-permute-start | bytes 786440 | tf_op jit(solution)/shard_map/ppermute | solution.py:26
  8.3 7.7 %collective-permute-done.refs_2_ = bf16[256,512]{1,0:T(8,128)(2,1)S(1)} collective-permute-done((bf16[256,512]{1,0:T(8,128)(2,1)}, bf16[256,512]{1,0:T(8,128)(2,1)S(1)}, u32[]{:S(2)}, u32[]{:S(2)}) %collective-permute-start) | collective-permute-done | bytes 262176 | tf_op jit(solution)/shard_map/ppermute | solution.py:26
  16.0 1.9 %collective-permute-start.1 = (bf16[256,512]{1,0:T(8,128)(2,1)S(1)}, bf16[256,512]{1,0:T(8,128)(2,1)S(1)}, u32[]{:S(2)}, u32[]{:S(2)}) collective-permute-start(bf16[256,512]{1,0:T(8,128)(2,1)S(1)} %collective-permute-done.refs_2_), channel_id=1, source_target_pairs={{0,1},{1,2},{2,3},{3,4},{4,5},{5,6},{6,7},{7,8},{8,9},{9,10},{10,1... | collective-permute-start | bytes 786440 | tf_op jit(solution)/shard_map/ppermute | solution.py:26
  17.9 2.8 %collective-permute-done.3.refs_6_ = bf16[256,512]{1,0:T(8,128)(2,1)S(1)} collective-permute-done((bf16[256,512]{1,0:T(8,128)(2,1)}, bf16[256,512]{1,0:T(8,128)(2,1)S(1)}, u32[]{:S(2)}, u32[]{:S(2)}) %collective-permute-start.3) | collective-permute-done | bytes 262176 | tf_op jit(solution)/shard_map/ppermute | solution.py:26
  20.8 1.9 %collective-permute-start.4 = (bf16[256,512]{1,0:T(8,128)(2,1)S(1)}, bf16[256,512]{1,0:T(8,128)(2,1)S(1)}, u32[]{:S(2)}, u32[]{:S(2)}) collective-permute-start(bf16[256,512]{1,0:T(8,128)(2,1)S(1)} %collective-permute-done.3.refs_6_), channel_id=1, source_target_pairs={{0,1},{1,2},{2,3},{3,4},{4,5},{5,6},{6,7},{7,8},{8,9},{9,10},{10,1... | collective-permute-start | bytes 786440 | tf_op jit(solution)/shard_map/ppermute | solution.py:26
  22.7 3.9 %collective-permute-done.1.refs_1_ = bf16[256,512]{1,0:T(8,128)(2,1)S(1)} collective-permute-done((bf16[256,512]{1,0:T(8,128)(2,1)S(1)}, bf16[256,512]{1,0:T(8,128)(2,1)S(1)}, u32[]{:S(2)}, u32[]{:S(2)}) %collective-permute-start.1) | collective-permute-done | bytes 262176 | tf_op jit(solution)/shard_map/ppermute | solution.py:26
  31.1 2.6 %collective-permute-done.4.refs_5_ = bf16[256,512]{1,0:T(8,128)(2,1)S(1)} collective-permute-done((bf16[256,512]{1,0:T(8,128)(2,1)S(1)}, bf16[256,512]{1,0:T(8,128)(2,1)S(1)}, u32[]{:S(2)}, u32[]{:S(2)}) %collective-permute-start.4) | collective-permute-done | bytes 262176 | tf_op jit(solution)/shard_map/ppermute | solution.py:26
  33.7 4.1 %collective-permute-done.2.refs_0_ = bf16[256,512]{1,0:T(8,128)(2,1)S(1)} collective-permute-done((bf16[256,512]{1,0:T(8,128)(2,1)S(1)}, bf16[256,512]{1,0:T(8,128)(2,1)S(1)}, u32[]{:S(2)}, u32[]{:S(2)}) %collective-permute-start.2) | collective-permute-done | bytes 262176 | tf_op jit(solution)/shard_map/ppermute | solution.py:26
  38.6 16.1 %probs.1 = (f32[20,1024,256]{2,1,0:T(8,128)}, s16[576,256]{1,0:T(8,128)(2,1)}, f32[512,256]{1,0:T(8,128)}, f32[512,256]{1,0:T(8,128)}, f32[512,256]{1,0:T(8,128)}) custom-call(s32[2]{0:T(128)} %subtract_bitcast_fusion.lo, bf16[256,2560]{1,0:T(8,128)(2,1)} %bitcast.10, bf16[256,2560]{1,0:T(8,128)(2,1)} %bitcast.13, f32[1,2560]{1,0:T(1,128)} %broadcast_in_dim.15.gain_ref, ...), custom_call_target="tpu_custom_call" | custom-call | flops 2684354560 | bytes 20971520 | tf_op jit(solution)/shard_map/probs/pallas_call | solution.py:156
  54.7 3.4 %collective-permute-start.5 = (s16[576,256]{1,0:T(8,128)(2,1)}, s16[576,256]{1,0:T(8,128)(2,1)S(1)}, u32[]{:S(2)}, u32[]{:S(2)}) collective-permute-start(s16[576,256]{1,0:T(8,128)(2,1)} %get-tuple-element.36), channel_id=1, source_target_pairs={{1,0},{2,1},{3,2},{4,3},{5,4},{6,5},{7,6},{8,7},{9,8},{10,9},{11,1... | collective-permute-start | bytes 884744 | tf_op jit(solution)/shard_map/ppermute | solution.py:26
  58.1 2.4 %collective-permute-start.6 = (bf16[256,512]{1,0:T(8,128)(2,1)S(1)}, bf16[256,512]{1,0:T(8,128)(2,1)S(1)}, u32[]{:S(2)}, u32[]{:S(2)}) collective-permute-start(bf16[256,512]{1,0:T(8,128)(2,1)S(1)} %collective-permute-done.4.refs_5_), channel_id=1, source_target_pairs={{0,1},{1,2},{2,3},{3,4},{4,5},{5,6},{6,7},{7,8},{8,9},{9,10},{10,1... | collective-permute-start | bytes 786440 | tf_op jit(solution)/shard_map/ppermute | solution.py:26
  60.5 3.3 %collective-permute-done.5.message = s16[576,256]{1,0:T(8,128)(2,1)S(1)} collective-permute-done((s16[576,256]{1,0:T(8,128)(2,1)}, s16[576,256]{1,0:T(8,128)(2,1)S(1)}, u32[]{:S(2)}, u32[]{:S(2)}) %collective-permute-start.5) | collective-permute-done | bytes 294944 | tf_op jit(solution)/shard_map/ppermute | solution.py:26
  65.1 6.3 %collective-permute-start.7 = (s16[576,256]{1,0:T(8,128)(2,1)S(1)}, s16[576,256]{1,0:T(8,128)(2,1)S(1)}, u32[]{:S(2)}, u32[]{:S(2)}) collective-permute-start(s16[576,256]{1,0:T(8,128)(2,1)S(1)} %hop.4), channel_id=1, source_target_pairs={{1,0},{2,1},{3,2},{4,3},{5,4},{6,5},{7,6},{8,7},{9,8},{10,9},{11,1... | collective-permute-start | bytes 884744 | tf_op jit(solution)/shard_map/ppermute | solution.py:26
  72.1 11.3 %shard_map.101 = (bf16[256,2560]{1,0:T(8,128)(2,1)}, bf16[256,2560]{1,0:T(8,128)(2,1)}, f32[1,2560]{1,0:T(1,128)}, s16[576,256]{1,0:T(8,128)(2,1)}, f32[512,256]...) custom-call(bf16[256,2560]{1,0:T(8,128)(2,1)} %bitcast.11, bf16[256,2560]{1,0:T(8,128)(2,1)} %bitcast.14, ...), custom_call_target="tpu_custom_call" | custom-call | flops 2684354560 | bytes 10485760 | tf_op jit(solution)/shard_map/pallas_call | solution.py:196
  83.4 11.3 %shard_map.102 = (bf16[256,2560]{1,0:T(8,128)(2,1)}, bf16[256,2560]{1,0:T(8,128)(2,1)}, f32[1,2560]{1,0:T(1,128)}, s16[576,256]{1,0:T(8,128)(2,1)}, f32[512,256]...) custom-call(bf16[256,2560]{1,0:T(8,128)(2,1)} %bitcast.12, ...), custom_call_target="tpu_custom_call", output_to_operand_aliasing={{0}: (12, {}), {1}: (13, {}), {2}: (14, {}), {3}: (15, {}),... | custom-call | flops 2684354560 | bytes 10485760 | tf_op jit(solution)/shard_map/pallas_call | solution.py:196
  96.2 2.9 %collective-permute-start.11 = (f32[2560]{0:T(1024)S(1)}, f32[2560]{0:T(1024)S(1)}, u32[]{:S(2)}, u32[]{:S(2)}) collective-permute-start(f32[2560]{0:T(1024)S(1)} %reduce), channel_id=1, source_target_pairs={{0,128},{1,129},{2,130},{3,131},{4,132},{5,133},{6,134},{7,135},{8... | collective-permute-start | bytes 30728 | tf_op jit(solution)/shard_map/ppermute | solution.py:32
  101.9 2.1 %collective-permute-start.9 = (s16[576,256]{1,0:T(8,128)(2,1)S(1)}, s16[576,256]{1,0:T(8,128)(2,1)S(1)}, u32[]{:S(2)}, u32[]{:S(2)}) collective-permute-start(s16[576,256]{1,0:T(8,128)(2,1)S(1)} %hop.5), channel_id=1, source_target_pairs={{1,0},{2,1},{3,2},{4,3},{5,4},{6,5},{7,6},{8,7},{9,8},{10,9},{11,1... | collective-permute-start | bytes 884744 | tf_op jit(solution)/shard_map/ppermute | solution.py:26
  104.1 2.6 %collective-permute-start.14 = (f32[2560]{0:T(1024)S(1)}, f32[2560]{0:T(1024)S(1)}, u32[]{:S(2)}, u32[]{:S(2)}) collective-permute-start(f32[2560]{0:T(1024)S(1)} %add_add_fusion.3), channel_id=1, source_target_pairs={{0,16},{1,17},{2,18},{3,19},{4,20},{5,21},{6,22},{7,23},{8,24},{9,... | collective-permute-start | bytes 30728 | tf_op jit(solution)/shard_map/ppermute | solution.py:32
  111.0 3.2 %collective-permute-done.9.message = s16[576,256]{1,0:T(8,128)(2,1)S(1)} collective-permute-done((s16[576,256]{1,0:T(8,128)(2,1)S(1)}, s16[576,256]{1,0:T(8,128)(2,1)S(1)}, u32[]{:S(2)}, u32[]{:S(2)}) %collective-permute-start.9) | collective-permute-done | bytes 294944 | tf_op jit(solution)/shard_map/ppermute | solution.py:26
  114.3 5.0 %collective-permute-start.16 = (s16[576,256]{1,0:T(8,128)(2,1)S(1)}, s16[576,256]{1,0:T(8,128)(2,1)S(1)}, u32[]{:S(2)}, u32[]{:S(2)}) collective-permute-start(s16[576,256]{1,0:T(8,128)(2,1)S(1)} %hop.6), channel_id=1, source_target_pairs={{1,0},{2,1},{3,2},{4,3},{5,4},{6,5},{7,6},{8,7},{9,8},{10,9},{11,1... | collective-permute-start | bytes 884744 | tf_op jit(solution)/shard_map/ppermute | solution.py:26
  119.9 3.9 %collective-permute-start.17 = (f32[2560]{0:T(1024)S(1)}, f32[2560]{0:T(1024)S(1)}, u32[]{:S(2)}, u32[]{:S(2)}) collective-permute-start(f32[2560]{0:T(1024)S(1)} %add_add_fusion.2), channel_id=1, source_target_pairs={{0,1},{1,0},{2,3},{3,2},{4,5},{5,4},{6,7},{7,6},{8,9},{9,8},{10,11... | collective-permute-start | bytes 30728 | tf_op jit(solution)/shard_map/ppermute | solution.py:32
  125.9 6.5 %collective-permute-start.20 = (s16[576,256]{1,0:T(8,128)(2,1)S(1)}, s16[576,256]{1,0:T(8,128)(2,1)S(1)}, u32[]{:S(2)}, u32[]{:S(2)}) collective-permute-start(s16[576,256]{1,0:T(8,128)(2,1)S(1)} %hop.7), channel_id=1, source_target_pairs={{1,0},{2,1},{3,2},{4,3},{5,4},{6,5},{7,6},{8,7},{9,8},{10,9},{11,1... | collective-permute-start | bytes 884744 | tf_op jit(solution)/shard_map/ppermute | solution.py:26
  132.8 5.7 %collective-permute-start.21 = (f32[2560]{0:T(1024)S(1)}, f32[2560]{0:T(1024)S(1)}, u32[]{:S(2)}, u32[]{:S(2)}) collective-permute-start(f32[2560]{0:T(1024)S(1)} %add_add_fusion.1), channel_id=1, source_target_pairs={{0,4},{1,5},{2,6},{3,7},{4,0},{5,1},{6,2},{7,3},{8,12},{9,13},{10,... | collective-permute-start | bytes 30728 | tf_op jit(solution)/shard_map/ppermute | solution.py:32
  (64 shorter events, 22.3 us)
Async XLA Ops:
  0.6 15.4 %collective-permute-start = (bf16[256,512]{1,0:T(8,128)(2,1)}, bf16[256,512]{1,0:T(8,128)(2,1)S(1)}, u32[]{:S(2)}, u32[]{:S(2)}) collective-permute-start(bf16[256,512]{1,0:T(8,128)(2,1)} %bitcast.18), channel_id=1, source_target_pairs={{0,1},{1,2},{2,3},{3,4},{4,5},{5,6},{6,7},{7,8},{8,9},{9,10},{10,1... | collective-permute-start | bytes 786440 | tf_op jit(solution)/shard_map/ppermute | solution.py:26
  4.5 16.3 %collective-permute-start.3 = (bf16[256,512]{1,0:T(8,128)(2,1)}, bf16[256,512]{1,0:T(8,128)(2,1)S(1)}, u32[]{:S(2)}, u32[]{:S(2)}) collective-permute-start(bf16[256,512]{1,0:T(8,128)(2,1)} %bitcast.22), channel_id=1, source_target_pairs={{0,1},{1,2},{2,3},{3,4},{4,5},{5,6},{6,7},{7,8},{8,9},{9,10},{10,1... | collective-permute-start | bytes 786440 | tf_op jit(solution)/shard_map/ppermute | solution.py:26
  16.0 10.6 %collective-permute-start.1 = (bf16[256,512]{1,0:T(8,128)(2,1)S(1)}, bf16[256,512]{1,0:T(8,128)(2,1)S(1)}, u32[]{:S(2)}, u32[]{:S(2)}) collective-permute-start(bf16[256,512]{1,0:T(8,128)(2,1)S(1)} %collective-permute-done.refs_2_), channel_id=1, source_target_pairs={{0,1},{1,2},{2,3},{3,4},{4,5},{5,6},{6,7},{7,8},{8,9},{9,10},{10,1... | collective-permute-start | bytes 786440 | tf_op jit(solution)/shard_map/ppermute | solution.py:26
  20.8 12.9 %collective-permute-start.4 = (bf16[256,512]{1,0:T(8,128)(2,1)S(1)}, bf16[256,512]{1,0:T(8,128)(2,1)S(1)}, u32[]{:S(2)}, u32[]{:S(2)}) collective-permute-start(bf16[256,512]{1,0:T(8,128)(2,1)S(1)} %collective-permute-done.3.refs_6_), channel_id=1, source_target_pairs={{0,1},{1,2},{2,3},{3,4},{4,5},{5,6},{6,7},{7,8},{8,9},{9,10},{10,1... | collective-permute-start | bytes 786440 | tf_op jit(solution)/shard_map/ppermute | solution.py:26
  26.6 11.2 %collective-permute-start.2 = (bf16[256,512]{1,0:T(8,128)(2,1)S(1)}, bf16[256,512]{1,0:T(8,128)(2,1)S(1)}, u32[]{:S(2)}, u32[]{:S(2)}) collective-permute-start(bf16[256,512]{1,0:T(8,128)(2,1)S(1)} %collective-permute-done.1.refs_1_), channel_id=1, source_target_pairs={{0,1},{1,2},{2,3},{3,4},{4,5},{5,6},{6,7},{7,8},{8,9},{9,10},{10,1... | collective-permute-start | bytes 786440 | tf_op jit(solution)/shard_map/ppermute | solution.py:26
  54.7 9.2 %collective-permute-start.5 = (s16[576,256]{1,0:T(8,128)(2,1)}, s16[576,256]{1,0:T(8,128)(2,1)S(1)}, u32[]{:S(2)}, u32[]{:S(2)}) collective-permute-start(s16[576,256]{1,0:T(8,128)(2,1)} %get-tuple-element.36), channel_id=1, source_target_pairs={{1,0},{2,1},{3,2},{4,3},{5,4},{6,5},{7,6},{8,7},{9,8},{10,9},{11,1... | collective-permute-start | bytes 884744 | tf_op jit(solution)/shard_map/ppermute | solution.py:26
  58.1 13.3 %collective-permute-start.6 = (bf16[256,512]{1,0:T(8,128)(2,1)S(1)}, bf16[256,512]{1,0:T(8,128)(2,1)S(1)}, u32[]{:S(2)}, u32[]{:S(2)}) collective-permute-start(bf16[256,512]{1,0:T(8,128)(2,1)S(1)} %collective-permute-done.4.refs_5_), channel_id=1, source_target_pairs={{0,1},{1,2},{2,3},{3,4},{4,5},{5,6},{6,7},{7,8},{8,9},{9,10},{10,1... | collective-permute-start | bytes 786440 | tf_op jit(solution)/shard_map/ppermute | solution.py:26
  65.1 34.7 %collective-permute-start.7 = (s16[576,256]{1,0:T(8,128)(2,1)S(1)}, s16[576,256]{1,0:T(8,128)(2,1)S(1)}, u32[]{:S(2)}, u32[]{:S(2)}) collective-permute-start(s16[576,256]{1,0:T(8,128)(2,1)S(1)} %hop.4), channel_id=1, source_target_pairs={{1,0},{2,1},{3,2},{4,3},{5,4},{6,5},{7,6},{8,7},{9,8},{10,9},{11,1... | collective-permute-start | bytes 884744 | tf_op jit(solution)/shard_map/ppermute | solution.py:26
  95.6 8.4 %collective-permute-start.12 = (f32[2560]{0:T(1024)S(1)}, f32[2560]{0:T(1024)S(1)}, u32[]{:S(2)}, u32[]{:S(2)}) collective-permute-start(f32[2560]{0:T(1024)S(1)} %reduce), channel_id=1, source_target_pairs={{0,192},{1,193},{2,194},{3,195},{4,196},{5,197},{6,198},{7,199},{8... | collective-permute-start | bytes 30728 | tf_op jit(solution)/shard_map/ppermute | solution.py:32
  96.2 7.8 %collective-permute-start.11 = (f32[2560]{0:T(1024)S(1)}, f32[2560]{0:T(1024)S(1)}, u32[]{:S(2)}, u32[]{:S(2)}) collective-permute-start(f32[2560]{0:T(1024)S(1)} %reduce), channel_id=1, source_target_pairs={{0,128},{1,129},{2,130},{3,131},{4,132},{5,133},{6,134},{7,135},{8... | collective-permute-start | bytes 30728 | tf_op jit(solution)/shard_map/ppermute | solution.py:32
  99.1 4.9 %collective-permute-start.10 = (f32[2560]{0:T(1024)S(1)}, f32[2560]{0:T(1024)S(1)}, u32[]{:S(2)}, u32[]{:S(2)}) collective-permute-start(f32[2560]{0:T(1024)S(1)} %reduce), channel_id=1, source_target_pairs={{0,64},{1,65},{2,66},{3,67},{4,68},{5,69},{6,70},{7,71},{8,72},{9,... | collective-permute-start | bytes 30728 | tf_op jit(solution)/shard_map/ppermute | solution.py:32
  99.8 11.2 %collective-permute-start.8 = (s16[576,256]{1,0:T(8,128)(2,1)}, s16[576,256]{1,0:T(8,128)(2,1)S(1)}, u32[]{:S(2)}, u32[]{:S(2)}) collective-permute-start(s16[576,256]{1,0:T(8,128)(2,1)} %get-tuple-element.52), channel_id=1, source_target_pairs={{1,0},{2,1},{3,2},{4,3},{5,4},{6,5},{7,6},{8,7},{9,8},{10,9},{11,1... | collective-permute-start | bytes 884744 | tf_op jit(solution)/shard_map/ppermute | solution.py:26
  101.9 12.2 %collective-permute-start.9 = (s16[576,256]{1,0:T(8,128)(2,1)S(1)}, s16[576,256]{1,0:T(8,128)(2,1)S(1)}, u32[]{:S(2)}, u32[]{:S(2)}) collective-permute-start(s16[576,256]{1,0:T(8,128)(2,1)S(1)} %hop.5), channel_id=1, source_target_pairs={{1,0},{2,1},{3,2},{4,3},{5,4},{6,5},{7,6},{8,7},{9,8},{10,9},{11,1... | collective-permute-start | bytes 884744 | tf_op jit(solution)/shard_map/ppermute | solution.py:26
  104.0 5.0 %collective-permute-start.15 = (f32[2560]{0:T(1024)S(1)}, f32[2560]{0:T(1024)S(1)}, u32[]{:S(2)}, u32[]{:S(2)}) collective-permute-start(f32[2560]{0:T(1024)S(1)} %add_add_fusion.3), channel_id=1, source_target_pairs={{0,24},{1,25},{2,26},{3,27},{4,28},{5,29},{6,30},{7,31},{8,16},{9,... | collective-permute-start | bytes 30728 | tf_op jit(solution)/shard_map/ppermute | solution.py:32
  104.1 5.3 %collective-permute-start.14 = (f32[2560]{0:T(1024)S(1)}, f32[2560]{0:T(1024)S(1)}, u32[]{:S(2)}, u32[]{:S(2)}) collective-permute-start(f32[2560]{0:T(1024)S(1)} %add_add_fusion.3), channel_id=1, source_target_pairs={{0,16},{1,17},{2,18},{3,19},{4,20},{5,21},{6,22},{7,23},{8,24},{9,... | collective-permute-start | bytes 30728 | tf_op jit(solution)/shard_map/ppermute | solution.py:32
  106.7 3.7 %collective-permute-start.13 = (f32[2560]{0:T(1024)S(1)}, f32[2560]{0:T(1024)S(1)}, u32[]{:S(2)}, u32[]{:S(2)}) collective-permute-start(f32[2560]{0:T(1024)S(1)} %add_add_fusion.3), channel_id=1, source_target_pairs={{0,8},{1,9},{2,10},{3,11},{4,12},{5,13},{6,14},{7,15},{8,0},{9,1},... | collective-permute-start | bytes 30728 | tf_op jit(solution)/shard_map/ppermute | solution.py:32
  114.3 11.4 %collective-permute-start.16 = (s16[576,256]{1,0:T(8,128)(2,1)S(1)}, s16[576,256]{1,0:T(8,128)(2,1)S(1)}, u32[]{:S(2)}, u32[]{:S(2)}) collective-permute-start(s16[576,256]{1,0:T(8,128)(2,1)S(1)} %hop.6), channel_id=1, source_target_pairs={{1,0},{2,1},{3,2},{4,3},{5,4},{6,5},{7,6},{8,7},{9,8},{10,9},{11,1... | collective-permute-start | bytes 884744 | tf_op jit(solution)/shard_map/ppermute | solution.py:26
  119.3 5.6 %collective-permute-start.19 = (f32[2560]{0:T(1024)S(1)}, f32[2560]{0:T(1024)S(1)}, u32[]{:S(2)}, u32[]{:S(2)}) collective-permute-start(f32[2560]{0:T(1024)S(1)} %add_add_fusion.2), channel_id=1, source_target_pairs={{0,3},{1,2},{2,1},{3,0},{4,7},{5,6},{6,5},{7,4},{8,11},{9,10},{10,... | collective-permute-start | bytes 30728 | tf_op jit(solution)/shard_map/ppermute | solution.py:32
  119.4 5.5 %collective-permute-start.18 = (f32[2560]{0:T(1024)S(1)}, f32[2560]{0:T(1024)S(1)}, u32[]{:S(2)}, u32[]{:S(2)}) collective-permute-start(f32[2560]{0:T(1024)S(1)} %add_add_fusion.2), channel_id=1, source_target_pairs={{0,2},{1,3},{2,0},{3,1},{4,6},{5,7},{6,4},{7,5},{8,10},{9,11},{10,... | collective-permute-start | bytes 30728 | tf_op jit(solution)/shard_map/ppermute | solution.py:32
  119.9 5.5 %collective-permute-start.17 = (f32[2560]{0:T(1024)S(1)}, f32[2560]{0:T(1024)S(1)}, u32[]{:S(2)}, u32[]{:S(2)}) collective-permute-start(f32[2560]{0:T(1024)S(1)} %add_add_fusion.2), channel_id=1, source_target_pairs={{0,1},{1,0},{2,3},{3,2},{4,5},{5,4},{6,7},{7,6},{8,9},{9,8},{10,11... | collective-permute-start | bytes 30728 | tf_op jit(solution)/shard_map/ppermute | solution.py:32
  125.9 15.1 %collective-permute-start.20 = (s16[576,256]{1,0:T(8,128)(2,1)S(1)}, s16[576,256]{1,0:T(8,128)(2,1)S(1)}, u32[]{:S(2)}, u32[]{:S(2)}) collective-permute-start(s16[576,256]{1,0:T(8,128)(2,1)S(1)} %hop.7), channel_id=1, source_target_pairs={{1,0},{2,1},{3,2},{4,3},{5,4},{6,5},{7,6},{8,7},{9,8},{10,9},{11,1... | collective-permute-start | bytes 884744 | tf_op jit(solution)/shard_map/ppermute | solution.py:26
  132.4 7.1 %collective-permute-start.23 = (f32[2560]{0:T(1024)S(1)}, f32[2560]{0:T(1024)S(1)}, u32[]{:S(2)}, u32[]{:S(2)}) collective-permute-start(f32[2560]{0:T(1024)S(1)} %add_add_fusion.1), channel_id=1, source_target_pairs={{0,36},{1,37},{2,38},{3,39},{4,32},{5,33},{6,34},{7,35},{8,44},{9,... | collective-permute-start | bytes 30728 | tf_op jit(solution)/shard_map/ppermute | solution.py:32
  132.5 7.0 %collective-permute-start.22 = (f32[2560]{0:T(1024)S(1)}, f32[2560]{0:T(1024)S(1)}, u32[]{:S(2)}, u32[]{:S(2)}) collective-permute-start(f32[2560]{0:T(1024)S(1)} %add_add_fusion.1), channel_id=1, source_target_pairs={{0,32},{1,33},{2,34},{3,35},{4,36},{5,37},{6,38},{7,39},{8,40},{9,... | collective-permute-start | bytes 30728 | tf_op jit(solution)/shard_map/ppermute | solution.py:32
  132.8 7.6 %collective-permute-start.21 = (f32[2560]{0:T(1024)S(1)}, f32[2560]{0:T(1024)S(1)}, u32[]{:S(2)}, u32[]{:S(2)}) collective-permute-start(f32[2560]{0:T(1024)S(1)} %add_add_fusion.1), channel_id=1, source_target_pairs={{0,4},{1,5},{2,6},{3,7},{4,0},{5,1},{6,2},{7,3},{8,12},{9,13},{10,... | collective-permute-start | bytes 30728 | tf_op jit(solution)/shard_map/ppermute | solution.py:32
  (12 other events, 225.8 us)

commit v3 on v2

v3 whole, which is shorter than its diff:
```python
import functools
import math

import jax
import jax.numpy as jnp
from jax import lax
from jax.experimental import pallas as pl
from jax.experimental.pallas import tpu as pltpu
from jax.sharding import PartitionSpec as P


HD = 128
BLOCK = 128
REACH = 4
EXPONENT = 1.4426950408889634 / math.sqrt(HD)
SCALE_STEPS = 64.0
SCALE_ROWS = 16
CODE_MAX = 32767.0
CODE_ROWS = HD + SCALE_ROWS


def shifted(value, steps):
    count = lax.axis_size("ctx")
    first, last = (max(0, -steps), min(count, count - steps))
    pairs = [(source, source + steps) for source in range(first, last)]
    return lax.ppermute(value, "ctx", pairs)


def exchange(value, axis, first, second):
    count = math.prod(lax.axis_size(a) for a in axis)
    one, two, three = (
        lax.ppermute(value, axis, [(i, i ^ bits) for i in range(count)])
        for bits in (first, second, first | second)
    )
    return (value + one) + (two + three)


def encode(value):
    top = jnp.maximum(jnp.max(jnp.abs(value), axis=0, keepdims=True), 2.0**-100)
    level = jnp.ceil(jnp.log2(top) * SCALE_STEPS)
    coded = jnp.round(value * (jnp.exp2(level * (-1.0 / SCALE_STEPS)) * CODE_MAX))
    level = jnp.broadcast_to(level, (SCALE_ROWS, value.shape[1]))
    return tuple(v.astype(jnp.int32).astype(jnp.int16) for v in (coded, level))


def decode(coded, level):
    level = level.astype(jnp.int32).astype(jnp.float32)[:1]
    return coded.astype(jnp.int32).astype(jnp.float32) * (
        jnp.exp2(level * (1.0 / SCALE_STEPS)) * (1.0 / CODE_MAX)
    )


def dot(a, b, dims=((1,), (0,))):
    return lax.dot_general(a, b, (dims, ((), ())), preferred_element_type=jnp.float32)


def softened(raw):
    top = jnp.max(raw, axis=0, keepdims=True)
    e = jnp.exp2((raw - top) * EXPONENT)
    return e, top, jnp.sum(e, axis=0, keepdims=True)


def scaled_query(q_ref, gain_ref, cols):
    return (q_ref[:, cols].astype(jnp.float32) * gain_ref[:, cols]).astype(jnp.bfloat16)


def scores_kernel(group, own, q_ref, gain_ref, k_ref, e_ref, top_ref, sum_ref):
    rows = k_ref.shape[0]
    per = rows // BLOCK
    if own:
        key = lax.broadcasted_iota(jnp.int32, (BLOCK, rows), 0)
        query = lax.broadcasted_iota(jnp.int32, (BLOCK, rows), 1)
    for g in range(group):
        scaled = scaled_query(q_ref, gain_ref, slice(g * HD, (g + 1) * HD))
        for b in range(per):
            here = slice(b * BLOCK, (b + 1) * BLOCK)
            raw = dot(k_ref[here, :], scaled, ((1,), (1,)))
            if own:
                later = (key + b * BLOCK > query) & (query >= b * BLOCK)
                raw = jnp.where(later, -jnp.inf, raw)
            e, top, total = softened(raw)
            at = slice(g * per + b, g * per + b + 1)
            e_ref[g, here, :], top_ref[0, at, :], sum_ref[0, at, :] = e, top, total


def far_kernel(group, lo, q_ref, g_ref, gain_ref, k_ref, *refs):
    stats = refs[: 2 * (REACH - 1)]
    e_ref, w_ref, dv_ref, p_low, g_all = refs[2 * (REACH - 1) :]
    rows = k_ref.shape[0]
    per = rows // BLOCK
    blocks = REACH * per
    half = lax.broadcasted_iota(jnp.int32, (1, rows), 1) // BLOCK
    begin = jnp.where(half == 0, lo[0], lo[1])
    allowed = [
        (begin <= b * BLOCK) & (half >= b - (REACH - 1) * per) for b in range(blocks)
    ]
    for g in range(group):
        cols = slice(g * HD, (g + 1) * HD)
        g_all[g * rows : (g + 1) * rows, :] = g_ref[:, cols]
        scaled = scaled_query(q_ref, gain_ref, cols)
        tops, sums = [], []
        for b in range(per):
            here = slice(b * BLOCK, (b + 1) * BLOCK)
            e, top, total = softened(dot(k_ref[here, :], scaled, ((1,), (1,))))
            e_ref[g, here, :] = e
            tops.append(top)
            sums.append(total)
        for j in range(REACH - 1):
            for b in range(per):
                at = slice(g * per + b, g * per + b + 1)
                tops.append(stats[2 * j][0, at, :])
                sums.append(stats[2 * j + 1][0, at, :])
        tops = [jnp.where(ok, top, -jnp.inf) for ok, top in zip(allowed, tops, strict=True)]
        highest = functools.reduce(jnp.maximum, tops)
        shares = [jnp.exp2((top - highest) * EXPONENT) for top in tops]
        total = sum(share * part for share, part in zip(shares, sums, strict=True))
        inverse = 1.0 / total
        for b in range(blocks):
            weight = shares[b] * inverse
            w_ref[0, g * blocks + b : g * blocks + b + 1, :] = weight
            if b < per:
                here = slice(b * BLOCK, (b + 1) * BLOCK)
                p_low[here, g * rows : (g + 1) * rows] = (e_ref[g, here, :] * weight).astype(
                    jnp.bfloat16
                )
    dv_ref[:HD, :], dv_ref[HD:, :] = encode(dot(p_low[...], g_all[...]).T)


def values_kernel(group, g_ref, w_ref, *refs):
    e_refs, dv_refs = refs[: REACH - 1], refs[REACH - 1 : 2 * (REACH - 1)]
    p_low, g_all = refs[2 * (REACH - 1) :]
    rows = g_ref.shape[0]
    per = rows // BLOCK
    blocks = REACH * per
    for g in range(group):
        g_all[g * rows : (g + 1) * rows, :] = g_ref[:, g * HD : (g + 1) * HD]
        for j in range(REACH - 1):
            for b in range(per):
                here = slice(b * BLOCK, (b + 1) * BLOCK)
                at = g * blocks + (j + 1) * per + b
                probs = e_refs[j][g, here, :] * w_ref[0, at : at + 1, :]
                there = slice(j * rows + b * BLOCK, j * rows + (b + 1) * BLOCK)
                p_low[there, g * rows : (g + 1) * rows] = probs.astype(jnp.bfloat16)
    dv = dot(p_low[...], g_all[...])
    for j in range(REACH - 1):
        dv_refs[j][...] = dv[j * rows : (j + 1) * rows, :].T


def grads_kernel(group, rows, skip, q_ref, g_ref, gain_ref, w_ref, *refs):
    e_refs, k_refs, v_refs = (refs[i * REACH : (i + 1) * REACH] for i in range(3))
    refs = refs[3 * REACH + skip :]
    o_ref, dq_ref, gain_out, *dk_refs = refs[: REACH + 3]
    k_t, v_t, v_all, p_all, ds_all, q_all = refs[REACH + 3 :]
    per = rows // BLOCK
    blocks = REACH * per
    factor = 1.0 / math.sqrt(HD)
    for j in range(REACH):
        part = slice(j * rows, (j + 1) * rows)
        v_all[part, :] = v_refs[j][...]
        k_t[:, part] = k_refs[j][...].T
        v_t[:, part] = v_refs[j][...].T

    def probs_of(g, b):
        here = slice(b % per * BLOCK, (b % per + 1) * BLOCK)
        at = g * blocks + b
        return e_refs[b // per][g, here, :] * w_ref[0, at : at + 1, :]

    for g in range(group):
        cols = slice(g * HD, (g + 1) * HD)
        mine = slice(g * rows, (g + 1) * rows)
        q32 = q_ref[:, cols].astype(jnp.float32)
        gain = gain_ref[:, cols]
        q_all[mine, :] = (q32 * gain).astype(jnp.bfloat16)
        for b in range(blocks):
            p_all[g % 2, b * BLOCK : (b + 1) * BLOCK, :] = probs_of(g, b).astype(jnp.bfloat16)
        out_t = dot(v_t[...], p_all[g % 2]).astype(jnp.bfloat16)
        o_ref[:, cols] = out_t.T
        g_t = g_ref[:, cols].T
        delta = jnp.sum(g_t.astype(jnp.float32) * out_t.astype(jnp.float32), axis=0, keepdims=True)
        for b in range(blocks):
            here = slice(b * BLOCK, (b + 1) * BLOCK)
            ds = probs_of(g, b) * (dot(v_all[here, :], g_t) - delta)
            ds_all[here, mine] = ds.astype(jnp.bfloat16)
        dscaled = (dot(k_t[...], ds_all[:, mine]) * factor).T
        dq_ref[:, cols] = (dscaled * gain).astype(jnp.bfloat16)
        gain_out[:, cols] = jnp.sum(dscaled * q32, axis=0, keepdims=True)
    dk = dot(ds_all[...], q_all[...]) * factor
    dk_refs[0][:HD, :], dk_refs[0][HD:, :] = encode(dk[:rows, :].T)
    for j in range(1, REACH):
        dk_refs[j][...] = dk[j * rows : (j + 1) * rows, :].T


def hop_kernel(kv_count, last, message, part, out):
    for c in range(kv_count):
        at, here = c * CODE_ROWS, slice(c * HD, (c + 1) * HD)
        total = part[here, :] + decode(
            message[at : at + HD, :], message[at + HD : at + CODE_ROWS, :]
        )
        if last:
            out[:, here] = total.T.astype(jnp.bfloat16)
        else:
            out[at : at + HD, :], out[at + HD : at + CODE_ROWS, :] = encode(total)


def hop(message, part, last):
    kv_channels, rows = part.shape
    shape = jax.ShapeDtypeStruct((rows, kv_channels), jnp.bfloat16) if last else message
    return pl.pallas_call(
        functools.partial(hop_kernel, kv_channels // HD, last),
        out_shape=jax.ShapeDtypeStruct(shape.shape, shape.dtype),
        compiler_params=pltpu.CompilerParams(vmem_limit_bytes=16 * 2**20),
        cost_estimate=pl.CostEstimate(
            flops=10 * part.size, bytes_accessed=8 * part.size, transcendentals=0
        ),
        name="last_hop" if last else "hop",
    )(message, part)


class Shapes:
    def __init__(self, queries, keys, first=0):
        self.rows, self.channels = queries.shape
        self.kv_channels = keys.shape[1]
        self.kv_count = self.kv_channels // HD
        self.group = self.channels // self.kv_channels
        self.blocks = REACH * self.rows // BLOCK
        self.stat_rows = self.group * self.rows // BLOCK
        rows, group = self.rows, self.group
        self.wide = pl.BlockSpec((rows, group * HD), lambda c, *_: (0, c + first))
        self.line = pl.BlockSpec((1, group * HD), lambda c, *_: (0, c + first))
        self.thin = pl.BlockSpec((rows, HD), lambda c, *_: (0, c + first))
        self.code = pl.BlockSpec((CODE_ROWS, rows), lambda c, *_: (c + first, 0))
        self.part = pl.BlockSpec((HD, rows), lambda c, *_: (c + first, 0))
        self.heads = pl.BlockSpec((group, rows, rows), lambda c, *_: (c + first, 0, 0))
        self.stat = pl.BlockSpec((1, self.stat_rows, rows), lambda c, *_: (c + first, 0, 0))
        self.weight = pl.BlockSpec(
            (1, group * self.blocks, rows), lambda c, *_: (c + first, 0, 0)
        )

    def array(self, dtype, *shape):
        return jax.ShapeDtypeStruct(shape, dtype)

    def heads_array(self):
        return self.array(jnp.float32, self.kv_count * self.group, self.rows, self.rows)

    def stat_array(self):
        return self.array(jnp.float32, self.kv_count, self.stat_rows, self.rows)

    def weight_array(self):
        return self.array(jnp.float32, self.kv_count, self.group * self.blocks, self.rows)

    def code_array(self):
        return self.array(jnp.int16, self.kv_count * CODE_ROWS, self.rows)

    def part_array(self):
        return self.array(jnp.float32, self.kv_channels, self.rows)

    def cost(self, products, chunks, exps, count=None):
        heads = (self.kv_count if count is None else count) * self.group
        size = heads * chunks * self.rows * self.rows
        return pl.CostEstimate(
            flops=2 * products * size * HD, bytes_accessed=4 * size, transcendentals=exps * size
        )


def chunk_scores(queries, gain, keys, own):
    s = Shapes(queries, keys)
    return pl.pallas_call(
        functools.partial(scores_kernel, s.group, own),
        out_shape=[s.heads_array(), s.stat_array(), s.stat_array()],
        grid=(s.kv_count,),
        in_specs=[s.wide, s.line, s.thin],
        out_specs=[s.heads, s.stat, s.stat],
        cost_estimate=s.cost(1, 1, 1),
        name="scores_own" if own else "scores",
    )(queries, gain, keys)


def far_scores(lo, queries, out_grad, gain, keys, stats):
    s = Shapes(queries, keys)
    return pl.pallas_call(
        functools.partial(far_kernel, s.group),
        out_shape=[s.heads_array(), s.weight_array(), s.code_array()],
        grid_spec=pltpu.PrefetchScalarGridSpec(
            num_scalar_prefetch=1,
            grid=(s.kv_count,),
            in_specs=[s.wide, s.wide, s.line, s.thin] + [s.stat] * len(stats),
            out_specs=[s.heads, s.weight, s.code],
            scratch_shapes=[
                pltpu.VMEM((s.rows, s.group * s.rows), jnp.bfloat16),
                pltpu.VMEM((s.group * s.rows, HD), jnp.bfloat16),
            ],
        ),
        cost_estimate=s.cost(2, 1, 1),
        name="far_scores",
    )(lo, queries, out_grad, gain, keys, *stats)


def near_values(queries, keys, out_grad, weights, heads):
    s = Shapes(queries, keys)
    near = REACH - 1
    return pl.pallas_call(
        functools.partial(values_kernel, s.group),
        out_shape=[s.part_array()] * near,
        grid=(s.kv_count,),
        in_specs=[s.wide, s.weight] + [s.heads] * near,
        out_specs=[s.part] * near,
        scratch_shapes=[
            pltpu.VMEM((near * s.rows, s.group * s.rows), jnp.bfloat16),
            pltpu.VMEM((s.group * s.rows, HD), jnp.bfloat16),
        ],
        cost_estimate=s.cost(1, near, 0),
        name="near_values",
    )(out_grad, weights, *heads)


def attention_grads(first, count, before, queries, out_grad, gain, weights, heads, keys, values):
    s = Shapes(queries, keys[0], first)
    width = REACH * s.rows
    n_in = 4 + 3 * REACH
    return pl.pallas_call(
        functools.partial(grads_kernel, s.group, s.rows, len(before)),
        out_shape=[s.array(jnp.bfloat16, s.rows, s.channels)] * 2
        + [s.array(jnp.float32, 1, s.channels), s.code_array()]
        + [s.part_array()] * (REACH - 1),
        grid=(count,),
        in_specs=[s.wide, s.wide, s.line, s.weight]
        + [s.heads] * REACH
        + [s.thin] * (2 * REACH)
        + [pl.BlockSpec(memory_space=pl.ANY)] * len(before),
        out_specs=[s.wide, s.wide, s.line, s.code] + [s.part] * (REACH - 1),
        scratch_shapes=[
            pltpu.VMEM((HD, width), jnp.bfloat16),
            pltpu.VMEM((HD, width), jnp.bfloat16),
            pltpu.VMEM((width, HD), jnp.bfloat16),
            pltpu.VMEM((2, width, s.rows), jnp.bfloat16),
            pltpu.VMEM((width, s.group * s.rows), jnp.bfloat16),
            pltpu.VMEM((s.group * s.rows, HD), jnp.bfloat16),
        ],
        input_output_aliases={n_in + i: i for i in range(len(before))},
        cost_estimate=s.cost(4, REACH, 0, count),
    )(queries, out_grad, gain, weights, *heads, *keys, *values, *before)


def step(queries, global_keys, global_values, out_grad, query_gain, doc_start):
    rows = queries.shape[1]
    device = lax.axis_index("ctx")
    q, do = queries[0], out_grad[0]
    gain = query_gain[None]
    together = lax.optimization_barrier
    lo = doc_start[0] * BLOCK - (device - (REACH - 1)) * rows
    own_keys, own_values = global_keys[0], global_values[0]
    near = [chunk_scores(q, gain, own_keys, True)]
    keys, values = [own_keys], [own_values]
    for i in range(1, REACH):
        keys.insert(0, shifted(keys[0], 1))
        if i < REACH - 1:
            near.insert(0, chunk_scores(q, gain, keys[0], False))
            values.insert(0, shifted(values[0], 1))
    keys[0], values[0] = together((keys[0], values[0]))
    values.insert(0, shifted(values[0], 1))
    half = own_keys.shape[1] // HD // 2

    stats = [stat for _, *pair in near for stat in pair]
    far, weights, moved = far_scores(lo, q, do, gain, keys[0], stats)
    heads = [far] + [e for e, *_ in near]
    moved = shifted(moved, -1)
    dv = near_values(q, own_keys, do, weights, heads[1:])
    moved = shifted(hop(moved, dv[0], False), -1)
    early = attention_grads(0, half, [], q, do, gain, weights, heads, keys, values)
    moved = shifted(hop(moved, dv[1], False), -1)
    attn_out, query_grad, gain_term, dk_moved, *dk = attention_grads(
        half, half, early, q, do, gain, weights, heads, keys, values
    )
    dk_moved = shifted(dk_moved, -1)
    both = ("dp", "ctx")
    total = exchange(gain_term[0], both, 64, 128)
    value_grad = hop(moved, dv[2], True)
    dk_moved, total = together((dk_moved, total))
    dk_moved = shifted(hop(dk_moved, dk[0], False), -1)
    total = exchange(total, both, 8, 16)
    dk_moved, total = together((dk_moved, total))
    dk_moved = shifted(hop(dk_moved, dk[1], False), -1)
    total = exchange(total, both, 1, 2)
    gain_grad = exchange(total, both, 4, 32)
    key_grad = hop(dk_moved, dk[2], True)
    return (
        attn_out[None],
        query_grad[None],
        key_grad[None],
        value_grad[None],
        gain_grad,
    )


def solution(mesh):
    rows = P("dp", "ctx", None)
    return jax.shard_map(
        step,
        mesh=mesh,
        in_specs=(rows, rows, rows, rows, P(), P("dp", "ctx")),
        out_specs=(rows, rows, rows, rows, P()),
        check_vma=False,
    )
```

time: 143 us -> 141 us (0.986)
  the two profiles are of different devices: /device:TPU:22 before, /device:TPU:1 now
where the time goes in v3:
time: 141 us
  starting transfers between devices  64.8 us (46%)
  Pallas kernels  51.6 us (37%)
  waiting for transfers between devices  17.1 us (12%)
  local copies, waits for them, and re-layouts  4.2 us (3%)
  other arithmetic  1.88 us (1%)
    ppermute x12, starting transfers between devices, exchange(): lax.ppermute(value, axis, [(i, i ^ bits) for i in range(count)])  32.6 us
    ppermute x12, starting transfers between devices, shifted(): return lax.ppermute(value, 'ctx', pairs)  32.2 us
    pallas_call x2, Pallas kernels, attention_grads(): pl.pallas_call(functools.partial(grads_kernel, s.group, s.rows, len(befor...  18.3 us
    pallas_call x3, Pallas kernels, chunk_scores(): pl.pallas_call(functools.partial(scores_kernel, s.group, own), out_shape=...  15.5 us
    ppermute x12, waiting for transfers between devices, exchange(): lax.ppermute(value, axis, [(i, i ^ bits) for i in range(count)])  11.7 us
    pallas_call x1, Pallas kernels, near_values(): pl.pallas_call(functools.partial(values_kernel, s.group), out_shape=[s.pa...  8.34 us
    pallas_call x1, Pallas kernels, far_scores(): pl.pallas_call(functools.partial(far_kernel, s.group), out_shape=[s.heads...  7.08 us
    ppermute x12, waiting for transfers between devices, shifted(): return lax.ppermute(value, 'ctx', pairs)  5.39 us
  transfers between devices with their start and end apart: 24, of which 9 were waited for; matrix products, arithmetic and copies ran while one was open for 2% of the time, Pallas kernels for 23%

profile of v3, /device:TPU:1, one launch (start us, length us, event | category | flops | bytes accessed | tf_op | source)
XLA Modules:
  0.0 140.5 jit_solution(3817439887260027840)
XLA Ops:
  0.6 4.4 %collective-permute-start = (bf16[256,512]{1,0:T(8,128)(2,1)}, bf16[256,512]{1,0:T(8,128)(2,1)S(1)}, u32[]{:S(2)}, u32[]{:S(2)}) collective-permute-start(bf16[256,512]{1,0:T(8,128)(2,1)} %bitcast.22), channel_id=1, source_target_pairs={{0,1},{1,2},{2,3},{3,4},{4,5},{5,6},{6,7},{7,8},{8,9},{9,10},{10,1... | collective-permute-start | bytes 786440 | tf_op jit(solution)/shard_map/ppermute | solution.py:26
  5.0 3.5 %collective-permute-start.3 = (bf16[256,512]{1,0:T(8,128)(2,1)}, bf16[256,512]{1,0:T(8,128)(2,1)S(1)}, u32[]{:S(2)}, u32[]{:S(2)}) collective-permute-start(bf16[256,512]{1,0:T(8,128)(2,1)} %bitcast.26), channel_id=1, source_target_pairs={{0,1},{1,2},{2,3},{3,4},{4,5},{5,6},{6,7},{7,8},{8,9},{9,10},{10,1... | collective-permute-start | bytes 786440 | tf_op jit(solution)/shard_map/ppermute | solution.py:26
  8.6 1.7 %collective-permute-done.k_ref.refs_6_ = bf16[256,512]{1,0:T(8,128)(2,1)S(1)} collective-permute-done((bf16[256,512]{1,0:T(8,128)(2,1)}, bf16[256,512]{1,0:T(8,128)(2,1)S(1)}, u32[]{:S(2)}, u32[]{:S(2)}) %collective-permute-start) | collective-permute-done | bytes 262176 | tf_op jit(solution)/shard_map/ppermute | solution.py:26
  10.3 4.0 %collective-permute-start.1 = (bf16[256,512]{1,0:T(8,128)(2,1)S(1)}, bf16[256,512]{1,0:T(8,128)(2,1)S(1)}, u32[]{:S(2)}, u32[]{:S(2)}) collective-permute-start(bf16[256,512]{1,0:T(8,128)(2,1)S(1)} %collective-permute-done.k_ref.refs_6_), channel_id=1, source_target_pairs={{0,1},{1,2},{2,3},{3,4},{4,5},{5,6},{6,7},{7,8},{8,9},{9,10},{10,1... | collective-permute-start | bytes 786440 | tf_op jit(solution)/shard_map/ppermute | solution.py:26
  14.3 1.6 %collective-permute-done.3.refs_10_ = bf16[256,512]{1,0:T(8,128)(2,1)S(1)} collective-permute-done((bf16[256,512]{1,0:T(8,128)(2,1)}, bf16[256,512]{1,0:T(8,128)(2,1)S(1)}, u32[]{:S(2)}, u32[]{:S(2)}) %collective-permute-start.3) | collective-permute-done | bytes 262176 | tf_op jit(solution)/shard_map/ppermute | solution.py:26
  15.9 4.0 %collective-permute-start.4 = (bf16[256,512]{1,0:T(8,128)(2,1)S(1)}, bf16[256,512]{1,0:T(8,128)(2,1)S(1)}, u32[]{:S(2)}, u32[]{:S(2)}) collective-permute-start(bf16[256,512]{1,0:T(8,128)(2,1)S(1)} %collective-permute-done.3.refs_10_), channel_id=1, source_target_pairs={{0,1},{1,2},{2,3},{3,4},{4,5},{5,6},{6,7},{7,8},{8,9},{9,10},{10,1... | collective-permute-start | bytes 786440 | tf_op jit(solution)/shard_map/ppermute | solution.py:26
  19.9 1.5 %collective-permute-done.1.k_ref.refs_5_ = bf16[256,512]{1,0:T(8,128)(2,1)S(1)} collective-permute-done((bf16[256,512]{1,0:T(8,128)(2,1)S(1)}, bf16[256,512]{1,0:T(8,128)(2,1)S(1)}, u32[]{:S(2)}, u32[]{:S(2)}) %collective-permute-start.1) | collective-permute-done | bytes 262176 | tf_op jit(solution)/shard_map/ppermute | solution.py:26
  21.4 4.1 %collective-permute-start.2 = (bf16[256,512]{1,0:T(8,128)(2,1)S(1)}, bf16[256,512]{1,0:T(8,128)(2,1)S(1)}, u32[]{:S(2)}, u32[]{:S(2)}) collective-permute-start(bf16[256,512]{1,0:T(8,128)(2,1)S(1)} %collective-permute-done.1.k_ref.refs_5_), channel_id=1, source_target_pairs={{0,1},{1,2},{2,3},{3,4},{4,5},{5,6},{6,7},{7,8},{8,9},{9,10},{10,1... | collective-permute-start | bytes 786440 | tf_op jit(solution)/shard_map/ppermute | solution.py:26
  26.9 5.2 %scores_own.1 = (f32[20,256,256]{2,1,0:T(8,128)}, f32[4,10,256]{2,1,0:T(8,128)}, f32[4,10,256]{2,1,0:T(8,128)}) custom-call(bf16[256,2560]{1,0:T(8,128)(2,1)} %bitcast.14, f32[1,2560]{1,0:T(1,128)} %broadcast_in_dim.15.gain_ref, bf16[256,512]{1,0:T(8,128)(2,1)} %bitcast.23), custom_call_target="tpu_custom_call" | custom-call | flops 335544320 | bytes 5242880 | tf_op jit(solution)/shard_map/scores_own/pallas_call | solution.py:267
  32.7 4.1 %collective-permute-start.5 = (bf16[256,512]{1,0:T(8,128)(2,1)S(1)}, bf16[256,512]{1,0:T(8,128)(2,1)S(1)}, u32[]{:S(2)}, u32[]{:S(2)}) collective-permute-start(bf16[256,512]{1,0:T(8,128)(2,1)S(1)} %collective-permute-done.4.refs_9_), channel_id=1, source_target_pairs={{0,1},{1,2},{2,3},{3,4},{4,5},{5,6},{6,7},{7,8},{8,9},{9,10},{10,1... | collective-permute-start | bytes 786440 | tf_op jit(solution)/shard_map/ppermute | solution.py:26
  37.3 5.1 %scores.3 = (f32[20,256,256]{2,1,0:T(8,128)}, f32[4,10,256]{2,1,0:T(8,128)}, f32[4,10,256]{2,1,0:T(8,128)}) custom-call(bf16[256,2560]{1,0:T(8,128)(2,1)} %bitcast.15, f32[1,2560]{1,0:T(1,128)} %broadcast_in_dim.15.gain_ref, bf16[256,512]{1,0:T(8,128)(2,1)} %copy-done.7), custom_call_target="tpu_custom_call" | custom-call | flops 335544320 | bytes 5242880 | tf_op jit(solution)/shard_map/scores/pallas_call | solution.py:267
  42.5 5.1 %scores.2 = (f32[20,256,256]{2,1,0:T(8,128)}, f32[4,10,256]{2,1,0:T(8,128)}, f32[4,10,256]{2,1,0:T(8,128)}) custom-call(bf16[256,2560]{1,0:T(8,128)(2,1)} %bitcast.16, f32[1,2560]{1,0:T(1,128)} %broadcast_in_dim.15.gain_ref, bf16[256,512]{1,0:T(8,128)(2,1)} %copy-done.9), custom_call_target="tpu_custom_call" | custom-call | flops 335544320 | bytes 5242880 | tf_op jit(solution)/shard_map/scores/pallas_call | solution.py:267
  47.6 7.1 %far_scores.1 = (f32[20,256,256]{2,1,0:T(8,128)}, f32[4,40,256]{2,1,0:T(8,128)}, s16[576,256]{1,0:T(8,128)(2,1)}) custom-call(s32[2]{0:T(128)} %subtract_bitcast_fusion.lo, bf16[256,2560]{1,0:T(8,128)(2,1)} %bitcast.17, bf16[256,2560]{1,0:T(8,128)(2,1)} %bitcast.10, f32[1,2560]{1,0:T(1,128)} %broadcast_in_dim.15.gain_ref, bf16[256,512]{1,0:T(8,128)(2,1)} %copy-done.6, ...), custom_call_target="tpu_custom_call" | custom-call | flops 671088640 | bytes 5242880 | tf_op jit(solution)/shard_map/far_scores/pallas_call | solution.py:280
  55.4 9.1 %shard_map.101 = (bf16[256,2560]{1,0:T(8,128)(2,1)}, bf16[256,2560]{1,0:T(8,128)(2,1)}, f32[1,2560]{1,0:T(1,128)}, s16[576,256]{1,0:T(8,128)(2,1)}, f32[512,256]...) custom-call(bf16[256,2560]{1,0:T(8,128)(2,1)} %bitcast.18, bf16[256,2560]{1,0:T(8,128)(2,1)} %bitcast.11, ...), custom_call_target="tpu_custom_call" | custom-call | flops 2684354560 | bytes 10485760 | tf_op jit(solution)/shard_map/pallas_call | solution.py:320
  64.5 9.2 %shard_map.102 = (bf16[256,2560]{1,0:T(8,128)(2,1)}, bf16[256,2560]{1,0:T(8,128)(2,1)}, f32[1,2560]{1,0:T(1,128)}, s16[576,256]{1,0:T(8,128)(2,1)}, f32[512,256]...) custom-call(bf16[256,2560]{1,0:T(8,128)(2,1)} %bitcast.19, ...), custom_call_target="tpu_custom_call", output_to_operand_aliasing={{0}: (16, {}), {1}: (17, {}), {2}: (18, {}), {3}: (19, {}),... | custom-call | flops 2684354560 | bytes 10485760 | tf_op jit(solution)/shard_map/pallas_call | solution.py:320
  75.8 2.8 %collective-permute-start.9 = (f32[2560]{0:T(1024)S(1)}, f32[2560]{0:T(1024)S(1)}, u32[]{:S(2)}, u32[]{:S(2)}) collective-permute-start(f32[2560]{0:T(1024)S(1)} %reduce), channel_id=1, source_target_pairs={{0,192},{1,193},{2,194},{3,195},{4,196},{5,197},{6,198},{7,199},{8... | collective-permute-start | bytes 30728 | tf_op jit(solution)/shard_map/ppermute | solution.py:32
  80.5 2.1 %collective-permute-done.8 = f32[2560]{0:T(1024)S(1)} collective-permute-done((f32[2560]{0:T(1024)S(1)}, f32[2560]{0:T(1024)S(1)}, u32[]{:S(2)}, u32[]{:S(2)}) %collective-permute-start.8) | collective-permute-done | bytes 10272 | tf_op jit(solution)/shard_map/ppermute | solution.py:32
  85.2 8.3 %near_values.1 = (f32[512,256]{1,0:T(8,128)}, f32[512,256]{1,0:T(8,128)}, f32[512,256]{1,0:T(8,128)}) custom-call(bf16[256,2560]{1,0:T(8,128)(2,1)} %bitcast.13, f32[4,40,256]{2,1,0:T(8,128)} %get-tuple-element.47.w_ref, f32[20,256,256]{2,1,0:T(8,128)} %get-tuple-element.49.refs_1_.refs_0_, f32[20,256,256]{2,1,0:T(8,128)} %get-tuple-element.50.refs_2_.refs_1_, ...), custom_call_target="tpu_custom_call" | custom-call | flops 1006632960 | bytes 15728640 | tf_op jit(solution)/shard_map/near_values/pallas_call | solution.py:301
  94.8 1.4 %collective-permute-start.16 = (s16[576,256]{1,0:T(8,128)(2,1)S(1)}, s16[576,256]{1,0:T(8,128)(2,1)S(1)}, u32[]{:S(2)}, u32[]{:S(2)}) collective-permute-start(s16[576,256]{1,0:T(8,128)(2,1)S(1)} %hop.6), channel_id=1, source_target_pairs={{1,0},{2,1},{3,2},{4,3},{5,4},{6,5},{7,6},{8,7},{9,8},{10,9},{11,1... | collective-permute-start | bytes 884744 | tf_op jit(solution)/shard_map/ppermute | solution.py:26
  96.3 11.0 %collective-permute-start.13 = (f32[2560]{0:T(1024)S(1)}, f32[2560]{0:T(1024)S(1)}, u32[]{:S(2)}, u32[]{:S(2)}) collective-permute-start(f32[2560]{0:T(1024)S(1)} %add_add_fusion.3), channel_id=1, source_target_pairs={{0,24},{1,25},{2,26},{3,27},{4,28},{5,29},{6,30},{7,31},{8,16},{9,... | collective-permute-start | bytes 30728 | tf_op jit(solution)/shard_map/ppermute | solution.py:32
  108.4 3.0 %collective-permute-done.12 = f32[2560]{0:T(1024)S(1)} collective-permute-done((f32[2560]{0:T(1024)S(1)}, f32[2560]{0:T(1024)S(1)}, u32[]{:S(2)}, u32[]{:S(2)}) %collective-permute-start.12) | collective-permute-done | bytes 10272 | tf_op jit(solution)/shard_map/ppermute | solution.py:32
  111.3 1.8 %collective-permute-start.20 = (f32[2560]{0:T(1024)S(1)}, f32[2560]{0:T(1024)S(1)}, u32[]{:S(2)}, u32[]{:S(2)}) collective-permute-start(f32[2560]{0:T(1024)S(1)} %add_add_fusion.2), channel_id=1, source_target_pairs={{0,3},{1,2},{2,1},{3,0},{4,7},{5,6},{6,5},{7,4},{8,11},{9,10},{10,... | collective-permute-start | bytes 30728 | tf_op jit(solution)/shard_map/ppermute | solution.py:32
  118.1 13.6 %collective-permute-start.23 = (f32[2560]{0:T(1024)S(1)}, f32[2560]{0:T(1024)S(1)}, u32[]{:S(2)}, u32[]{:S(2)}) collective-permute-start(f32[2560]{0:T(1024)S(1)} %add_add_fusion.1), channel_id=1, source_target_pairs={{0,36},{1,37},{2,38},{3,39},{4,32},{5,33},{6,34},{7,35},{8,44},{9,... | collective-permute-start | bytes 30728 | tf_op jit(solution)/shard_map/ppermute | solution.py:32
  133.1 5.1 %collective-permute-done.21 = f32[2560]{0:T(1024)S(1)} collective-permute-done((f32[2560]{0:T(1024)S(1)}, f32[2560]{0:T(1024)S(1)}, u32[]{:S(2)}, u32[]{:S(2)}) %collective-permute-start.21) | collective-permute-done | bytes 10272 | tf_op jit(solution)/shard_map/ppermute | solution.py:32
  (72 shorter events, 20.6 us)
Async XLA Ops:
  0.6 9.7 %collective-permute-start = (bf16[256,512]{1,0:T(8,128)(2,1)}, bf16[256,512]{1,0:T(8,128)(2,1)S(1)}, u32[]{:S(2)}, u32[]{:S(2)}) collective-permute-start(bf16[256,512]{1,0:T(8,128)(2,1)} %bitcast.22), channel_id=1, source_target_pairs={{0,1},{1,2},{2,3},{3,4},{4,5},{5,6},{6,7},{7,8},{8,9},{9,10},{10,1... | collective-permute-start | bytes 786440 | tf_op jit(solution)/shard_map/ppermute | solution.py:26
  5.0 10.9 %collective-permute-start.3 = (bf16[256,512]{1,0:T(8,128)(2,1)}, bf16[256,512]{1,0:T(8,128)(2,1)S(1)}, u32[]{:S(2)}, u32[]{:S(2)}) collective-permute-start(bf16[256,512]{1,0:T(8,128)(2,1)} %bitcast.26), channel_id=1, source_target_pairs={{0,1},{1,2},{2,3},{3,4},{4,5},{5,6},{6,7},{7,8},{8,9},{9,10},{10,1... | collective-permute-start | bytes 786440 | tf_op jit(solution)/shard_map/ppermute | solution.py:26
  10.3 11.1 %collective-permute-start.1 = (bf16[256,512]{1,0:T(8,128)(2,1)S(1)}, bf16[256,512]{1,0:T(8,128)(2,1)S(1)}, u32[]{:S(2)}, u32[]{:S(2)}) collective-permute-start(bf16[256,512]{1,0:T(8,128)(2,1)S(1)} %collective-permute-done.k_ref.refs_6_), channel_id=1, source_target_pairs={{0,1},{1,2},{2,3},{3,4},{4,5},{5,6},{6,7},{7,8},{8,9},{9,10},{10,1... | collective-permute-start | bytes 786440 | tf_op jit(solution)/shard_map/ppermute | solution.py:26
  15.9 16.2 %collective-permute-start.4 = (bf16[256,512]{1,0:T(8,128)(2,1)S(1)}, bf16[256,512]{1,0:T(8,128)(2,1)S(1)}, u32[]{:S(2)}, u32[]{:S(2)}) collective-permute-start(bf16[256,512]{1,0:T(8,128)(2,1)S(1)} %collective-permute-done.3.refs_10_), channel_id=1, source_target_pairs={{0,1},{1,2},{2,3},{3,4},{4,5},{5,6},{6,7},{7,8},{8,9},{9,10},{10,1... | collective-permute-start | bytes 786440 | tf_op jit(solution)/shard_map/ppermute | solution.py:26
  21.4 11.2 %collective-permute-start.2 = (bf16[256,512]{1,0:T(8,128)(2,1)S(1)}, bf16[256,512]{1,0:T(8,128)(2,1)S(1)}, u32[]{:S(2)}, u32[]{:S(2)}) collective-permute-start(bf16[256,512]{1,0:T(8,128)(2,1)S(1)} %collective-permute-done.1.k_ref.refs_5_), channel_id=1, source_target_pairs={{0,1},{1,2},{2,3},{3,4},{4,5},{5,6},{6,7},{7,8},{8,9},{9,10},{10,1... | collective-permute-start | bytes 786440 | tf_op jit(solution)/shard_map/ppermute | solution.py:26
  32.7 22.0 %collective-permute-start.5 = (bf16[256,512]{1,0:T(8,128)(2,1)S(1)}, bf16[256,512]{1,0:T(8,128)(2,1)S(1)}, u32[]{:S(2)}, u32[]{:S(2)}) collective-permute-start(bf16[256,512]{1,0:T(8,128)(2,1)S(1)} %collective-permute-done.4.refs_9_), channel_id=1, source_target_pairs={{0,1},{1,2},{2,3},{3,4},{4,5},{5,6},{6,7},{7,8},{8,9},{9,10},{10,1... | collective-permute-start | bytes 786440 | tf_op jit(solution)/shard_map/ppermute | solution.py:26
  73.7 8.9 %collective-permute-start.6 = (s16[576,256]{1,0:T(8,128)(2,1)}, s16[576,256]{1,0:T(8,128)(2,1)S(1)}, u32[]{:S(2)}, u32[]{:S(2)}) collective-permute-start(s16[576,256]{1,0:T(8,128)(2,1)} %get-tuple-element.62), channel_id=1, source_target_pairs={{1,0},{2,1},{3,2},{4,3},{5,4},{6,5},{7,6},{8,7},{9,8},{10,9},{11,1... | collective-permute-start | bytes 884744 | tf_op jit(solution)/shard_map/ppermute | solution.py:26
  75.8 4.8 %collective-permute-start.9 = (f32[2560]{0:T(1024)S(1)}, f32[2560]{0:T(1024)S(1)}, u32[]{:S(2)}, u32[]{:S(2)}) collective-permute-start(f32[2560]{0:T(1024)S(1)} %reduce), channel_id=1, source_target_pairs={{0,192},{1,193},{2,194},{3,195},{4,196},{5,197},{6,198},{7,199},{8... | collective-permute-start | bytes 30728 | tf_op jit(solution)/shard_map/ppermute | solution.py:32
  78.6 4.0 %collective-permute-start.8 = (f32[2560]{0:T(1024)S(1)}, f32[2560]{0:T(1024)S(1)}, u32[]{:S(2)}, u32[]{:S(2)}) collective-permute-start(f32[2560]{0:T(1024)S(1)} %reduce), channel_id=1, source_target_pairs={{0,128},{1,129},{2,130},{3,131},{4,132},{5,133},{6,134},{7,135},{8... | collective-permute-start | bytes 30728 | tf_op jit(solution)/shard_map/ppermute | solution.py:32
  78.9 3.7 %collective-permute-start.7 = (f32[2560]{0:T(1024)S(1)}, f32[2560]{0:T(1024)S(1)}, u32[]{:S(2)}, u32[]{:S(2)}) collective-permute-start(f32[2560]{0:T(1024)S(1)} %reduce), channel_id=1, source_target_pairs={{0,64},{1,65},{2,66},{3,67},{4,68},{5,69},{6,70},{7,71},{8,72},{9,... | collective-permute-start | bytes 30728 | tf_op jit(solution)/shard_map/ppermute | solution.py:32
  79.3 14.3 %collective-permute-start.15 = (s16[576,256]{1,0:T(8,128)(2,1)S(1)}, s16[576,256]{1,0:T(8,128)(2,1)S(1)}, u32[]{:S(2)}, u32[]{:S(2)}) collective-permute-start(s16[576,256]{1,0:T(8,128)(2,1)S(1)} %copy-done.12), channel_id=1, source_target_pairs={{1,0},{2,1},{3,2},{4,3},{5,4},{6,5},{7,6},{8,7},{9,8},{10,9},{11,1... | collective-permute-start | bytes 884744 | tf_op jit(solution)/shard_map/ppermute | solution.py:26
  83.9 27.5 %collective-permute-start.10 = (s16[576,256]{1,0:T(8,128)(2,1)S(1)}, s16[576,256]{1,0:T(8,128)(2,1)S(1)}, u32[]{:S(2)}, u32[]{:S(2)}) collective-permute-start(s16[576,256]{1,0:T(8,128)(2,1)S(1)} %hop.4), channel_id=1, source_target_pairs={{1,0},{2,1},{3,2},{4,3},{5,4},{6,5},{7,6},{8,7},{9,8},{10,9},{11,1... | collective-permute-start | bytes 884744 | tf_op jit(solution)/shard_map/ppermute | solution.py:26
  94.8 20.1 %collective-permute-start.16 = (s16[576,256]{1,0:T(8,128)(2,1)S(1)}, s16[576,256]{1,0:T(8,128)(2,1)S(1)}, u32[]{:S(2)}, u32[]{:S(2)}) collective-permute-start(s16[576,256]{1,0:T(8,128)(2,1)S(1)} %hop.6), channel_id=1, source_target_pairs={{1,0},{2,1},{3,2},{4,3},{5,4},{6,5},{7,6},{8,7},{9,8},{10,9},{11,1... | collective-permute-start | bytes 884744 | tf_op jit(solution)/shard_map/ppermute | solution.py:26
  96.3 12.1 %collective-permute-start.13 = (f32[2560]{0:T(1024)S(1)}, f32[2560]{0:T(1024)S(1)}, u32[]{:S(2)}, u32[]{:S(2)}) collective-permute-start(f32[2560]{0:T(1024)S(1)} %add_add_fusion.3), channel_id=1, source_target_pairs={{0,24},{1,25},{2,26},{3,27},{4,28},{5,29},{6,30},{7,31},{8,16},{9,... | collective-permute-start | bytes 30728 | tf_op jit(solution)/shard_map/ppermute | solution.py:32
  107.3 4.0 %collective-permute-start.12 = (f32[2560]{0:T(1024)S(1)}, f32[2560]{0:T(1024)S(1)}, u32[]{:S(2)}, u32[]{:S(2)}) collective-permute-start(f32[2560]{0:T(1024)S(1)} %add_add_fusion.3), channel_id=1, source_target_pairs={{0,16},{1,17},{2,18},{3,19},{4,20},{5,21},{6,22},{7,23},{8,24},{9,... | collective-permute-start | bytes 30728 | tf_op jit(solution)/shard_map/ppermute | solution.py:32
  107.5 3.8 %collective-permute-start.11 = (f32[2560]{0:T(1024)S(1)}, f32[2560]{0:T(1024)S(1)}, u32[]{:S(2)}, u32[]{:S(2)}) collective-permute-start(f32[2560]{0:T(1024)S(1)} %add_add_fusion.3), channel_id=1, source_target_pairs={{0,8},{1,9},{2,10},{3,11},{4,12},{5,13},{6,14},{7,15},{8,0},{9,1},... | collective-permute-start | bytes 30728 | tf_op jit(solution)/shard_map/ppermute | solution.py:32
  111.3 6.8 %collective-permute-start.20 = (f32[2560]{0:T(1024)S(1)}, f32[2560]{0:T(1024)S(1)}, u32[]{:S(2)}, u32[]{:S(2)}) collective-permute-start(f32[2560]{0:T(1024)S(1)} %add_add_fusion.2), channel_id=1, source_target_pairs={{0,3},{1,2},{2,1},{3,0},{4,7},{5,6},{6,5},{7,4},{8,11},{9,10},{10,... | collective-permute-start | bytes 30728 | tf_op jit(solution)/shard_map/ppermute | solution.py:32
  113.2 4.9 %collective-permute-start.19 = (f32[2560]{0:T(1024)S(1)}, f32[2560]{0:T(1024)S(1)}, u32[]{:S(2)}, u32[]{:S(2)}) collective-permute-start(f32[2560]{0:T(1024)S(1)} %add_add_fusion.2), channel_id=1, source_target_pairs={{0,2},{1,3},{2,0},{3,1},{4,6},{5,7},{6,4},{7,5},{8,10},{9,11},{10,... | collective-permute-start | bytes 30728 | tf_op jit(solution)/shard_map/ppermute | solution.py:32
  114.0 4.1 %collective-permute-start.18 = (f32[2560]{0:T(1024)S(1)}, f32[2560]{0:T(1024)S(1)}, u32[]{:S(2)}, u32[]{:S(2)}) collective-permute-start(f32[2560]{0:T(1024)S(1)} %add_add_fusion.2), channel_id=1, source_target_pairs={{0,1},{1,0},{2,3},{3,2},{4,5},{5,4},{6,7},{7,6},{8,9},{9,8},{10,11... | collective-permute-start | bytes 30728 | tf_op jit(solution)/shard_map/ppermute | solution.py:32
  115.2 23.6 %collective-permute-start.17 = (s16[576,256]{1,0:T(8,128)(2,1)S(1)}, s16[576,256]{1,0:T(8,128)(2,1)S(1)}, u32[]{:S(2)}, u32[]{:S(2)}) collective-permute-start(s16[576,256]{1,0:T(8,128)(2,1)S(1)} %hop.7), channel_id=1, source_target_pairs={{1,0},{2,1},{3,2},{4,3},{5,4},{6,5},{7,6},{8,7},{9,8},{10,9},{11,1... | collective-permute-start | bytes 884744 | tf_op jit(solution)/shard_map/ppermute | solution.py:26
  116.8 22.9 %collective-permute-start.14 = (s16[576,256]{1,0:T(8,128)(2,1)S(1)}, s16[576,256]{1,0:T(8,128)(2,1)S(1)}, u32[]{:S(2)}, u32[]{:S(2)}) collective-permute-start(s16[576,256]{1,0:T(8,128)(2,1)S(1)} %hop.5), channel_id=1, source_target_pairs={{1,0},{2,1},{3,2},{4,3},{5,4},{6,5},{7,6},{8,7},{9,8},{10,9},{11,1... | collective-permute-start | bytes 884744 | tf_op jit(solution)/shard_map/ppermute | solution.py:26
  118.1 15.0 %collective-permute-start.23 = (f32[2560]{0:T(1024)S(1)}, f32[2560]{0:T(1024)S(1)}, u32[]{:S(2)}, u32[]{:S(2)}) collective-permute-start(f32[2560]{0:T(1024)S(1)} %add_add_fusion.1), channel_id=1, source_target_pairs={{0,36},{1,37},{2,38},{3,39},{4,32},{5,33},{6,34},{7,35},{8,44},{9,... | collective-permute-start | bytes 30728 | tf_op jit(solution)/shard_map/ppermute | solution.py:32
  131.7 1.4 collective-permute-start.22
  131.7 6.5 %collective-permute-start.21 = (f32[2560]{0:T(1024)S(1)}, f32[2560]{0:T(1024)S(1)}, u32[]{:S(2)}, u32[]{:S(2)}) collective-permute-start(f32[2560]{0:T(1024)S(1)} %add_add_fusion.1), channel_id=1, source_target_pairs={{0,4},{1,5},{2,6},{3,7},{4,0},{5,1},{6,2},{7,3},{8,12},{9,13},{10,... | collective-permute-start | bytes 30728 | tf_op jit(solution)/shard_map/ppermute | solution.py:32
  (14 other events, 271.8 us)

commit v4 on v3

--- a/solution.py
+++ b/solution.py
@@ -12,6 +12,7 @@
 HD = 128
 BLOCK = 128
 REACH = 4
+Z_CHIPS = 8
 EXPONENT = 1.4426950408889634 / math.sqrt(HD)
 SCALE_STEPS = 64.0
 SCALE_ROWS = 16
@@ -26,13 +27,15 @@
     return lax.ppermute(value, "ctx", pairs)
 
 
-def exchange(value, axis, first, second):
-    count = math.prod(lax.axis_size(a) for a in axis)
-    one, two, three = (
-        lax.ppermute(value, axis, [(i, i ^ bits) for i in range(count)])
-        for bits in (first, second, first | second)
-    )
-    return (value + one) + (two + three)
+def gathered_sum(value, axis, size, groups=None):
+    copies = jnp.broadcast_to(value[None], (size, *value.shape))
+    parts = lax.all_to_all(copies, axis, 0, 0, tiled=True, axis_index_groups=groups)
+    return jnp.sum(parts, axis=0)
+
+
+def pair_sum(value, step):
+    pairs = [(i, i ^ step) for i in range(lax.axis_size("ctx"))]
+    return value + lax.ppermute(value, "ctx", pairs)
 
 
 def encode(value):
@@ -270,6 +273,7 @@
         grid=(s.kv_count,),
         in_specs=[s.wide, s.line, s.thin],
         out_specs=[s.heads, s.stat, s.stat],
+        compiler_params=pltpu.CompilerParams(vmem_limit_bytes=8 * 2**20),
         cost_estimate=s.cost(1, 1, 1),
         name="scores_own" if own else "scores",
     )(queries, gain, keys)
@@ -290,6 +294,7 @@
                 pltpu.VMEM((s.group * s.rows, HD), jnp.bfloat16),
             ],
         ),
+        compiler_params=pltpu.CompilerParams(vmem_limit_bytes=16 * 2**20),
         cost_estimate=s.cost(2, 1, 1),
         name="far_scores",
     )(lo, queries, out_grad, gain, keys, *stats)
@@ -308,6 +313,7 @@
             pltpu.VMEM((near * s.rows, s.group * s.rows), jnp.bfloat16),
             pltpu.VMEM((s.group * s.rows, HD), jnp.bfloat16),
         ],
+        compiler_params=pltpu.CompilerParams(vmem_limit_bytes=15 * 2**20),
         cost_estimate=s.cost(1, near, 0),
         name="near_values",
     )(out_grad, weights, *heads)
@@ -337,6 +343,7 @@
             pltpu.VMEM((s.group * s.rows, HD), jnp.bfloat16),
         ],
         input_output_aliases={n_in + i: i for i in range(len(before))},
+        compiler_params=pltpu.CompilerParams(vmem_limit_bytes=20 * 2**20),
         cost_estimate=s.cost(4, REACH, 0, count),
     )(queries, out_grad, gain, weights, *heads, *keys, *values, *before)
 
@@ -348,6 +355,7 @@
     gain = query_gain[None]
     together = lax.optimization_barrier
     lo = doc_start[0] * BLOCK - (device - (REACH - 1)) * rows
+    lo, gain = together((lo, gain))
     own_keys, own_values = global_keys[0], global_values[0]
     near = [chunk_scores(q, gain, own_keys, True)]
     keys, values = [own_keys], [own_values]
@@ -356,7 +364,6 @@
         if i < REACH - 1:
             near.insert(0, chunk_scores(q, gain, keys[0], False))
             values.insert(0, shifted(values[0], 1))
-    keys[0], values[0] = together((keys[0], values[0]))
     values.insert(0, shifted(values[0], 1))
     half = own_keys.shape[1] // HD // 2
 
@@ -372,23 +379,25 @@
         half, half, early, q, do, gain, weights, heads, keys, values
     )
     dk_moved = shifted(dk_moved, -1)
-    both = ("dp", "ctx")
-    total = exchange(gain_term[0], both, 64, 128)
+    count = lax.axis_size("ctx")
+    columns = [[i + z for i in range(0, count, Z_CHIPS)] for z in range(Z_CHIPS)]
+    total = gathered_sum(gain_term, "dp", lax.axis_size("dp"))
     value_grad = hop(moved, dv[2], True)
     dk_moved, total = together((dk_moved, total))
     dk_moved = shifted(hop(dk_moved, dk[0], False), -1)
-    total = exchange(total, both, 8, 16)
+    total = gathered_sum(total, "ctx", count // Z_CHIPS, columns)
     dk_moved, total = together((dk_moved, total))
     dk_moved = shifted(hop(dk_moved, dk[1], False), -1)
-    total = exchange(total, both, 1, 2)
-    gain_grad = exchange(total, both, 4, 32)
+    total = pair_sum(total, 1)
+    total = pair_sum(total, 2)
+    gain_grad = pair_sum(total, 4)
     key_grad = hop(dk_moved, dk[2], True)
     return (
         attn_out[None],
         query_grad[None],
         key_grad[None],
         value_grad[None],
-        gain_grad,
+        gain_grad[0],
     )
 
 

time: 141 us -> 146 us (1.035)
  the two profiles are of different devices: /device:TPU:1 before, /device:TPU:22 now
where the time goes in v4:
time: 146 us; the launch traced here: 145 us
  starting transfers between devices  48.5 us (33%)
  Pallas kernels  35.6 us (24%)
  waiting for transfers between devices  35.5 us (24%)
  local copies, waits for them, and re-layouts  14.7 us (10%)
  blocking collectives  7.73 us (5%)
  other arithmetic  1.48 us (1%)
    ppermute x12, starting transfers between devices, shifted(): return lax.ppermute(value, 'ctx', pairs)  38.5 us
    ppermute x12, waiting for transfers between devices, shifted(): return lax.ppermute(value, 'ctx', pairs)  19.7 us
    ppermute x3, waiting for transfers between devices, pair_sum(): return value + lax.ppermute(value, 'ctx', pairs)  15.8 us
    pallas_call x2, Pallas kernels, attention_grads(): pl.pallas_call(functools.partial(grads_kernel, s.group, s.rows, len(befor...  14.2 us
    unnamed x48, local copies, waits for them, and re-layouts  13.3 us
    all_to_all x1, blocking collectives, gathered_sum(): lax.all_to_all(copies, axis, 0, 0, tiled=True, axis_index_groups=groups)  7.73 us
    pallas_call x3, Pallas kernels, chunk_scores(): pl.pallas_call(functools.partial(scores_kernel, s.group, own), out_shape=...  6.68 us
    pallas_call x6, Pallas kernels, hop(): pl.pallas_call(functools.partial(hop_kernel, kv_channels // HD, last), ou...  5.76 us
  transfers between devices with their start and end apart: 16, of which 7 were waited for; matrix products, arithmetic and copies ran while one was open for 2% of the time, Pallas kernels for 24%

profile of v4, /device:TPU:22, one launch (start us, length us, event | category | flops | bytes accessed | tf_op | source)
XLA Modules:
  0.0 144.6 jit_solution(3153125115781898958)
XLA Ops:
  0.6 3.8 %collective-permute-start = (bf16[256,512]{1,0:T(8,128)(2,1)}, bf16[256,512]{1,0:T(8,128)(2,1)S(1)}, u32[]{:S(2)}, u32[]{:S(2)}) collective-permute-start(bf16[256,512]{1,0:T(8,128)(2,1)} %bitcast.20), channel_id=1, source_target_pairs={{0,1},{1,2},{2,3},{3,4},{4,5},{5,6},{6,7},{7,8},{8,9},{9,10},{10,1... | collective-permute-start | bytes 786440 | tf_op jit(solution)/shard_map/ppermute | solution.py:27
  4.5 3.8 %collective-permute-start.3 = (bf16[256,512]{1,0:T(8,128)(2,1)}, bf16[256,512]{1,0:T(8,128)(2,1)S(1)}, u32[]{:S(2)}, u32[]{:S(2)}) collective-permute-start(bf16[256,512]{1,0:T(8,128)(2,1)} %bitcast.24), channel_id=1, source_target_pairs={{0,1},{1,2},{2,3},{3,4},{4,5},{5,6},{6,7},{7,8},{8,9},{9,10},{10,1... | collective-permute-start | bytes 786440 | tf_op jit(solution)/shard_map/ppermute | solution.py:27
  8.3 7.7 %collective-permute-done.k_ref.refs_6_ = bf16[256,512]{1,0:T(8,128)(2,1)S(1)} collective-permute-done((bf16[256,512]{1,0:T(8,128)(2,1)}, bf16[256,512]{1,0:T(8,128)(2,1)S(1)}, u32[]{:S(2)}, u32[]{:S(2)}) %collective-permute-start) | collective-permute-done | bytes 262176 | tf_op jit(solution)/shard_map/ppermute | solution.py:27
  17.9 2.9 %collective-permute-done.3.refs_10_ = bf16[256,512]{1,0:T(8,128)(2,1)S(1)} collective-permute-done((bf16[256,512]{1,0:T(8,128)(2,1)}, bf16[256,512]{1,0:T(8,128)(2,1)S(1)}, u32[]{:S(2)}, u32[]{:S(2)}) %collective-permute-start.3) | collective-permute-done | bytes 262176 | tf_op jit(solution)/shard_map/ppermute | solution.py:27
  22.7 3.9 %collective-permute-done.1.k_ref.refs_5_ = bf16[256,512]{1,0:T(8,128)(2,1)S(1)} collective-permute-done((bf16[256,512]{1,0:T(8,128)(2,1)S(1)}, bf16[256,512]{1,0:T(8,128)(2,1)S(1)}, u32[]{:S(2)}, u32[]{:S(2)}) %collective-permute-start.1) | collective-permute-done | bytes 262176 | tf_op jit(solution)/shard_map/ppermute | solution.py:27
  28.6 5.2 %collective-permute-done.4.refs_9_ = bf16[256,512]{1,0:T(8,128)(2,1)S(1)} collective-permute-done((bf16[256,512]{1,0:T(8,128)(2,1)S(1)}, bf16[256,512]{1,0:T(8,128)(2,1)S(1)}, u32[]{:S(2)}, u32[]{:S(2)}) %collective-permute-start.4) | collective-permute-done | bytes 262176 | tf_op jit(solution)/shard_map/ppermute | solution.py:27
  39.3 2.3 %scores_own.1 = (f32[20,256,256]{2,1,0:T(8,128)S(1)}, f32[4,10,256]{2,1,0:T(8,128)S(1)}, f32[4,10,256]{2,1,0:T(8,128)S(1)}) custom-call(bf16[256,2560]{1,0:T(8,128)(2,1)S(1)} %bitcast.14, f32[1,2560]{1,0:T(1,128)S(1)} %broadcast_in_dim.31.gain_ref, bf16[256,512]{1,0:T(8,128)(2,1)S(1)} %bitcast.21), custom_call_target="tpu_custom_call" | custom-call | flops 335544320 | bytes 5242880 | tf_op jit(solution)/shard_map/scores_own/pallas_call | solution.py:270
  41.6 2.2 %scores.3 = (f32[20,256,256]{2,1,0:T(8,128)S(1)}, f32[4,10,256]{2,1,0:T(8,128)S(1)}, f32[4,10,256]{2,1,0:T(8,128)S(1)}) custom-call(bf16[256,2560]{1,0:T(8,128)(2,1)S(1)} %bitcast.15, f32[1,2560]{1,0:T(1,128)S(1)} %broadcast_in_dim.31.gain_ref, bf16[256,512]{1,0:T(8,128)(2,1)S(1)} %collective-permute-done.k_ref.refs_6_), custom_call_target="tpu_custom_call" | custom-call | flops 335544320 | bytes 5242880 | tf_op jit(solution)/shard_map/scores/pallas_call | solution.py:270
  46.2 5.6 %far_scores.1 = (f32[20,256,256]{2,1,0:T(8,128)S(1)}, f32[4,40,256]{2,1,0:T(8,128)S(1)}, s16[576,256]{1,0:T(8,128)(2,1)}) custom-call(s32[2]{0:T(128)S(1)} %subtract_bitcast_fusion.lo, bf16[256,2560]{1,0:T(8,128)(2,1)S(1)} %bitcast.17, bf16[256,2560]{1,0:T(8,128)(2,1)S(1)} %bitcast.10, f32[1,2560]{1,0:T(1,128)S(1)} %broadcast_in_dim.31.gain_ref, ...), custom_call_target="tpu_custom_call" | custom-call | flops 671088640 | bytes 5242880 | tf_op jit(solution)/shard_map/far_scores/pallas_call | solution.py:284
  51.8 6.0 %collective-permute-start.9 = (s16[576,256]{1,0:T(8,128)(2,1)}, s16[576,256]{1,0:T(8,128)(2,1)}, u32[]{:S(2)}, u32[]{:S(2)}) collective-permute-start(s16[576,256]{1,0:T(8,128)(2,1)} %get-tuple-element.70), channel_id=1, source_target_pairs={{1,0},{2,1},{3,2},{4,3},{5,4},{6,5},{7,6},{8,7},{9,8},{10,9},{11,1... | collective-permute-start | bytes 884744 | tf_op jit(solution)/shard_map/ppermute | solution.py:27
  57.9 7.0 %shard_map.101 = (bf16[256,2560]{1,0:T(8,128)(2,1)}, bf16[256,2560]{1,0:T(8,128)(2,1)}, f32[1,2560]{1,0:T(1,128)S(1)}, s16[576,256]{1,0:T(8,128)(2,1)}, f32[512,...) custom-call(bf16[256,2560]{1,0:T(8,128)(2,1)S(1)} %bitcast.18, bf16[256,2560]{1,0:T(8,128)(2,1)S(1)} %bitcast.11, ...), custom_call_target="tpu_custom_call" | custom-call | flops 2684354560 | bytes 10485760 | tf_op jit(solution)/shard_map/pallas_call | solution.py:326
  64.9 7.1 %shard_map.102 = (bf16[256,2560]{1,0:T(8,128)(2,1)}, bf16[256,2560]{1,0:T(8,128)(2,1)}, f32[1,2560]{1,0:T(1,128)S(1)}, s16[576,256]{1,0:T(8,128)(2,1)}, f32[512,...) custom-call(bf16[256,2560]{1,0:T(8,128)(2,1)S(1)} %bitcast.19, ...), custom_call_target="tpu_custom_call", output_to_operand_aliasing={{0}: (16, {}), {1}: (17, {}), {2}: (18, {}), {3}: (19, {}),... | custom-call | flops 2684354560 | bytes 10485760 | tf_op jit(solution)/shard_map/pallas_call | solution.py:326
  74.7 4.8 %all-to-all-start = ((f32[8,1,2560]{2,1,0:T(1,128)}), f32[8,1,2560]{2,1,0:T(1,128)S(1)}, u32[]{:S(2)}, u32[]{:S(2)}) async-start(f32[8,1,2560]{2,1,0:T(1,128)} %broadcast_in_dim.35), calls=%async_computation | async-start | bytes 163840 | tf_op jit(solution)/shard_map/all_to_all | solution.py:32
  79.5 2.5 %copy-done.1 = f32[20,256,256]{2,1,0:T(8,128)S(1)} copy-done((f32[20,256,256]{2,1,0:T(8,128)S(1)}, f32[20,256,256]{2,1,0:T(8,128)}, u32[]{:S(2)}) %copy-start.1) | copy-done | bytes 5242904
  82.0 2.5 %copy-done.3 = f32[20,256,256]{2,1,0:T(8,128)S(1)} copy-done((f32[20,256,256]{2,1,0:T(8,128)S(1)}, f32[20,256,256]{2,1,0:T(8,128)}, u32[]{:S(2)}) %copy-start.3) | copy-done | bytes 5242904
  84.5 2.5 %copy-done.5 = f32[20,256,256]{2,1,0:T(8,128)S(1)} copy-done((f32[20,256,256]{2,1,0:T(8,128)S(1)}, f32[20,256,256]{2,1,0:T(8,128)}, u32[]{:S(2)}) %copy-start.5) | copy-done | bytes 5242904
  87.0 3.3 %near_values.1 = (f32[512,256]{1,0:T(8,128)S(1)}, f32[512,256]{1,0:T(8,128)S(1)}, f32[512,256]{1,0:T(8,128)S(1)}) custom-call(bf16[256,2560]{1,0:T(8,128)(2,1)S(1)} %bitcast.13, f32[4,40,256]{2,1,0:T(8,128)S(1)} %get-tuple-element.48.w_ref, f32[20,256,256]{2,1,0:T(8,128)S(1)} %copy-done.5, f32[20,256,256]{2,1,0:T(8,128)S(1)} %copy-done.3, ...), custom_call_target="tpu_custom_call" | custom-call | flops 1006632960 | bytes 15728640 | tf_op jit(solution)/shard_map/near_values/pallas_call | solution.py:306
  98.6 4.1 %collective-permute-start.7 = (s16[576,256]{1,0:T(8,128)(2,1)}, s16[576,256]{1,0:T(8,128)(2,1)S(1)}, u32[]{:S(2)}, u32[]{:S(2)}) collective-permute-start(s16[576,256]{1,0:T(8,128)(2,1)} %hop.4), channel_id=1, source_target_pairs={{1,0},{2,1},{3,2},{4,3},{5,4},{6,5},{7,6},{8,7},{9,8},{10,9},{11,1... | collective-permute-start | bytes 884744 | tf_op jit(solution)/shard_map/ppermute | solution.py:27
  102.8 7.7 %all_to_all.10 = f32[4,1,2560]{2,1,0:T(1,128)S(1)} all-to-all(f32[4,1,2560]{2,1,0:T(1,128)S(1)} %broadcast_in_dim.37), channel_id=1, replica_groups={{0,8,16,24},{1,9,17,25},{2,10,18,26},{3,11,19,27},{4,12,20,28},{5,13,21..., dimensions={0} | all-to-all | bytes 81920 | tf_op jit(solution)/shard_map/all_to_all | solution.py:32
  111.7 7.3 %collective-permute-start.11 = (s16[576,256]{1,0:T(8,128)(2,1)S(1)}, s16[576,256]{1,0:T(8,128)(2,1)S(1)}, u32[]{:S(2)}, u32[]{:S(2)}) collective-permute-start(s16[576,256]{1,0:T(8,128)(2,1)S(1)} %hop.7), channel_id=1, source_target_pairs={{1,0},{2,1},{3,2},{4,3},{5,4},{6,5},{7,6},{8,7},{9,8},{10,9},{11,1... | collective-permute-start | bytes 884744 | tf_op jit(solution)/shard_map/ppermute | solution.py:27
  123.2 6.6 %collective-permute-done.12 = f32[1,2560]{1,0:T(1,128)S(1)} collective-permute-done((f32[1,2560]{1,0:T(1,128)S(1)}, f32[1,2560]{1,0:T(1,128)S(1)}, u32[]{:S(2)}, u32[]{:S(2)}) %collective-permute-start.12) | collective-permute-done | bytes 10272 | tf_op jit(solution)/shard_map/ppermute | solution.py:38
  130.0 4.6 %collective-permute-done.13 = f32[1,2560]{1,0:T(1,128)S(1)} collective-permute-done((f32[1,2560]{1,0:T(1,128)S(1)}, f32[1,2560]{1,0:T(1,128)S(1)}, u32[]{:S(2)}, u32[]{:S(2)}) %collective-permute-start.13) | collective-permute-done | bytes 10272 | tf_op jit(solution)/shard_map/ppermute | solution.py:38
  134.6 3.1 %collective-permute-start.14 = (f32[1,2560]{1,0:T(1,128)S(1)}, f32[1,2560]{1,0:T(1,128)S(1)}, u32[]{:S(2)}, u32[]{:S(2)}) collective-permute-start(f32[1,2560]{1,0:T(1,128)S(1)} %add.11), channel_id=1, source_target_pairs={{0,4},{1,5},{2,6},{3,7},{4,0},{5,1},{6,2},{7,3},{8,12},{9,13},{10,... | collective-permute-start | bytes 30728 | tf_op jit(solution)/shard_map/ppermute | solution.py:38
  137.6 4.6 %collective-permute-done.14 = f32[1,2560]{1,0:T(1,128)S(1)} collective-permute-done((f32[1,2560]{1,0:T(1,128)S(1)}, f32[1,2560]{1,0:T(1,128)S(1)}, u32[]{:S(2)}, u32[]{:S(2)}) %collective-permute-start.14) | collective-permute-done | bytes 10272 | tf_op jit(solution)/shard_map/ppermute | solution.py:38
  (83 shorter events, 32.3 us)
Async XLA Ops:
  0.6 15.4 %collective-permute-start = (bf16[256,512]{1,0:T(8,128)(2,1)}, bf16[256,512]{1,0:T(8,128)(2,1)S(1)}, u32[]{:S(2)}, u32[]{:S(2)}) collective-permute-start(bf16[256,512]{1,0:T(8,128)(2,1)} %bitcast.20), channel_id=1, source_target_pairs={{0,1},{1,2},{2,3},{3,4},{4,5},{5,6},{6,7},{7,8},{8,9},{9,10},{10,1... | collective-permute-start | bytes 786440 | tf_op jit(solution)/shard_map/ppermute | solution.py:27
  4.5 16.3 %collective-permute-start.3 = (bf16[256,512]{1,0:T(8,128)(2,1)}, bf16[256,512]{1,0:T(8,128)(2,1)S(1)}, u32[]{:S(2)}, u32[]{:S(2)}) collective-permute-start(bf16[256,512]{1,0:T(8,128)(2,1)} %bitcast.24), channel_id=1, source_target_pairs={{0,1},{1,2},{2,3},{3,4},{4,5},{5,6},{6,7},{7,8},{8,9},{9,10},{10,1... | collective-permute-start | bytes 786440 | tf_op jit(solution)/shard_map/ppermute | solution.py:27
  16.0 10.6 %collective-permute-start.1 = (bf16[256,512]{1,0:T(8,128)(2,1)S(1)}, bf16[256,512]{1,0:T(8,128)(2,1)S(1)}, u32[]{:S(2)}, u32[]{:S(2)}) collective-permute-start(bf16[256,512]{1,0:T(8,128)(2,1)S(1)} %collective-permute-done.k_ref.refs_6_), channel_id=1, source_target_pairs={{0,1},{1,2},{2,3},{3,4},{4,5},{5,6},{6,7},{7,8},{8,9},{9,10},{10,1... | collective-permute-start | bytes 786440 | tf_op jit(solution)/shard_map/ppermute | solution.py:27
  20.8 20.8 %copy-start.12 = (bf16[256,512]{1,0:T(8,128)(2,1)}, bf16[256,512]{1,0:T(8,128)(2,1)S(1)}, u32[]{:S(2)}) copy-start(bf16[256,512]{1,0:T(8,128)(2,1)S(1)} %collective-permute-done.3.refs_10_) | copy-start | bytes 786436
  20.8 12.9 %collective-permute-start.4 = (bf16[256,512]{1,0:T(8,128)(2,1)S(1)}, bf16[256,512]{1,0:T(8,128)(2,1)S(1)}, u32[]{:S(2)}, u32[]{:S(2)}) collective-permute-start(bf16[256,512]{1,0:T(8,128)(2,1)S(1)} %collective-permute-done.3.refs_10_), channel_id=1, source_target_pairs={{0,1},{1,2},{2,3},{3,4},{4,5},{5,6},{6,7},{7,8},{8,9},{9,10},{10,1... | collective-permute-start | bytes 786440 | tf_op jit(solution)/shard_map/ppermute | solution.py:27
  26.6 17.2 %copy-start.14 = (bf16[256,512]{1,0:T(8,128)(2,1)}, bf16[256,512]{1,0:T(8,128)(2,1)S(1)}, u32[]{:S(2)}) copy-start(bf16[256,512]{1,0:T(8,128)(2,1)S(1)} %collective-permute-done.1.k_ref.refs_5_) | copy-start | bytes 786436
  26.6 19.4 %collective-permute-start.2 = (bf16[256,512]{1,0:T(8,128)(2,1)S(1)}, bf16[256,512]{1,0:T(8,128)(2,1)S(1)}, u32[]{:S(2)}, u32[]{:S(2)}) collective-permute-start(bf16[256,512]{1,0:T(8,128)(2,1)S(1)} %collective-permute-done.1.k_ref.refs_5_), channel_id=1, source_target_pairs={{0,1},{1,2},{2,3},{3,4},{4,5},{5,6},{6,7},{7,8},{8,9},{9,10},{10,1... | collective-permute-start | bytes 786440 | tf_op jit(solution)/shard_map/ppermute | solution.py:27
  33.7 24.1 %collective-permute-start.5 = (bf16[256,512]{1,0:T(8,128)(2,1)S(1)}, bf16[256,512]{1,0:T(8,128)(2,1)S(1)}, u32[]{:S(2)}, u32[]{:S(2)}) collective-permute-start(bf16[256,512]{1,0:T(8,128)(2,1)S(1)} %collective-permute-done.4.refs_9_), channel_id=1, source_target_pairs={{0,1},{1,2},{2,3},{3,4},{4,5},{5,6},{6,7},{7,8},{8,9},{9,10},{10,1... | collective-permute-start | bytes 786440 | tf_op jit(solution)/shard_map/ppermute | solution.py:27
  41.6 23.3 %copy-start = (f32[20,256,256]{2,1,0:T(8,128)}, f32[20,256,256]{2,1,0:T(8,128)S(1)}, u32[]{:S(2)}) copy-start(f32[20,256,256]{2,1,0:T(8,128)S(1)} %get-tuple-element.52.refs_3_.refs_2_) | copy-start | bytes 15728644
  43.8 21.1 %copy-start.2 = (f32[20,256,256]{2,1,0:T(8,128)}, f32[20,256,256]{2,1,0:T(8,128)S(1)}, u32[]{:S(2)}) copy-start(f32[20,256,256]{2,1,0:T(8,128)S(1)} %get-tuple-element.51.refs_2_.refs_1_) | copy-start | bytes 15728644
  46.1 18.9 %copy-start.4 = (f32[20,256,256]{2,1,0:T(8,128)}, f32[20,256,256]{2,1,0:T(8,128)S(1)}, u32[]{:S(2)}) copy-start(f32[20,256,256]{2,1,0:T(8,128)S(1)} %get-tuple-element.50.refs_1_.refs_0_) | copy-start | bytes 15728644
  46.1 11.7 %copy-start.10 = (bf16[1,256,512]{2,1,0:T(8,128)(2,1)S(1)}, bf16[1,256,512]{2,1,0:T(8,128)(2,1)}, u32[]{:S(2)}) copy-start(bf16[1,256,512]{2,1,0:T(8,128)(2,1)} %param.7) | copy-start | bytes 786436
  51.8 41.0 %collective-permute-start.9 = (s16[576,256]{1,0:T(8,128)(2,1)}, s16[576,256]{1,0:T(8,128)(2,1)}, u32[]{:S(2)}, u32[]{:S(2)}) collective-permute-start(s16[576,256]{1,0:T(8,128)(2,1)} %get-tuple-element.70), channel_id=1, source_target_pairs={{1,0},{2,1},{3,2},{4,3},{5,4},{6,5},{7,6},{8,7},{9,8},{10,9},{11,1... | collective-permute-start | bytes 884744 | tf_op jit(solution)/shard_map/ppermute | solution.py:27
  72.1 25.6 %collective-permute-start.6 = (s16[576,256]{1,0:T(8,128)(2,1)}, s16[576,256]{1,0:T(8,128)(2,1)S(1)}, u32[]{:S(2)}, u32[]{:S(2)}) collective-permute-start(s16[576,256]{1,0:T(8,128)(2,1)} %get-tuple-element.62), channel_id=1, source_target_pairs={{1,0},{2,1},{3,2},{4,3},{5,4},{6,5},{7,6},{8,7},{9,8},{10,9},{11,1... | collective-permute-start | bytes 884744 | tf_op jit(solution)/shard_map/ppermute | solution.py:27
  74.7 18.0 %all-to-all-start = ((f32[8,1,2560]{2,1,0:T(1,128)}), f32[8,1,2560]{2,1,0:T(1,128)S(1)}, u32[]{:S(2)}, u32[]{:S(2)}) async-start(f32[8,1,2560]{2,1,0:T(1,128)} %broadcast_in_dim.35), calls=%async_computation | async-start | bytes 163840 | tf_op jit(solution)/shard_map/all_to_all | solution.py:32
  92.7 17.9 %copy-start.21 = (f32[512,256]{1,0:T(8,128)S(1)}, f32[512,256]{1,0:T(8,128)}, u32[]{:S(2)}) copy-start(f32[512,256]{1,0:T(8,128)} %copy-done.20) | copy-start | bytes 1572868
  95.7 14.8 %collective-permute-start.10 = (s16[576,256]{1,0:T(8,128)(2,1)}, s16[576,256]{1,0:T(8,128)(2,1)}, u32[]{:S(2)}, u32[]{:S(2)}) collective-permute-start(s16[576,256]{1,0:T(8,128)(2,1)} %hop.6), channel_id=1, source_target_pairs={{1,0},{2,1},{3,2},{4,3},{5,4},{6,5},{7,6},{8,7},{9,8},{10,9},{11,1... | collective-permute-start | bytes 884744 | tf_op jit(solution)/shard_map/ppermute | solution.py:27
  98.6 44.3 %copy-start.19 = (f32[512,256]{1,0:T(8,128)S(1)}, f32[512,256]{1,0:T(8,128)}, u32[]{:S(2)}) copy-start(f32[512,256]{1,0:T(8,128)} %copy-done.18) | copy-start | bytes 1572868
  98.6 20.5 %collective-permute-start.7 = (s16[576,256]{1,0:T(8,128)(2,1)}, s16[576,256]{1,0:T(8,128)(2,1)S(1)}, u32[]{:S(2)}, u32[]{:S(2)}) collective-permute-start(s16[576,256]{1,0:T(8,128)(2,1)} %hop.4), channel_id=1, source_target_pairs={{1,0},{2,1},{3,2},{4,3},{5,4},{6,5},{7,6},{8,7},{9,8},{10,9},{11,1... | collective-permute-start | bytes 884744 | tf_op jit(solution)/shard_map/ppermute | solution.py:27
  111.7 31.2 %collective-permute-start.11 = (s16[576,256]{1,0:T(8,128)(2,1)S(1)}, s16[576,256]{1,0:T(8,128)(2,1)S(1)}, u32[]{:S(2)}, u32[]{:S(2)}) collective-permute-start(s16[576,256]{1,0:T(8,128)(2,1)S(1)} %hop.7), channel_id=1, source_target_pairs={{1,0},{2,1},{3,2},{4,3},{5,4},{6,5},{7,6},{8,7},{9,8},{10,9},{11,1... | collective-permute-start | bytes 884744 | tf_op jit(solution)/shard_map/ppermute | solution.py:27
  119.2 24.5 %collective-permute-start.8 = (s16[576,256]{1,0:T(8,128)(2,1)S(1)}, s16[576,256]{1,0:T(8,128)(2,1)S(1)}, u32[]{:S(2)}, u32[]{:S(2)}) collective-permute-start(s16[576,256]{1,0:T(8,128)(2,1)S(1)} %hop.5), channel_id=1, source_target_pairs={{1,0},{2,1},{3,2},{4,3},{5,4},{6,5},{7,6},{8,7},{9,8},{10,9},{11,1... | collective-permute-start | bytes 884744 | tf_op jit(solution)/shard_map/ppermute | solution.py:27
  121.1 8.7 %collective-permute-start.12 = (f32[1,2560]{1,0:T(1,128)S(1)}, f32[1,2560]{1,0:T(1,128)S(1)}, u32[]{:S(2)}, u32[]{:S(2)}) collective-permute-start(f32[1,2560]{1,0:T(1,128)S(1)} %reduce_sum.25), channel_id=1, source_target_pairs={{0,1},{1,0},{2,3},{3,2},{4,5},{5,4},{6,7},{7,6},{8,9},{9,8},{10,11... | collective-permute-start | bytes 30728 | tf_op jit(solution)/shard_map/ppermute | solution.py:38
  129.9 4.7 %collective-permute-start.13 = (f32[1,2560]{1,0:T(1,128)S(1)}, f32[1,2560]{1,0:T(1,128)S(1)}, u32[]{:S(2)}, u32[]{:S(2)}) collective-permute-start(f32[1,2560]{1,0:T(1,128)S(1)} %add.10), channel_id=1, source_target_pairs={{0,2},{1,3},{2,0},{3,1},{4,6},{5,7},{6,4},{7,5},{8,10},{9,11},{10,... | collective-permute-start | bytes 30728 | tf_op jit(solution)/shard_map/ppermute | solution.py:38
  134.6 7.7 %collective-permute-start.14 = (f32[1,2560]{1,0:T(1,128)S(1)}, f32[1,2560]{1,0:T(1,128)S(1)}, u32[]{:S(2)}, u32[]{:S(2)}) collective-permute-start(f32[1,2560]{1,0:T(1,128)S(1)} %add.11), channel_id=1, source_target_pairs={{0,4},{1,5},{2,6},{3,7},{4,0},{5,1},{6,2},{7,3},{8,12},{9,13},{10,... | collective-permute-start | bytes 30728 | tf_op jit(solution)/shard_map/ppermute | solution.py:38
  (16 other events, 76.9 us)

commit v5 on v4

--- a/solution.py
+++ b/solution.py
@@ -129,6 +129,12 @@
     dv_ref[:HD, :], dv_ref[HD:, :] = encode(dot(p_low[...], g_all[...]).T)
 
 
+def store_parts(refs, total, rows):
+    middle, nearest, own = (total[j * rows : (j + 1) * rows, :].T for j in range(REACH - 1))
+    refs[0][...], refs[2][...] = middle, own
+    refs[1][:HD, :], refs[1][HD:, :] = encode(nearest)
+
+
 def values_kernel(group, g_ref, w_ref, *refs):
     e_refs, dv_refs = refs[: REACH - 1], refs[REACH - 1 : 2 * (REACH - 1)]
     p_low, g_all = refs[2 * (REACH - 1) :]
@@ -145,8 +151,7 @@
                 there = slice(j * rows + b * BLOCK, j * rows + (b + 1) * BLOCK)
                 p_low[there, g * rows : (g + 1) * rows] = probs.astype(jnp.bfloat16)
     dv = dot(p_low[...], g_all[...])
-    for j in range(REACH - 1):
-        dv_refs[j][...] = dv[j * rows : (j + 1) * rows, :].T
+    store_parts(dv_refs, dv, rows)
 
 
 def grads_kernel(group, rows, skip, q_ref, g_ref, gain_ref, w_ref, *refs):
@@ -189,34 +194,34 @@
         gain_out[:, cols] = jnp.sum(dscaled * q32, axis=0, keepdims=True)
     dk = dot(ds_all[...], q_all[...]) * factor
     dk_refs[0][:HD, :], dk_refs[0][HD:, :] = encode(dk[:rows, :].T)
-    for j in range(1, REACH):
-        dk_refs[j][...] = dk[j * rows : (j + 1) * rows, :].T
-
-
-def hop_kernel(kv_count, last, message, part, out):
+    store_parts(dk_refs[1:], dk[rows:, :], rows)
+
+
+def hop_kernel(kv_count, last, *refs):
+    *messages, part, out = refs
     for c in range(kv_count):
         at, here = c * CODE_ROWS, slice(c * HD, (c + 1) * HD)
-        total = part[here, :] + decode(
-            message[at : at + HD, :], message[at + HD : at + CODE_ROWS, :]
-        )
+        total = part[here, :]
+        for message in messages:
+            total = total + decode(message[at : at + HD, :], message[at + HD : at + CODE_ROWS, :])
         if last:
             out[:, here] = total.T.astype(jnp.bfloat16)
         else:
             out[at : at + HD, :], out[at + HD : at + CODE_ROWS, :] = encode(total)
 
 
-def hop(message, part, last):
+def hop(messages, part, last):
     kv_channels, rows = part.shape
-    shape = jax.ShapeDtypeStruct((rows, kv_channels), jnp.bfloat16) if last else message
+    shape = jax.ShapeDtypeStruct((rows, kv_channels), jnp.bfloat16) if last else messages[0]
     return pl.pallas_call(
         functools.partial(hop_kernel, kv_channels // HD, last),
         out_shape=jax.ShapeDtypeStruct(shape.shape, shape.dtype),
-        compiler_params=pltpu.CompilerParams(vmem_limit_bytes=16 * 2**20),
+        compiler_params=pltpu.CompilerParams(vmem_limit_bytes=8 * 2**20),
         cost_estimate=pl.CostEstimate(
             flops=10 * part.size, bytes_accessed=8 * part.size, transcendentals=0
         ),
         name="last_hop" if last else "hop",
-    )(message, part)
+    )(*messages, part)
 
 
 class Shapes:
@@ -305,10 +310,10 @@
     near = REACH - 1
     return pl.pallas_call(
         functools.partial(values_kernel, s.group),
-        out_shape=[s.part_array()] * near,
+        out_shape=[s.part_array(), s.code_array(), s.part_array()],
         grid=(s.kv_count,),
         in_specs=[s.wide, s.weight] + [s.heads] * near,
-        out_specs=[s.part] * near,
+        out_specs=[s.part, s.code, s.part],
         scratch_shapes=[
             pltpu.VMEM((near * s.rows, s.group * s.rows), jnp.bfloat16),
             pltpu.VMEM((s.group * s.rows, HD), jnp.bfloat16),
@@ -326,14 +331,14 @@
     return pl.pallas_call(
         functools.partial(grads_kernel, s.group, s.rows, len(before)),
         out_shape=[s.array(jnp.bfloat16, s.rows, s.channels)] * 2
-        + [s.array(jnp.float32, 1, s.channels), s.code_array()]
-        + [s.part_array()] * (REACH - 1),
+        + [s.array(jnp.float32, 1, s.channels)]
+        + [s.code_array(), s.part_array()] * 2,
         grid=(count,),
         in_specs=[s.wide, s.wide, s.line, s.weight]
         + [s.heads] * REACH
         + [s.thin] * (2 * REACH)
         + [pl.BlockSpec(memory_space=pl.ANY)] * len(before),
-        out_specs=[s.wide, s.wide, s.line, s.code] + [s.part] * (REACH - 1),
+        out_specs=[s.wide, s.wide, s.line] + [s.code, s.part] * 2,
         scratch_shapes=[
             pltpu.VMEM((HD, width), jnp.bfloat16),
             pltpu.VMEM((HD, width), jnp.bfloat16),
@@ -370,28 +375,27 @@
     stats = [stat for _, *pair in near for stat in pair]
     far, weights, moved = far_scores(lo, q, do, gain, keys[0], stats)
     heads = [far] + [e for e, *_ in near]
-    moved = shifted(moved, -1)
-    dv = near_values(q, own_keys, do, weights, heads[1:])
-    moved = shifted(hop(moved, dv[0], False), -1)
+    dv_far = shifted(moved, -1)
+    dv_middle, dv_near, dv_own = near_values(q, own_keys, do, weights, heads[1:])
+    dv_near = shifted(dv_near, -1)
     early = attention_grads(0, half, [], q, do, gain, weights, heads, keys, values)
-    moved = shifted(hop(moved, dv[1], False), -1)
-    attn_out, query_grad, gain_term, dk_moved, *dk = attention_grads(
+    dv_middle = shifted(hop([dv_far], dv_middle, False), -2)
+    attn_out, query_grad, gain_term, dk_far, dk_middle, dk_near, dk_own = attention_grads(
         half, half, early, q, do, gain, weights, heads, keys, values
     )
-    dk_moved = shifted(dk_moved, -1)
+    dk_far = shifted(dk_far, -1)
+    dk_near = shifted(dk_near, -1)
     count = lax.axis_size("ctx")
     columns = [[i + z for i in range(0, count, Z_CHIPS)] for z in range(Z_CHIPS)]
     total = gathered_sum(gain_term, "dp", lax.axis_size("dp"))
-    value_grad = hop(moved, dv[2], True)
-    dk_moved, total = together((dk_moved, total))
-    dk_moved = shifted(hop(dk_moved, dk[0], False), -1)
+    dk_far, total = together((dk_far, total))
+    dk_middle = shifted(hop([dk_far], dk_middle, False), -2)
     total = gathered_sum(total, "ctx", count // Z_CHIPS, columns)
-    dk_moved, total = together((dk_moved, total))
-    dk_moved = shifted(hop(dk_moved, dk[1], False), -1)
     total = pair_sum(total, 1)
     total = pair_sum(total, 2)
     gain_grad = pair_sum(total, 4)
-    key_grad = hop(dk_moved, dk[2], True)
+    value_grad = hop([dv_middle, dv_near], dv_own, True)
+    key_grad = hop([dk_middle, dk_near], dk_own, True)
     return (
         attn_out[None],
         query_grad[None],

time: 146 us -> 158 us (1.082)
  the two profiles are of different devices: /device:TPU:22 before, /device:TPU:2 now
where the time goes in v5:
time: 158 us; the launch traced here: 157 us
  waiting for transfers between devices  47.5 us (30%)
  starting transfers between devices  45.4 us (29%)
  Pallas kernels  31.8 us (20%)
  blocking collectives  18.7 us (12%)
  local copies, waits for them, and re-layouts  11.3 us (7%)
    ppermute x12, starting transfers between devices, shifted(): return lax.ppermute(value, 'ctx', pairs)  36.6 us
    ppermute x3, waiting for transfers between devices, pair_sum(): return value + lax.ppermute(value, 'ctx', pairs)  28.1 us
    ppermute x12, waiting for transfers between devices, shifted(): return lax.ppermute(value, 'ctx', pairs)  19.4 us
    all_to_all x2, blocking collectives, gathered_sum(): lax.all_to_all(copies, axis, 0, 0, tiled=True, axis_index_groups=groups)  18.7 us
    pallas_call x2, Pallas kernels, attention_grads(): pl.pallas_call(functools.partial(grads_kernel, s.group, s.rows, len(befor...  14 us
    unnamed x32, local copies, waits for them, and re-layouts  10.5 us
    ppermute x3, starting transfers between devices, pair_sum(): return value + lax.ppermute(value, 'ctx', pairs)  8.81 us
    pallas_call x3, Pallas kernels, chunk_scores(): pl.pallas_call(functools.partial(scores_kernel, s.group, own), out_shape=...  6.66 us
  transfers between devices with their start and end apart: 15, of which 6 were waited for; matrix products, arithmetic and copies ran while one was open for 1% of the time, Pallas kernels for 11%

profile of v5, /device:TPU:2, one launch (start us, length us, event | category | flops | bytes accessed | tf_op | source)
XLA Modules:
  0.0 157.1 jit_solution(14683320387238580307)
XLA Ops:
  0.6 3.8 %collective-permute-start = (bf16[256,512]{1,0:T(8,128)(2,1)}, bf16[256,512]{1,0:T(8,128)(2,1)S(1)}, u32[]{:S(2)}, u32[]{:S(2)}) collective-permute-start(bf16[256,512]{1,0:T(8,128)(2,1)} %bitcast.20), channel_id=1, source_target_pairs={{0,1},{1,2},{2,3},{3,4},{4,5},{5,6},{6,7},{7,8},{8,9},{9,10},{10,1... | collective-permute-start | bytes 786440 | tf_op jit(solution)/shard_map/ppermute | solution.py:27
  4.5 3.8 %collective-permute-start.3 = (bf16[256,512]{1,0:T(8,128)(2,1)}, bf16[256,512]{1,0:T(8,128)(2,1)S(1)}, u32[]{:S(2)}, u32[]{:S(2)}) collective-permute-start(bf16[256,512]{1,0:T(8,128)(2,1)} %bitcast.24), channel_id=1, source_target_pairs={{0,1},{1,2},{2,3},{3,4},{4,5},{5,6},{6,7},{7,8},{8,9},{9,10},{10,1... | collective-permute-start | bytes 786440 | tf_op jit(solution)/shard_map/ppermute | solution.py:27
  8.3 7.4 %collective-permute-done.k_ref.refs_6_ = bf16[256,512]{1,0:T(8,128)(2,1)S(1)} collective-permute-done((bf16[256,512]{1,0:T(8,128)(2,1)}, bf16[256,512]{1,0:T(8,128)(2,1)S(1)}, u32[]{:S(2)}, u32[]{:S(2)}) %collective-permute-start) | collective-permute-done | bytes 262176 | tf_op jit(solution)/shard_map/ppermute | solution.py:27
  17.6 2.9 %collective-permute-done.3.refs_10_ = bf16[256,512]{1,0:T(8,128)(2,1)S(1)} collective-permute-done((bf16[256,512]{1,0:T(8,128)(2,1)}, bf16[256,512]{1,0:T(8,128)(2,1)S(1)}, u32[]{:S(2)}, u32[]{:S(2)}) %collective-permute-start.3) | collective-permute-done | bytes 262176 | tf_op jit(solution)/shard_map/ppermute | solution.py:27
  22.4 3.9 %collective-permute-done.1.k_ref.refs_5_ = bf16[256,512]{1,0:T(8,128)(2,1)S(1)} collective-permute-done((bf16[256,512]{1,0:T(8,128)(2,1)S(1)}, bf16[256,512]{1,0:T(8,128)(2,1)S(1)}, u32[]{:S(2)}, u32[]{:S(2)}) %collective-permute-start.1) | collective-permute-done | bytes 262176 | tf_op jit(solution)/shard_map/ppermute | solution.py:27
  28.3 5.2 %collective-permute-done.4.refs_9_ = bf16[256,512]{1,0:T(8,128)(2,1)S(1)} collective-permute-done((bf16[256,512]{1,0:T(8,128)(2,1)S(1)}, bf16[256,512]{1,0:T(8,128)(2,1)S(1)}, u32[]{:S(2)}, u32[]{:S(2)}) %collective-permute-start.4) | collective-permute-done | bytes 262176 | tf_op jit(solution)/shard_map/ppermute | solution.py:27
  39.0 2.3 %scores_own.1 = (f32[20,256,256]{2,1,0:T(8,128)S(1)}, f32[4,10,256]{2,1,0:T(8,128)S(1)}, f32[4,10,256]{2,1,0:T(8,128)S(1)}) custom-call(bf16[256,2560]{1,0:T(8,128)(2,1)S(1)} %bitcast.14, f32[1,2560]{1,0:T(1,128)S(1)} %broadcast_in_dim.31.gain_ref, bf16[256,512]{1,0:T(8,128)(2,1)S(1)} %bitcast.21), custom_call_target="tpu_custom_call" | custom-call | flops 335544320 | bytes 5242880 | tf_op jit(solution)/shard_map/scores_own/pallas_call | solution.py:275
  41.3 2.2 %scores.3 = (f32[20,256,256]{2,1,0:T(8,128)S(1)}, f32[4,10,256]{2,1,0:T(8,128)S(1)}, f32[4,10,256]{2,1,0:T(8,128)S(1)}) custom-call(bf16[256,2560]{1,0:T(8,128)(2,1)S(1)} %bitcast.15, f32[1,2560]{1,0:T(1,128)S(1)} %broadcast_in_dim.31.gain_ref, bf16[256,512]{1,0:T(8,128)(2,1)S(1)} %collective-permute-done.k_ref.refs_6_), custom_call_target="tpu_custom_call" | custom-call | flops 335544320 | bytes 5242880 | tf_op jit(solution)/shard_map/scores/pallas_call | solution.py:275
  45.8 5.7 %far_scores.1 = (f32[20,256,256]{2,1,0:T(8,128)S(1)}, f32[4,40,256]{2,1,0:T(8,128)S(1)}, s16[576,256]{1,0:T(8,128)(2,1)}) custom-call(s32[2]{0:T(128)S(1)} %subtract_bitcast_fusion.lo, bf16[256,2560]{1,0:T(8,128)(2,1)S(1)} %bitcast.17, bf16[256,2560]{1,0:T(8,128)(2,1)S(1)} %bitcast.10, f32[1,2560]{1,0:T(1,128)S(1)} %broadcast_in_dim.31.gain_ref, ...), custom_call_target="tpu_custom_call" | custom-call | flops 671088640 | bytes 5242880 | tf_op jit(solution)/shard_map/far_scores/pallas_call | solution.py:289
  51.5 6.9 %shard_map.101 = (bf16[256,2560]{1,0:T(8,128)(2,1)}, bf16[256,2560]{1,0:T(8,128)(2,1)}, f32[1,2560]{1,0:T(1,128)S(1)}, s16[576,256]{1,0:T(8,128)(2,1)}, f32[512,...) custom-call(bf16[256,2560]{1,0:T(8,128)(2,1)S(1)} %bitcast.18, ...), custom_call_target="tpu_custom_call" | custom-call | flops 2684354560 | bytes 10485760 | tf_op jit(solution)/shard_map/pallas_call | solution.py:331
  58.4 7.0 %shard_map.102 = (bf16[256,2560]{1,0:T(8,128)(2,1)}, bf16[256,2560]{1,0:T(8,128)(2,1)}, f32[1,2560]{1,0:T(1,128)S(1)}, s16[576,256]{1,0:T(8,128)(2,1)}, f32[512,...) custom-call(bf16[256,2560]{1,0:T(8,128)(2,1)S(1)} %bitcast.19, ...), custom_call_target="tpu_custom_call", output_to_operand_aliasing={{0}: (16, {}), {1}: (17, {}), {2}: (18, {}), {3}: (19, {}),... | custom-call | flops 2684354560 | bytes 10485760 | tf_op jit(solution)/shard_map/pallas_call | solution.py:331
  66.2 6.0 %collective-permute-start.6 = (s16[576,256]{1,0:T(8,128)(2,1)}, s16[576,256]{1,0:T(8,128)(2,1)S(1)}, u32[]{:S(2)}, u32[]{:S(2)}) collective-permute-start(s16[576,256]{1,0:T(8,128)(2,1)} %get-tuple-element.60), channel_id=1, source_target_pairs={{1,0},{2,1},{3,2},{4,3},{5,4},{6,5},{7,6},{8,7},{9,8},{10,9},{11,1... | collective-permute-start | bytes 884744 | tf_op jit(solution)/shard_map/ppermute | solution.py:27
  74.2 10.0 %all_to_all.10 = f32[8,1,2560]{2,1,0:T(1,128)S(1)} all-to-all(f32[8,1,2560]{2,1,0:T(1,128)S(1)} %broadcast_in_dim.35), channel_id=1, replica_groups=mesh['dp'=8,'ctx'=32] {'dp'}, dimensions={0} | all-to-all | bytes 163840 | tf_op jit(solution)/shard_map/all_to_all | solution.py:32
  84.4 8.7 %all_to_all.11 = f32[4,1,2560]{2,1,0:T(1,128)S(1)} all-to-all(f32[4,1,2560]{2,1,0:T(1,128)S(1)} %broadcast_in_dim.39), channel_id=1, replica_groups={{0,8,16,24},{1,9,17,25},{2,10,18,26},{3,11,19,27},{4,12,20,28},{5,13,21..., dimensions={0} | all-to-all | bytes 81920 | tf_op jit(solution)/shard_map/all_to_all | solution.py:32
  95.2 2.5 %copy-done.1 = f32[20,256,256]{2,1,0:T(8,128)S(1)} copy-done((f32[20,256,256]{2,1,0:T(8,128)S(1)}, f32[20,256,256]{2,1,0:T(8,128)}, u32[]{:S(2)}) %copy-start.1) | copy-done | bytes 5242904
  97.7 2.5 %copy-done.3 = f32[20,256,256]{2,1,0:T(8,128)S(1)} copy-done((f32[20,256,256]{2,1,0:T(8,128)S(1)}, f32[20,256,256]{2,1,0:T(8,128)}, u32[]{:S(2)}) %copy-start.3) | copy-done | bytes 5242904
  100.2 2.5 %copy-done.5 = f32[20,256,256]{2,1,0:T(8,128)S(1)} copy-done((f32[20,256,256]{2,1,0:T(8,128)S(1)}, f32[20,256,256]{2,1,0:T(8,128)}, u32[]{:S(2)}) %copy-start.5) | copy-done | bytes 5242904
  102.7 3.3 %near_values.1 = (f32[512,256]{1,0:T(8,128)S(1)}, s16[576,256]{1,0:T(8,128)(2,1)S(1)}, f32[512,256]{1,0:T(8,128)S(1)}) custom-call(bf16[256,2560]{1,0:T(8,128)(2,1)S(1)} %bitcast.13, f32[4,40,256]{2,1,0:T(8,128)S(1)} %get-tuple-element.46.w_ref, f32[20,256,256]{2,1,0:T(8,128)S(1)} %copy-done.5, f32[20,256,256]{2,1,0:T(8,128)S(1)} %copy-done.3, ...), custom_call_target="tpu_custom_call" | custom-call | flops 1006632960 | bytes 15728640 | tf_op jit(solution)/shard_map/near_values/pallas_call | solution.py:311
  106.0 2.9 %collective-permute-start.11 = (s16[576,256]{1,0:T(8,128)(2,1)S(1)}, s16[576,256]{1,0:T(8,128)(2,1)S(1)}, u32[]{:S(2)}, u32[]{:S(2)}) collective-permute-start(s16[576,256]{1,0:T(8,128)(2,1)S(1)} %get-tuple-element.68), channel_id=1, source_target_pairs={{1,0},{2,1},{3,2},{4,3},{5,4},{6,5},{7,6},{8,7},{9,8},{10,9},{11,1... | collective-permute-start | bytes 884744 | tf_op jit(solution)/shard_map/ppermute | solution.py:27
  111.0 6.6 %collective-permute-start.10 = (s16[576,256]{1,0:T(8,128)(2,1)S(1)}, s16[576,256]{1,0:T(8,128)(2,1)S(1)}, u32[]{:S(2)}, u32[]{:S(2)}) collective-permute-start(s16[576,256]{1,0:T(8,128)(2,1)S(1)} %hop.3), channel_id=1, source_target_pairs={{2,0},{3,1},{4,2},{5,3},{6,4},{7,5},{8,6},{9,7},{10,8},{11,9},{12,... | collective-permute-start | bytes 884744 | tf_op jit(solution)/shard_map/ppermute | solution.py:27
  119.8 3.0 %collective-permute-start.13 = (f32[1,2560]{1,0:T(1,128)S(1)}, f32[1,2560]{1,0:T(1,128)S(1)}, u32[]{:S(2)}, u32[]{:S(2)}) collective-permute-start(f32[1,2560]{1,0:T(1,128)S(1)} %reshape_add_fusion), channel_id=1, source_target_pairs={{0,2},{1,3},{2,0},{3,1},{4,6},{5,7},{6,4},{7,5},{8,10},{9,11},{10,... | collective-permute-start | bytes 30728 | tf_op jit(solution)/shard_map/ppermute | solution.py:38
  122.8 24.1 %collective-permute-done.13 = f32[1,2560]{1,0:T(1,128)S(1)} collective-permute-done((f32[1,2560]{1,0:T(1,128)S(1)}, f32[1,2560]{1,0:T(1,128)S(1)}, u32[]{:S(2)}, u32[]{:S(2)}) %collective-permute-start.13) | collective-permute-done | bytes 10272 | tf_op jit(solution)/shard_map/ppermute | solution.py:38
  146.9 3.7 %collective-permute-start.14 = (f32[1,2560]{1,0:T(1,128)S(1)}, f32[1,2560]{1,0:T(1,128)S(1)}, u32[]{:S(2)}, u32[]{:S(2)}) collective-permute-start(f32[1,2560]{1,0:T(1,128)S(1)} %add.11), channel_id=1, source_target_pairs={{0,4},{1,5},{2,6},{3,7},{4,0},{5,1},{6,2},{7,3},{8,12},{9,13},{10,... | collective-permute-start | bytes 30728 | tf_op jit(solution)/shard_map/ppermute | solution.py:38
  150.6 4.0 %collective-permute-done.14 = f32[1,2560]{1,0:T(1,128)S(1)} collective-permute-done((f32[1,2560]{1,0:T(1,128)S(1)}, f32[1,2560]{1,0:T(1,128)S(1)}, u32[]{:S(2)}, u32[]{:S(2)}) %collective-permute-start.14) | collective-permute-done | bytes 10272 | tf_op jit(solution)/shard_map/ppermute | solution.py:38
  (64 shorter events, 25.3 us)
Async XLA Ops:
  0.6 15.1 %collective-permute-start = (bf16[256,512]{1,0:T(8,128)(2,1)}, bf16[256,512]{1,0:T(8,128)(2,1)S(1)}, u32[]{:S(2)}, u32[]{:S(2)}) collective-permute-start(bf16[256,512]{1,0:T(8,128)(2,1)} %bitcast.20), channel_id=1, source_target_pairs={{0,1},{1,2},{2,3},{3,4},{4,5},{5,6},{6,7},{7,8},{8,9},{9,10},{10,1... | collective-permute-start | bytes 786440 | tf_op jit(solution)/shard_map/ppermute | solution.py:27
  4.5 16.0 %collective-permute-start.3 = (bf16[256,512]{1,0:T(8,128)(2,1)}, bf16[256,512]{1,0:T(8,128)(2,1)S(1)}, u32[]{:S(2)}, u32[]{:S(2)}) collective-permute-start(bf16[256,512]{1,0:T(8,128)(2,1)} %bitcast.24), channel_id=1, source_target_pairs={{0,1},{1,2},{2,3},{3,4},{4,5},{5,6},{6,7},{7,8},{8,9},{9,10},{10,1... | collective-permute-start | bytes 786440 | tf_op jit(solution)/shard_map/ppermute | solution.py:27
  15.7 10.6 %collective-permute-start.1 = (bf16[256,512]{1,0:T(8,128)(2,1)S(1)}, bf16[256,512]{1,0:T(8,128)(2,1)S(1)}, u32[]{:S(2)}, u32[]{:S(2)}) collective-permute-start(bf16[256,512]{1,0:T(8,128)(2,1)S(1)} %collective-permute-done.k_ref.refs_6_), channel_id=1, source_target_pairs={{0,1},{1,2},{2,3},{3,4},{4,5},{5,6},{6,7},{7,8},{8,9},{9,10},{10,1... | collective-permute-start | bytes 786440 | tf_op jit(solution)/shard_map/ppermute | solution.py:27
  20.5 12.9 %collective-permute-start.4 = (bf16[256,512]{1,0:T(8,128)(2,1)S(1)}, bf16[256,512]{1,0:T(8,128)(2,1)S(1)}, u32[]{:S(2)}, u32[]{:S(2)}) collective-permute-start(bf16[256,512]{1,0:T(8,128)(2,1)S(1)} %collective-permute-done.3.refs_10_), channel_id=1, source_target_pairs={{0,1},{1,2},{2,3},{3,4},{4,5},{5,6},{6,7},{7,8},{8,9},{9,10},{10,1... | collective-permute-start | bytes 786440 | tf_op jit(solution)/shard_map/ppermute | solution.py:27
  26.3 19.4 %collective-permute-start.2 = (bf16[256,512]{1,0:T(8,128)(2,1)S(1)}, bf16[256,512]{1,0:T(8,128)(2,1)S(1)}, u32[]{:S(2)}, u32[]{:S(2)}) collective-permute-start(bf16[256,512]{1,0:T(8,128)(2,1)S(1)} %collective-permute-done.1.k_ref.refs_5_), channel_id=1, source_target_pairs={{0,1},{1,2},{2,3},{3,4},{4,5},{5,6},{6,7},{7,8},{8,9},{9,10},{10,1... | collective-permute-start | bytes 786440 | tf_op jit(solution)/shard_map/ppermute | solution.py:27
  33.4 10.1 %copy-start.12 = (bf16[256,512]{1,0:T(8,128)(2,1)}, bf16[256,512]{1,0:T(8,128)(2,1)S(1)}, u32[]{:S(2)}) copy-start(bf16[256,512]{1,0:T(8,128)(2,1)S(1)} %collective-permute-done.4.refs_9_) | copy-start | bytes 786436
  33.4 18.0 %collective-permute-start.5 = (bf16[256,512]{1,0:T(8,128)(2,1)S(1)}, bf16[256,512]{1,0:T(8,128)(2,1)S(1)}, u32[]{:S(2)}, u32[]{:S(2)}) collective-permute-start(bf16[256,512]{1,0:T(8,128)(2,1)S(1)} %collective-permute-done.4.refs_9_), channel_id=1, source_target_pairs={{0,1},{1,2},{2,3},{3,4},{4,5},{5,6},{6,7},{7,8},{8,9},{9,10},{10,1... | collective-permute-start | bytes 786440 | tf_op jit(solution)/shard_map/ppermute | solution.py:27
  41.3 17.2 %copy-start = (f32[20,256,256]{2,1,0:T(8,128)}, f32[20,256,256]{2,1,0:T(8,128)S(1)}, u32[]{:S(2)}) copy-start(f32[20,256,256]{2,1,0:T(8,128)S(1)} %get-tuple-element.50.refs_3_.refs_2_) | copy-start | bytes 15728644
  41.3 4.5 %copy-start.8 = (bf16[1,256,2560]{2,1,0:T(8,128)(2,1)S(1)}, bf16[1,256,2560]{2,1,0:T(8,128)(2,1)}, u32[]{:S(2)}) copy-start(bf16[1,256,2560]{2,1,0:T(8,128)(2,1)} %param.6) | copy-start | bytes 3932164
  43.5 14.9 %copy-start.2 = (f32[20,256,256]{2,1,0:T(8,128)}, f32[20,256,256]{2,1,0:T(8,128)S(1)}, u32[]{:S(2)}) copy-start(f32[20,256,256]{2,1,0:T(8,128)S(1)} %get-tuple-element.49.refs_2_.refs_1_) | copy-start | bytes 15728644
  45.7 12.7 %copy-start.4 = (f32[20,256,256]{2,1,0:T(8,128)}, f32[20,256,256]{2,1,0:T(8,128)S(1)}, u32[]{:S(2)}) copy-start(f32[20,256,256]{2,1,0:T(8,128)S(1)} %get-tuple-element.48.refs_1_.refs_0_) | copy-start | bytes 15728644
  45.8 5.7 %copy-start.10 = (bf16[1,256,512]{2,1,0:T(8,128)(2,1)S(1)}, bf16[1,256,512]{2,1,0:T(8,128)(2,1)}, u32[]{:S(2)}) copy-start(bf16[1,256,512]{2,1,0:T(8,128)(2,1)} %param.7) | copy-start | bytes 786436
  45.8 5.7 %copy-start.11 = (bf16[1,256,512]{2,1,0:T(8,128)(2,1)S(1)}, bf16[1,256,512]{2,1,0:T(8,128)(2,1)}, u32[]{:S(2)}) copy-start(bf16[1,256,512]{2,1,0:T(8,128)(2,1)} %param.8) | copy-start | bytes 786436
  45.8 5.7 %copy-start.13 = (bf16[256,512]{1,0:T(8,128)(2,1)S(1)}, bf16[256,512]{1,0:T(8,128)(2,1)}, u32[]{:S(2)}) copy-start(bf16[256,512]{1,0:T(8,128)(2,1)} %copy-done.12) | copy-start | bytes 786436
  66.2 18.1 %collective-permute-start.6 = (s16[576,256]{1,0:T(8,128)(2,1)}, s16[576,256]{1,0:T(8,128)(2,1)S(1)}, u32[]{:S(2)}, u32[]{:S(2)}) collective-permute-start(s16[576,256]{1,0:T(8,128)(2,1)} %get-tuple-element.60), channel_id=1, source_target_pairs={{1,0},{2,1},{3,2},{4,3},{5,4},{6,5},{7,6},{8,7},{9,8},{10,9},{11,1... | collective-permute-start | bytes 884744 | tf_op jit(solution)/shard_map/ppermute | solution.py:27
  72.2 38.7 %collective-permute-start.9 = (s16[576,256]{1,0:T(8,128)(2,1)}, s16[576,256]{1,0:T(8,128)(2,1)S(1)}, u32[]{:S(2)}, u32[]{:S(2)}) collective-permute-start(s16[576,256]{1,0:T(8,128)(2,1)} %get-tuple-element.66), channel_id=1, source_target_pairs={{1,0},{2,1},{3,2},{4,3},{5,4},{6,5},{7,6},{8,7},{9,8},{10,9},{11,1... | collective-permute-start | bytes 884744 | tf_op jit(solution)/shard_map/ppermute | solution.py:27
  93.1 26.6 %collective-permute-start.12 = (f32[1,2560]{1,0:T(1,128)S(1)}, f32[1,2560]{1,0:T(1,128)S(1)}, u32[]{:S(2)}, u32[]{:S(2)}) collective-permute-start(f32[1,2560]{1,0:T(1,128)S(1)} %reduce_sum.25), channel_id=1, source_target_pairs={{0,1},{1,0},{2,3},{3,2},{4,5},{5,4},{6,7},{7,6},{8,9},{9,8},{10,11... | collective-permute-start | bytes 30728 | tf_op jit(solution)/shard_map/ppermute | solution.py:38
  102.7 6.2 %copy-start.15 = (s16[576,256]{1,0:T(8,128)(2,1)S(1)}, s16[576,256]{1,0:T(8,128)(2,1)}, u32[]{:S(2)}) copy-start(s16[576,256]{1,0:T(8,128)(2,1)} %copy-done.14) | copy-start | bytes 884740
  106.0 49.2 %collective-permute-start.11 = (s16[576,256]{1,0:T(8,128)(2,1)S(1)}, s16[576,256]{1,0:T(8,128)(2,1)S(1)}, u32[]{:S(2)}, u32[]{:S(2)}) collective-permute-start(s16[576,256]{1,0:T(8,128)(2,1)S(1)} %get-tuple-element.68), channel_id=1, source_target_pairs={{1,0},{2,1},{3,2},{4,3},{5,4},{6,5},{7,6},{8,7},{9,8},{10,9},{11,1... | collective-permute-start | bytes 884744 | tf_op jit(solution)/shard_map/ppermute | solution.py:27
  108.9 47.2 %collective-permute-start.8 = (s16[576,256]{1,0:T(8,128)(2,1)S(1)}, s16[576,256]{1,0:T(8,128)(2,1)S(1)}, u32[]{:S(2)}, u32[]{:S(2)}) collective-permute-start(s16[576,256]{1,0:T(8,128)(2,1)S(1)} %copy-done.15), channel_id=1, source_target_pairs={{1,0},{2,1},{3,2},{4,3},{5,4},{6,5},{7,6},{8,7},{9,8},{10,9},{11,1... | collective-permute-start | bytes 884744 | tf_op jit(solution)/shard_map/ppermute | solution.py:27
  111.0 44.2 %collective-permute-start.10 = (s16[576,256]{1,0:T(8,128)(2,1)S(1)}, s16[576,256]{1,0:T(8,128)(2,1)S(1)}, u32[]{:S(2)}, u32[]{:S(2)}) collective-permute-start(s16[576,256]{1,0:T(8,128)(2,1)S(1)} %hop.3), channel_id=1, source_target_pairs={{2,0},{3,1},{4,2},{5,3},{6,4},{7,5},{8,6},{9,7},{10,8},{11,9},{12,... | collective-permute-start | bytes 884744 | tf_op jit(solution)/shard_map/ppermute | solution.py:27
  117.8 38.3 %collective-permute-start.7 = (s16[576,256]{1,0:T(8,128)(2,1)S(1)}, s16[576,256]{1,0:T(8,128)(2,1)S(1)}, u32[]{:S(2)}, u32[]{:S(2)}) collective-permute-start(s16[576,256]{1,0:T(8,128)(2,1)S(1)} %hop.2), channel_id=1, source_target_pairs={{2,0},{3,1},{4,2},{5,3},{6,4},{7,5},{8,6},{9,7},{10,8},{11,9},{12,... | collective-permute-start | bytes 884744 | tf_op jit(solution)/shard_map/ppermute | solution.py:27
  119.8 27.1 %collective-permute-start.13 = (f32[1,2560]{1,0:T(1,128)S(1)}, f32[1,2560]{1,0:T(1,128)S(1)}, u32[]{:S(2)}, u32[]{:S(2)}) collective-permute-start(f32[1,2560]{1,0:T(1,128)S(1)} %reshape_add_fusion), channel_id=1, source_target_pairs={{0,2},{1,3},{2,0},{3,1},{4,6},{5,7},{6,4},{7,5},{8,10},{9,11},{10,... | collective-permute-start | bytes 30728 | tf_op jit(solution)/shard_map/ppermute | solution.py:38
  146.9 7.7 %collective-permute-start.14 = (f32[1,2560]{1,0:T(1,128)S(1)}, f32[1,2560]{1,0:T(1,128)S(1)}, u32[]{:S(2)}, u32[]{:S(2)}) collective-permute-start(f32[1,2560]{1,0:T(1,128)S(1)} %add.11), channel_id=1, source_target_pairs={{0,4},{1,5},{2,6},{3,7},{4,0},{5,1},{6,2},{7,3},{8,12},{9,13},{10,... | collective-permute-start | bytes 30728 | tf_op jit(solution)/shard_map/ppermute | solution.py:38
  (7 other events, 12.7 us)

commit v6 on v5

--- a/solution.py
+++ b/solution.py
@@ -33,9 +33,35 @@
     return jnp.sum(parts, axis=0)
 
 
-def pair_sum(value, step):
-    pairs = [(i, i ^ step) for i in range(lax.axis_size("ctx"))]
-    return value + lax.ppermute(value, "ctx", pairs)
+def ring_kernel(place, parts, out):
+    count = parts.shape[0]
+    total = parts[pl.ds(place[0], 1), :]
+    for r in range(1, count):
+        total = total + parts[pl.ds((place[0] + r) % count, 1), :]
+    out[...] = total
+
+
+def ring_sum(value):
+    count = lax.axis_size("ctx")
+    step = 1
+    while step < Z_CHIPS:
+        pairs = [
+            (i, i - i % Z_CHIPS + (i + step) % Z_CHIPS) for i in range(count)
+        ]
+        value = jnp.concatenate([value, lax.ppermute(value, "ctx", pairs)], axis=0)
+        step *= 2
+    place = (lax.axis_index("ctx") % Z_CHIPS).reshape(1)
+    return pl.pallas_call(
+        ring_kernel,
+        out_shape=jax.ShapeDtypeStruct((1, value.shape[1]), jnp.float32),
+        in_specs=[
+            pl.BlockSpec(memory_space=pltpu.SMEM),
+            pl.BlockSpec(memory_space=pltpu.VMEM),
+        ],
+        out_specs=pl.BlockSpec(memory_space=pltpu.VMEM),
+        compiler_params=pltpu.CompilerParams(vmem_limit_bytes=4 * 2**20),
+        name="ring_sum",
+    )(place, value)
 
 
 def encode(value):
@@ -126,13 +152,13 @@
                 p_low[here, g * rows : (g + 1) * rows] = (e_ref[g, here, :] * weight).astype(
                     jnp.bfloat16
                 )
-    dv_ref[:HD, :], dv_ref[HD:, :] = encode(dot(p_low[...], g_all[...]).T)
-
-
-def store_parts(refs, total, rows):
+    dv_ref[0, :HD, :], dv_ref[0, HD:, :] = encode(dot(p_low[...], g_all[...]).T)
+
+
+def store_parts(middle_ref, near_ref, own_ref, total, rows):
     middle, nearest, own = (total[j * rows : (j + 1) * rows, :].T for j in range(REACH - 1))
-    refs[0][...], refs[2][...] = middle, own
-    refs[1][:HD, :], refs[1][HD:, :] = encode(nearest)
+    middle_ref[...], own_ref[...] = middle, own
+    near_ref[:HD, :], near_ref[HD:, :] = encode(nearest)
 
 
 def values_kernel(group, g_ref, w_ref, *refs):
@@ -151,14 +177,14 @@
                 there = slice(j * rows + b * BLOCK, j * rows + (b + 1) * BLOCK)
                 p_low[there, g * rows : (g + 1) * rows] = probs.astype(jnp.bfloat16)
     dv = dot(p_low[...], g_all[...])
-    store_parts(dv_refs, dv, rows)
+    store_parts(dv_refs[0], dv_refs[1].at[0], dv_refs[2], dv, rows)
 
 
 def grads_kernel(group, rows, skip, q_ref, g_ref, gain_ref, w_ref, *refs):
     e_refs, k_refs, v_refs = (refs[i * REACH : (i + 1) * REACH] for i in range(3))
     refs = refs[3 * REACH + skip :]
-    o_ref, dq_ref, gain_out, *dk_refs = refs[: REACH + 3]
-    k_t, v_t, v_all, p_all, ds_all, q_all = refs[REACH + 3 :]
+    o_ref, dq_ref, gain_out, *dk_refs = refs[:6]
+    k_t, v_t, v_all, p_all, ds_all, q_all = refs[6:]
     per = rows // BLOCK
     blocks = REACH * per
     factor = 1.0 / math.sqrt(HD)
@@ -193,28 +219,36 @@
         dq_ref[:, cols] = (dscaled * gain).astype(jnp.bfloat16)
         gain_out[:, cols] = jnp.sum(dscaled * q32, axis=0, keepdims=True)
     dk = dot(ds_all[...], q_all[...]) * factor
-    dk_refs[0][:HD, :], dk_refs[0][HD:, :] = encode(dk[:rows, :].T)
-    store_parts(dk_refs[1:], dk[rows:, :], rows)
-
-
-def hop_kernel(kv_count, last, *refs):
+    dk_codes, dk_middle, dk_own = dk_refs
+    dk_codes[0, :HD, :], dk_codes[0, HD:, :] = encode(dk[:rows, :].T)
+    store_parts(dk_middle, dk_codes.at[1], dk_own, dk[rows:, :], rows)
+
+
+def hop_kernel(kv_count, picks, last, *refs):
     *messages, part, out = refs
     for c in range(kv_count):
         at, here = c * CODE_ROWS, slice(c * HD, (c + 1) * HD)
         total = part[here, :]
-        for message in messages:
-            total = total + decode(message[at : at + HD, :], message[at + HD : at + CODE_ROWS, :])
+        for message, pick in zip(messages, picks, strict=True):
+            total = total + decode(
+                message[pick, at : at + HD, :], message[pick, at + HD : at + CODE_ROWS, :]
+            )
         if last:
             out[:, here] = total.T.astype(jnp.bfloat16)
         else:
-            out[at : at + HD, :], out[at + HD : at + CODE_ROWS, :] = encode(total)
+            out[0, at : at + HD, :], out[0, at + HD : at + CODE_ROWS, :] = encode(total)
 
 
 def hop(messages, part, last):
     kv_channels, rows = part.shape
-    shape = jax.ShapeDtypeStruct((rows, kv_channels), jnp.bfloat16) if last else messages[0]
-    return pl.pallas_call(
-        functools.partial(hop_kernel, kv_channels // HD, last),
+    messages, picks = zip(*messages, strict=True)
+    shape = (
+        jax.ShapeDtypeStruct((rows, kv_channels), jnp.bfloat16)
+        if last
+        else jax.ShapeDtypeStruct((1, *messages[0].shape[1:]), jnp.int16)
+    )
+    return pl.pallas_call(
+        functools.partial(hop_kernel, kv_channels // HD, picks, last),
         out_shape=jax.ShapeDtypeStruct(shape.shape, shape.dtype),
         compiler_params=pltpu.CompilerParams(vmem_limit_bytes=8 * 2**20),
         cost_estimate=pl.CostEstimate(
@@ -236,7 +270,9 @@
         self.wide = pl.BlockSpec((rows, group * HD), lambda c, *_: (0, c + first))
         self.line = pl.BlockSpec((1, group * HD), lambda c, *_: (0, c + first))
         self.thin = pl.BlockSpec((rows, HD), lambda c, *_: (0, c + first))
-        self.code = pl.BlockSpec((CODE_ROWS, rows), lambda c, *_: (c + first, 0))
+        self.code, self.codes = (
+            pl.BlockSpec((n, CODE_ROWS, rows), lambda c, *_: (0, c + first, 0)) for n in (1, 2)
+        )
         self.part = pl.BlockSpec((HD, rows), lambda c, *_: (c + first, 0))
         self.heads = pl.BlockSpec((group, rows, rows), lambda c, *_: (c + first, 0, 0))
         self.stat = pl.BlockSpec((1, self.stat_rows, rows), lambda c, *_: (c + first, 0, 0))
@@ -256,8 +292,8 @@
     def weight_array(self):
         return self.array(jnp.float32, self.kv_count, self.group * self.blocks, self.rows)
 
-    def code_array(self):
-        return self.array(jnp.int16, self.kv_count * CODE_ROWS, self.rows)
+    def code_array(self, count=1):
+        return self.array(jnp.int16, count, self.kv_count * CODE_ROWS, self.rows)
 
     def part_array(self):
         return self.array(jnp.float32, self.kv_channels, self.rows)
@@ -332,13 +368,13 @@
         functools.partial(grads_kernel, s.group, s.rows, len(before)),
         out_shape=[s.array(jnp.bfloat16, s.rows, s.channels)] * 2
         + [s.array(jnp.float32, 1, s.channels)]
-        + [s.code_array(), s.part_array()] * 2,
+        + [s.code_array(2), s.part_array(), s.part_array()],
         grid=(count,),
         in_specs=[s.wide, s.wide, s.line, s.weight]
         + [s.heads] * REACH
         + [s.thin] * (2 * REACH)
         + [pl.BlockSpec(memory_space=pl.ANY)] * len(before),
-        out_specs=[s.wide, s.wide, s.line] + [s.code, s.part] * 2,
+        out_specs=[s.wide, s.wide, s.line, s.codes, s.part, s.part],
         scratch_shapes=[
             pltpu.VMEM((HD, width), jnp.bfloat16),
             pltpu.VMEM((HD, width), jnp.bfloat16),
@@ -379,23 +415,20 @@
     dv_middle, dv_near, dv_own = near_values(q, own_keys, do, weights, heads[1:])
     dv_near = shifted(dv_near, -1)
     early = attention_grads(0, half, [], q, do, gain, weights, heads, keys, values)
-    dv_middle = shifted(hop([dv_far], dv_middle, False), -2)
-    attn_out, query_grad, gain_term, dk_far, dk_middle, dk_near, dk_own = attention_grads(
+    dv_middle = shifted(hop([(dv_far, 0)], dv_middle, False), -2)
+    attn_out, query_grad, gain_term, dk_codes, dk_middle, dk_own = attention_grads(
         half, half, early, q, do, gain, weights, heads, keys, values
     )
-    dk_far = shifted(dk_far, -1)
-    dk_near = shifted(dk_near, -1)
+    dk_codes = shifted(dk_codes, -1)
     count = lax.axis_size("ctx")
     columns = [[i + z for i in range(0, count, Z_CHIPS)] for z in range(Z_CHIPS)]
     total = gathered_sum(gain_term, "dp", lax.axis_size("dp"))
-    dk_far, total = together((dk_far, total))
-    dk_middle = shifted(hop([dk_far], dk_middle, False), -2)
     total = gathered_sum(total, "ctx", count // Z_CHIPS, columns)
-    total = pair_sum(total, 1)
-    total = pair_sum(total, 2)
-    gain_grad = pair_sum(total, 4)
-    value_grad = hop([dv_middle, dv_near], dv_own, True)
-    key_grad = hop([dk_middle, dk_near], dk_own, True)
+    dk_codes, total = together((dk_codes, total))
+    dk_middle = shifted(hop([(dk_codes, 0)], dk_middle, False), -2)
+    gain_grad = ring_sum(total)
+    value_grad = hop([(dv_middle, 0), (dv_near, 0)], dv_own, True)
+    key_grad = hop([(dk_middle, 0), (dk_codes, 1)], dk_own, True)
     return (
         attn_out[None],
         query_grad[None],

time: 158 us -> 147 us (0.930)
  the two profiles are of different devices: /device:TPU:2 before, /device:TPU:32 now
where the time goes in v6:
time: 147 us; the launch traced here: 146 us
  starting transfers between devices  47.5 us (32%)
  Pallas kernels  31.8 us (22%)
  waiting for transfers between devices  30.9 us (21%)
  blocking collectives  22.4 us (15%)
  local copies, waits for them, and re-layouts  11.4 us (8%)
  other arithmetic  1.53 us (1%)
    ppermute x11, starting transfers between devices, shifted(): return lax.ppermute(value, 'ctx', pairs)  35.1 us
    ppermute x11, waiting for transfers between devices, shifted(): return lax.ppermute(value, 'ctx', pairs)  30.9 us
    all_to_all x2, blocking collectives, gathered_sum(): lax.all_to_all(copies, axis, 0, 0, tiled=True, axis_index_groups=groups)  22.4 us
    pallas_call x2, Pallas kernels, attention_grads(): pl.pallas_call(functools.partial(grads_kernel, s.group, s.rows, len(befor...  13.3 us
    ppermute x3, starting transfers between devices, ring_sum(): value = jnp.concatenate([value, lax.ppermute(value, 'ctx', pairs)], axis=0)  12.4 us
    unnamed x36, local copies, waits for them, and re-layouts  10.6 us
    pallas_call x3, Pallas kernels, chunk_scores(): pl.pallas_call(functools.partial(scores_kernel, s.group, own), out_shape=...  6.66 us
    pallas_call x1, Pallas kernels, far_scores(): pl.pallas_call(functools.partial(far_kernel, s.group), out_shape=[s.heads...  4.92 us
  transfers between devices with their start and end apart: 14, of which 6 were waited for; matrix products, arithmetic and copies ran while one was open for 2% of the time, Pallas kernels for 12%

profile of v6, /device:TPU:32, one launch (start us, length us, event | category | flops | bytes accessed | tf_op | source)
XLA Modules:
  0.0 146.5 jit_solution(3807736740483358273)
XLA Ops:
  0.6 3.8 %collective-permute-start = (bf16[256,512]{1,0:T(8,128)(2,1)}, bf16[256,512]{1,0:T(8,128)(2,1)S(1)}, u32[]{:S(2)}, u32[]{:S(2)}) collective-permute-start(bf16[256,512]{1,0:T(8,128)(2,1)} %bitcast.21), channel_id=1, source_target_pairs={{0,1},{1,2},{2,3},{3,4},{4,5},{5,6},{6,7},{7,8},{8,9},{9,10},{10,1... | collective-permute-start | bytes 786440 | tf_op jit(solution)/shard_map/ppermute | solution.py:27
  4.5 3.8 %collective-permute-start.3 = (bf16[256,512]{1,0:T(8,128)(2,1)}, bf16[256,512]{1,0:T(8,128)(2,1)S(1)}, u32[]{:S(2)}, u32[]{:S(2)}) collective-permute-start(bf16[256,512]{1,0:T(8,128)(2,1)} %bitcast.25), channel_id=1, source_target_pairs={{0,1},{1,2},{2,3},{3,4},{4,5},{5,6},{6,7},{7,8},{8,9},{9,10},{10,1... | collective-permute-start | bytes 786440 | tf_op jit(solution)/shard_map/ppermute | solution.py:27
  8.3 3.6 %collective-permute-done.k_ref.refs_6_ = bf16[256,512]{1,0:T(8,128)(2,1)S(1)} collective-permute-done((bf16[256,512]{1,0:T(8,128)(2,1)}, bf16[256,512]{1,0:T(8,128)(2,1)S(1)}, u32[]{:S(2)}, u32[]{:S(2)}) %collective-permute-start) | collective-permute-done | bytes 262176 | tf_op jit(solution)/shard_map/ppermute | solution.py:27
  11.9 3.8 %collective-permute-start.1 = (bf16[256,512]{1,0:T(8,128)(2,1)S(1)}, bf16[256,512]{1,0:T(8,128)(2,1)S(1)}, u32[]{:S(2)}, u32[]{:S(2)}) collective-permute-start(bf16[256,512]{1,0:T(8,128)(2,1)S(1)} %collective-permute-done.k_ref.refs_6_), channel_id=1, source_target_pairs={{0,1},{1,2},{2,3},{3,4},{4,5},{5,6},{6,7},{7,8},{8,9},{9,10},{10,1... | collective-permute-start | bytes 786440 | tf_op jit(solution)/shard_map/ppermute | solution.py:27
  17.5 3.8 %collective-permute-start.4 = (bf16[256,512]{1,0:T(8,128)(2,1)S(1)}, bf16[256,512]{1,0:T(8,128)(2,1)S(1)}, u32[]{:S(2)}, u32[]{:S(2)}) collective-permute-start(bf16[256,512]{1,0:T(8,128)(2,1)S(1)} %collective-permute-done.3.refs_10_), channel_id=1, source_target_pairs={{0,1},{1,2},{2,3},{3,4},{4,5},{5,6},{6,7},{7,8},{8,9},{9,10},{10,1... | collective-permute-start | bytes 786440 | tf_op jit(solution)/shard_map/ppermute | solution.py:27
  23.2 3.8 %collective-permute-start.2 = (bf16[256,512]{1,0:T(8,128)(2,1)S(1)}, bf16[256,512]{1,0:T(8,128)(2,1)S(1)}, u32[]{:S(2)}, u32[]{:S(2)}) collective-permute-start(bf16[256,512]{1,0:T(8,128)(2,1)S(1)} %collective-permute-done.1.k_ref.refs_5_), channel_id=1, source_target_pairs={{0,1},{1,2},{2,3},{3,4},{4,5},{5,6},{6,7},{7,8},{8,9},{9,10},{10,1... | collective-permute-start | bytes 786440 | tf_op jit(solution)/shard_map/ppermute | solution.py:27
  28.8 3.8 %collective-permute-start.5 = (bf16[256,512]{1,0:T(8,128)(2,1)S(1)}, bf16[256,512]{1,0:T(8,128)(2,1)S(1)}, u32[]{:S(2)}, u32[]{:S(2)}) collective-permute-start(bf16[256,512]{1,0:T(8,128)(2,1)S(1)} %collective-permute-done.4.refs_9_), channel_id=1, source_target_pairs={{0,1},{1,2},{2,3},{3,4},{4,5},{5,6},{6,7},{7,8},{8,9},{9,10},{10,1... | collective-permute-start | bytes 786440 | tf_op jit(solution)/shard_map/ppermute | solution.py:27
  36.2 2.3 %scores_own.1 = (f32[20,256,256]{2,1,0:T(8,128)S(1)}, f32[4,10,256]{2,1,0:T(8,128)S(1)}, f32[4,10,256]{2,1,0:T(8,128)S(1)}) custom-call(bf16[256,2560]{1,0:T(8,128)(2,1)S(1)} %bitcast.15, f32[1,2560]{1,0:T(1,128)S(1)} %broadcast_in_dim.29.gain_ref, bf16[256,512]{1,0:T(8,128)(2,1)S(1)} %bitcast.22), custom_call_target="tpu_custom_call" | custom-call | flops 335544320 | bytes 5242880 | tf_op jit(solution)/shard_map/scores_own/pallas_call | solution.py:311
  38.5 2.2 %scores.3 = (f32[20,256,256]{2,1,0:T(8,128)S(1)}, f32[4,10,256]{2,1,0:T(8,128)S(1)}, f32[4,10,256]{2,1,0:T(8,128)S(1)}) custom-call(bf16[256,2560]{1,0:T(8,128)(2,1)S(1)} %bitcast.16, f32[1,2560]{1,0:T(1,128)S(1)} %broadcast_in_dim.29.gain_ref, bf16[256,512]{1,0:T(8,128)(2,1)S(1)} %collective-permute-done.k_ref.refs_6_), custom_call_target="tpu_custom_call" | custom-call | flops 335544320 | bytes 5242880 | tf_op jit(solution)/shard_map/scores/pallas_call | solution.py:311
  40.8 2.2 %scores.2 = (f32[20,256,256]{2,1,0:T(8,128)S(1)}, f32[4,10,256]{2,1,0:T(8,128)S(1)}, f32[4,10,256]{2,1,0:T(8,128)S(1)}) custom-call(bf16[256,2560]{1,0:T(8,128)(2,1)S(1)} %bitcast.17, f32[1,2560]{1,0:T(1,128)S(1)} %broadcast_in_dim.29.gain_ref, bf16[256,512]{1,0:T(8,128)(2,1)S(1)} %collective-permute-done.1.k_ref.refs_5_), custom_call_target="tpu_custom_call" | custom-call | flops 335544320 | bytes 5242880 | tf_op jit(solution)/shard_map/scores/pallas_call | solution.py:311
  43.1 4.9 %far_scores.1 = (f32[20,256,256]{2,1,0:T(8,128)S(1)}, f32[4,40,256]{2,1,0:T(8,128)S(1)}, s16[1,576,256]{2,1,0:T(8,128)(2,1)S(1)}) custom-call(s32[2]{0:T(128)S(1)} %subtract_bitcast_fusion.lo, bf16[256,2560]{1,0:T(8,128)(2,1)S(1)} %bitcast.18, bf16[256,2560]{1,0:T(8,128)(2,1)S(1)} %bitcast.11, f32[1,2560]{1,0:T(1,128)S(1)} %broadcast_in_dim.29.gain_ref, ...), custom_call_target="tpu_custom_call" | custom-call | flops 671088640 | bytes 5242880 | tf_op jit(solution)/shard_map/far_scores/pallas_call | solution.py:325
  48.1 6.7 %shard_map.101 = (bf16[256,2560]{1,0:T(8,128)(2,1)}, bf16[256,2560]{1,0:T(8,128)(2,1)}, f32[1,2560]{1,0:T(1,128)S(1)}, s16[2,576,256]{2,1,0:T(8,128)(2,1)}, f32[...) custom-call(bf16[256,2560]{1,0:T(8,128)(2,1)S(1)} %bitcast.19, bf16[256,2560]{1,0:T(8,128)(2,1)S(1)} %bitcast.12, ...), custom_call_target="tpu_custom_call" | custom-call | flops 2684354560 | bytes 10485760 | tf_op jit(solution)/shard_map/pallas_call | solution.py:367
  54.7 6.6 %shard_map.102 = (bf16[256,2560]{1,0:T(8,128)(2,1)}, bf16[256,2560]{1,0:T(8,128)(2,1)}, f32[1,2560]{1,0:T(1,128)S(1)}, s16[2,576,256]{2,1,0:T(8,128)(2,1)}, f32[...) custom-call(bf16[256,2560]{1,0:T(8,128)(2,1)S(1)} %bitcast.20, ...), custom_call_target="tpu_custom_call", output_to_operand_aliasing={{0}: (16, {}), {1}: (17, {}), {2}: (18, {}), {3}: (19, {}),... | custom-call | flops 2684354560 | bytes 10485760 | tf_op jit(solution)/shard_map/pallas_call | solution.py:367
  63.5 10.0 %all_to_all.10 = f32[8,1,2560]{2,1,0:T(1,128)S(1)} all-to-all(f32[8,1,2560]{2,1,0:T(1,128)S(1)} %broadcast_in_dim.33), channel_id=1, replica_groups=mesh['dp'=8,'ctx'=32] {'dp'}, dimensions={0} | all-to-all | bytes 163840 | tf_op jit(solution)/shard_map/all_to_all | solution.py:32
  73.6 12.4 %all_to_all.11 = f32[4,1,2560]{2,1,0:T(1,128)S(1)} all-to-all(f32[4,1,2560]{2,1,0:T(1,128)S(1)} %broadcast_in_dim.34), channel_id=1, replica_groups={{0,8,16,24},{1,9,17,25},{2,10,18,26},{3,11,19,27},{4,12,20,28},{5,13,21..., dimensions={0} | all-to-all | bytes 81920 | tf_op jit(solution)/shard_map/all_to_all | solution.py:32
  86.6 5.5 %collective-permute-start.8 = (s16[1,576,256]{2,1,0:T(8,128)(2,1)S(1)}, s16[1,576,256]{2,1,0:T(8,128)(2,1)S(1)}, u32[]{:S(2)}, u32[]{:S(2)}) collective-permute-start(s16[1,576,256]{2,1,0:T(8,128)(2,1)S(1)} %get-tuple-element.62), channel_id=1, source_target_pairs={{1,0},{2,1},{3,2},{4,3},{5,4},{6,5},{7,6},{8,7},{9,8},{10,9},{11,1... | collective-permute-start | bytes 884744 | tf_op jit(solution)/shard_map/ppermute | solution.py:27
  92.2 3.0 %collective-permute-start.12 = (f32[2,2560]{1,0:T(2,128)S(1)}, f32[2,2560]{1,0:T(2,128)S(1)}, u32[]{:S(2)}, u32[]{:S(2)}) collective-permute-start(f32[2,2560]{1,0:T(2,128)S(1)} %pad_maximum_fusion.2), channel_id=1, source_target_pairs={{0,2},{1,3},{2,4},{3,5},{4,6},{5,7},{6,0},{7,1},{8,10},{9,11},{10,... | collective-permute-start | bytes 61448 | tf_op jit(solution)/shard_map/ppermute | solution.py:51
  95.2 2.5 %copy-done.1 = f32[20,256,256]{2,1,0:T(8,128)S(1)} copy-done((f32[20,256,256]{2,1,0:T(8,128)S(1)}, f32[20,256,256]{2,1,0:T(8,128)}, u32[]{:S(2)}) %copy-start.1) | copy-done | bytes 5242904
  97.7 2.5 %copy-done.3 = f32[20,256,256]{2,1,0:T(8,128)S(1)} copy-done((f32[20,256,256]{2,1,0:T(8,128)S(1)}, f32[20,256,256]{2,1,0:T(8,128)}, u32[]{:S(2)}) %copy-start.3) | copy-done | bytes 5242904
  100.2 2.5 %copy-done.5 = f32[20,256,256]{2,1,0:T(8,128)S(1)} copy-done((f32[20,256,256]{2,1,0:T(8,128)S(1)}, f32[20,256,256]{2,1,0:T(8,128)}, u32[]{:S(2)}) %copy-start.5) | copy-done | bytes 5242904
  102.7 3.9 %near_values.1 = (f32[512,256]{1,0:T(8,128)S(1)}, s16[1,576,256]{2,1,0:T(8,128)(2,1)}, f32[512,256]{1,0:T(8,128)S(1)}) custom-call(bf16[256,2560]{1,0:T(8,128)(2,1)S(1)} %bitcast.14, f32[4,40,256]{2,1,0:T(8,128)S(1)} %get-tuple-element.44.w_ref, f32[20,256,256]{2,1,0:T(8,128)S(1)} %copy-done.5, f32[20,256,256]{2,1,0:T(8,128)S(1)} %copy-done.3, ...), custom_call_target="tpu_custom_call" | custom-call | flops 1006632960 | bytes 15728640 | tf_op jit(solution)/shard_map/near_values/pallas_call | solution.py:347
  111.0 8.8 %collective-permute-start.13 = (f32[4,2560]{1,0:T(4,128)S(1)}, f32[4,2560]{1,0:T(4,128)S(1)}, u32[]{:S(2)}, u32[]{:S(2)}) collective-permute-start(f32[4,2560]{1,0:T(4,128)S(1)} %pad_maximum_fusion.1), channel_id=1, source_target_pairs={{0,4},{1,5},{2,6},{3,7},{4,0},{5,1},{6,2},{7,3},{8,12},{9,13},{10,... | collective-permute-start | bytes 122888 | tf_op jit(solution)/shard_map/ppermute | solution.py:51
  122.0 12.4 %collective-permute-done.10.refs_1_ = s16[1,576,256]{2,1,0:T(8,128)(2,1)S(1)} collective-permute-done((s16[1,576,256]{2,1,0:T(8,128)(2,1)}, s16[1,576,256]{2,1,0:T(8,128)(2,1)S(1)}, u32[]{:S(2)}, u32[]{:S(2)}) %collective-permute-start.10) | collective-permute-done | bytes 294944 | tf_op jit(solution)/shard_map/ppermute | solution.py:27
  136.0 9.5 %collective-permute-done.7.refs_0_ = s16[1,576,256]{2,1,0:T(8,128)(2,1)S(1)} collective-permute-done((s16[1,576,256]{2,1,0:T(8,128)(2,1)}, s16[1,576,256]{2,1,0:T(8,128)(2,1)S(1)}, u32[]{:S(2)}, u32[]{:S(2)}) %collective-permute-start.7) | collective-permute-done | bytes 294944 | tf_op jit(solution)/shard_map/ppermute | solution.py:27
  (66 shorter events, 21.1 us)
Async XLA Ops:
  0.6 11.3 %collective-permute-start = (bf16[256,512]{1,0:T(8,128)(2,1)}, bf16[256,512]{1,0:T(8,128)(2,1)S(1)}, u32[]{:S(2)}, u32[]{:S(2)}) collective-permute-start(bf16[256,512]{1,0:T(8,128)(2,1)} %bitcast.21), channel_id=1, source_target_pairs={{0,1},{1,2},{2,3},{3,4},{4,5},{5,6},{6,7},{7,8},{8,9},{9,10},{10,1... | collective-permute-start | bytes 786440 | tf_op jit(solution)/shard_map/ppermute | solution.py:27
  4.5 13.1 %collective-permute-start.3 = (bf16[256,512]{1,0:T(8,128)(2,1)}, bf16[256,512]{1,0:T(8,128)(2,1)S(1)}, u32[]{:S(2)}, u32[]{:S(2)}) collective-permute-start(bf16[256,512]{1,0:T(8,128)(2,1)} %bitcast.25), channel_id=1, source_target_pairs={{0,1},{1,2},{2,3},{3,4},{4,5},{5,6},{6,7},{7,8},{8,9},{9,10},{10,1... | collective-permute-start | bytes 786440 | tf_op jit(solution)/shard_map/ppermute | solution.py:27
  11.9 11.2 %collective-permute-start.1 = (bf16[256,512]{1,0:T(8,128)(2,1)S(1)}, bf16[256,512]{1,0:T(8,128)(2,1)S(1)}, u32[]{:S(2)}, u32[]{:S(2)}) collective-permute-start(bf16[256,512]{1,0:T(8,128)(2,1)S(1)} %collective-permute-done.k_ref.refs_6_), channel_id=1, source_target_pairs={{0,1},{1,2},{2,3},{3,4},{4,5},{5,6},{6,7},{7,8},{8,9},{9,10},{10,1... | collective-permute-start | bytes 786440 | tf_op jit(solution)/shard_map/ppermute | solution.py:27
  17.5 11.2 %collective-permute-start.4 = (bf16[256,512]{1,0:T(8,128)(2,1)S(1)}, bf16[256,512]{1,0:T(8,128)(2,1)S(1)}, u32[]{:S(2)}, u32[]{:S(2)}) collective-permute-start(bf16[256,512]{1,0:T(8,128)(2,1)S(1)} %collective-permute-done.3.refs_10_), channel_id=1, source_target_pairs={{0,1},{1,2},{2,3},{3,4},{4,5},{5,6},{6,7},{7,8},{8,9},{9,10},{10,1... | collective-permute-start | bytes 786440 | tf_op jit(solution)/shard_map/ppermute | solution.py:27
  23.1 17.6 %copy-start.12 = (bf16[256,512]{1,0:T(8,128)(2,1)}, bf16[256,512]{1,0:T(8,128)(2,1)S(1)}, u32[]{:S(2)}) copy-start(bf16[256,512]{1,0:T(8,128)(2,1)S(1)} %collective-permute-done.1.k_ref.refs_5_) | copy-start | bytes 786436
  23.2 19.8 %collective-permute-start.2 = (bf16[256,512]{1,0:T(8,128)(2,1)S(1)}, bf16[256,512]{1,0:T(8,128)(2,1)S(1)}, u32[]{:S(2)}, u32[]{:S(2)}) collective-permute-start(bf16[256,512]{1,0:T(8,128)(2,1)S(1)} %collective-permute-done.1.k_ref.refs_5_), channel_id=1, source_target_pairs={{0,1},{1,2},{2,3},{3,4},{4,5},{5,6},{6,7},{7,8},{8,9},{9,10},{10,1... | collective-permute-start | bytes 786440 | tf_op jit(solution)/shard_map/ppermute | solution.py:27
  28.8 12.0 %copy-start.14 = (bf16[256,512]{1,0:T(8,128)(2,1)}, bf16[256,512]{1,0:T(8,128)(2,1)S(1)}, u32[]{:S(2)}) copy-start(bf16[256,512]{1,0:T(8,128)(2,1)S(1)} %collective-permute-done.4.refs_9_) | copy-start | bytes 786436
  28.8 19.2 %collective-permute-start.5 = (bf16[256,512]{1,0:T(8,128)(2,1)S(1)}, bf16[256,512]{1,0:T(8,128)(2,1)S(1)}, u32[]{:S(2)}, u32[]{:S(2)}) collective-permute-start(bf16[256,512]{1,0:T(8,128)(2,1)S(1)} %collective-permute-done.4.refs_9_), channel_id=1, source_target_pairs={{0,1},{1,2},{2,3},{3,4},{4,5},{5,6},{6,7},{7,8},{8,9},{9,10},{10,1... | collective-permute-start | bytes 786440 | tf_op jit(solution)/shard_map/ppermute | solution.py:27
  38.5 16.2 %copy-start = (f32[20,256,256]{2,1,0:T(8,128)}, f32[20,256,256]{2,1,0:T(8,128)S(1)}, u32[]{:S(2)}) copy-start(f32[20,256,256]{2,1,0:T(8,128)S(1)} %get-tuple-element.48.refs_3_.refs_2_) | copy-start | bytes 15728644
  40.8 14.0 %copy-start.2 = (f32[20,256,256]{2,1,0:T(8,128)}, f32[20,256,256]{2,1,0:T(8,128)S(1)}, u32[]{:S(2)}) copy-start(f32[20,256,256]{2,1,0:T(8,128)S(1)} %get-tuple-element.47.refs_2_.refs_1_) | copy-start | bytes 15728644
  43.0 11.7 %copy-start.4 = (f32[20,256,256]{2,1,0:T(8,128)}, f32[20,256,256]{2,1,0:T(8,128)S(1)}, u32[]{:S(2)}) copy-start(f32[20,256,256]{2,1,0:T(8,128)S(1)} %get-tuple-element.46.refs_1_.refs_0_) | copy-start | bytes 15728644
  43.0 5.0 %copy-start.10 = (bf16[1,256,512]{2,1,0:T(8,128)(2,1)S(1)}, bf16[1,256,512]{2,1,0:T(8,128)(2,1)}, u32[]{:S(2)}) copy-start(bf16[1,256,512]{2,1,0:T(8,128)(2,1)} %param.7) | copy-start | bytes 786436
  43.0 5.0 %copy-start.11 = (bf16[1,256,512]{2,1,0:T(8,128)(2,1)S(1)}, bf16[1,256,512]{2,1,0:T(8,128)(2,1)}, u32[]{:S(2)}) copy-start(bf16[1,256,512]{2,1,0:T(8,128)(2,1)} %param.8) | copy-start | bytes 786436
  43.0 5.0 %copy-start.13 = (bf16[256,512]{1,0:T(8,128)(2,1)S(1)}, bf16[256,512]{1,0:T(8,128)(2,1)}, u32[]{:S(2)}) copy-start(bf16[256,512]{1,0:T(8,128)(2,1)} %copy-done.12) | copy-start | bytes 786436
  43.1 5.0 %copy-start.15 = (bf16[256,512]{1,0:T(8,128)(2,1)S(1)}, bf16[256,512]{1,0:T(8,128)(2,1)}, u32[]{:S(2)}) copy-start(bf16[256,512]{1,0:T(8,128)(2,1)} %copy-done.14) | copy-start | bytes 786436
  61.4 24.6 %collective-permute-start.6 = (s16[2,576,256]{2,1,0:T(8,128)(2,1)}, s16[2,576,256]{2,1,0:T(8,128)(2,1)S(1)}, u32[]{:S(2)}, u32[]{:S(2)}) collective-permute-start(s16[2,576,256]{2,1,0:T(8,128)(2,1)} %get-tuple-element.57), channel_id=1, source_target_pairs={{1,0},{2,1},{3,2},{4,3},{5,4},{6,5},{7,6},{8,7},{9,8},{10,9},{11,1... | collective-permute-start | bytes 1769480 | tf_op jit(solution)/shard_map/ppermute | solution.py:27
  86.0 6.1 %collective-permute-start.11 = (f32[1,2560]{1,0:T(1,128)S(1)}, f32[1,2560]{1,0:T(1,128)S(1)}, u32[]{:S(2)}, u32[]{:S(2)}) collective-permute-start(f32[1,2560]{1,0:T(1,128)S(1)} %reduce_sum.22), channel_id=1, source_target_pairs={{0,1},{1,2},{2,3},{3,4},{4,5},{5,6},{6,7},{7,0},{8,9},{9,10},{10,1... | collective-permute-start | bytes 30728 | tf_op jit(solution)/shard_map/ppermute | solution.py:51
  86.6 22.9 %collective-permute-start.8 = (s16[1,576,256]{2,1,0:T(8,128)(2,1)S(1)}, s16[1,576,256]{2,1,0:T(8,128)(2,1)S(1)}, u32[]{:S(2)}, u32[]{:S(2)}) collective-permute-start(s16[1,576,256]{2,1,0:T(8,128)(2,1)S(1)} %get-tuple-element.62), channel_id=1, source_target_pairs={{1,0},{2,1},{3,2},{4,3},{5,4},{6,5},{7,6},{8,7},{9,8},{10,9},{11,1... | collective-permute-start | bytes 884744 | tf_op jit(solution)/shard_map/ppermute | solution.py:27
  92.2 18.8 %collective-permute-start.12 = (f32[2,2560]{1,0:T(2,128)S(1)}, f32[2,2560]{1,0:T(2,128)S(1)}, u32[]{:S(2)}, u32[]{:S(2)}) collective-permute-start(f32[2,2560]{1,0:T(2,128)S(1)} %pad_maximum_fusion.2), channel_id=1, source_target_pairs={{0,2},{1,3},{2,4},{3,5},{4,6},{5,7},{6,0},{7,1},{8,10},{9,11},{10,... | collective-permute-start | bytes 61448 | tf_op jit(solution)/shard_map/ppermute | solution.py:51
  107.4 27.0 %collective-permute-start.10 = (s16[1,576,256]{2,1,0:T(8,128)(2,1)}, s16[1,576,256]{2,1,0:T(8,128)(2,1)S(1)}, u32[]{:S(2)}, u32[]{:S(2)}) collective-permute-start(s16[1,576,256]{2,1,0:T(8,128)(2,1)} %get-tuple-element.64), channel_id=1, source_target_pairs={{1,0},{2,1},{3,2},{4,3},{5,4},{6,5},{7,6},{8,7},{9,8},{10,9},{11,1... | collective-permute-start | bytes 884744 | tf_op jit(solution)/shard_map/ppermute | solution.py:27
  109.5 24.9 %copy-start.17 = (f32[512,256]{1,0:T(8,128)S(1)}, f32[512,256]{1,0:T(8,128)}, u32[]{:S(2)}) copy-start(f32[512,256]{1,0:T(8,128)} %copy-done.16) | copy-start | bytes 1572868
  109.7 24.7 %collective-permute-start.9 = (s16[1,576,256]{2,1,0:T(8,128)(2,1)S(1)}, s16[1,576,256]{2,1,0:T(8,128)(2,1)S(1)}, u32[]{:S(2)}, u32[]{:S(2)}) collective-permute-start(s16[1,576,256]{2,1,0:T(8,128)(2,1)S(1)} %hop.3), channel_id=1, source_target_pairs={{2,0},{3,1},{4,2},{5,3},{6,4},{7,5},{8,6},{9,7},{10,8},{11,9},{12,... | collective-permute-start | bytes 884744 | tf_op jit(solution)/shard_map/ppermute | solution.py:27
  111.0 24.3 %collective-permute-start.13 = (f32[4,2560]{1,0:T(4,128)S(1)}, f32[4,2560]{1,0:T(4,128)S(1)}, u32[]{:S(2)}, u32[]{:S(2)}) collective-permute-start(f32[4,2560]{1,0:T(4,128)S(1)} %pad_maximum_fusion.1), channel_id=1, source_target_pairs={{0,4},{1,5},{2,6},{3,7},{4,0},{5,1},{6,2},{7,3},{8,12},{9,13},{10,... | collective-permute-start | bytes 122888 | tf_op jit(solution)/shard_map/ppermute | solution.py:51
  120.7 24.8 %collective-permute-start.7 = (s16[1,576,256]{2,1,0:T(8,128)(2,1)}, s16[1,576,256]{2,1,0:T(8,128)(2,1)S(1)}, u32[]{:S(2)}, u32[]{:S(2)}) collective-permute-start(s16[1,576,256]{2,1,0:T(8,128)(2,1)} %hop.2), channel_id=1, source_target_pairs={{2,0},{3,1},{4,2},{5,3},{6,4},{7,5},{8,6},{9,7},{10,8},{11,9},{12,... | collective-permute-start | bytes 884744 | tf_op jit(solution)/shard_map/ppermute | solution.py:27
  (8 other events, 17.3 us)

commit v7 on v6

--- a/solution.py
+++ b/solution.py
@@ -114,7 +114,7 @@
 
 def far_kernel(group, lo, q_ref, g_ref, gain_ref, k_ref, *refs):
     stats = refs[: 2 * (REACH - 1)]
-    e_ref, w_ref, dv_ref, p_low, g_all = refs[2 * (REACH - 1) :]
+    near_ref, e_ref, w_ref, dv_ref, p_low, g_all = refs[2 * (REACH - 1) :]
     rows = k_ref.shape[0]
     per = rows // BLOCK
     blocks = REACH * per
@@ -147,37 +147,37 @@
         for b in range(blocks):
             weight = shares[b] * inverse
             w_ref[0, g * blocks + b : g * blocks + b + 1, :] = weight
-            if b < per:
+            chunk, b = b // per, b % per
+            if chunk in (0, REACH - 2):
                 here = slice(b * BLOCK, (b + 1) * BLOCK)
-                p_low[here, g * rows : (g + 1) * rows] = (e_ref[g, here, :] * weight).astype(
+                e = (near_ref if chunk else e_ref)[g, here, :]
+                at = (rows if chunk else 0) + b * BLOCK
+                p_low[at : at + BLOCK, g * rows : (g + 1) * rows] = (e * weight).astype(
                     jnp.bfloat16
                 )
-    dv_ref[0, :HD, :], dv_ref[0, HD:, :] = encode(dot(p_low[...], g_all[...]).T)
-
-
-def store_parts(middle_ref, near_ref, own_ref, total, rows):
-    middle, nearest, own = (total[j * rows : (j + 1) * rows, :].T for j in range(REACH - 1))
-    middle_ref[...], own_ref[...] = middle, own
-    near_ref[:HD, :], near_ref[HD:, :] = encode(nearest)
+    dv = dot(p_low[...], g_all[...])
+    for i in range(2):
+        part = dv[i * rows : (i + 1) * rows, :].T
+        dv_ref[i, :HD, :], dv_ref[i, HD:, :] = encode(part)
 
 
 def values_kernel(group, g_ref, w_ref, *refs):
-    e_refs, dv_refs = refs[: REACH - 1], refs[REACH - 1 : 2 * (REACH - 1)]
-    p_low, g_all = refs[2 * (REACH - 1) :]
+    e_refs, dv_refs, (p_low, g_all) = refs[:2], refs[2:4], refs[4:]
     rows = g_ref.shape[0]
     per = rows // BLOCK
     blocks = REACH * per
     for g in range(group):
         g_all[g * rows : (g + 1) * rows, :] = g_ref[:, g * HD : (g + 1) * HD]
-        for j in range(REACH - 1):
+        for j, chunk in enumerate((1, REACH - 1)):
             for b in range(per):
                 here = slice(b * BLOCK, (b + 1) * BLOCK)
-                at = g * blocks + (j + 1) * per + b
+                at = g * blocks + chunk * per + b
                 probs = e_refs[j][g, here, :] * w_ref[0, at : at + 1, :]
                 there = slice(j * rows + b * BLOCK, j * rows + (b + 1) * BLOCK)
                 p_low[there, g * rows : (g + 1) * rows] = probs.astype(jnp.bfloat16)
     dv = dot(p_low[...], g_all[...])
-    store_parts(dv_refs[0], dv_refs[1].at[0], dv_refs[2], dv, rows)
+    for j in range(2):
+        dv_refs[j][...] = dv[j * rows : (j + 1) * rows, :].T
 
 
 def grads_kernel(group, rows, skip, q_ref, g_ref, gain_ref, w_ref, *refs):
@@ -220,8 +220,10 @@
         gain_out[:, cols] = jnp.sum(dscaled * q32, axis=0, keepdims=True)
     dk = dot(ds_all[...], q_all[...]) * factor
     dk_codes, dk_middle, dk_own = dk_refs
-    dk_codes[0, :HD, :], dk_codes[0, HD:, :] = encode(dk[:rows, :].T)
-    store_parts(dk_middle, dk_codes.at[1], dk_own, dk[rows:, :], rows)
+    far, middle, nearest, own = (dk[j * rows : (j + 1) * rows, :].T for j in range(REACH))
+    dk_middle[...], dk_own[...] = middle, own
+    for i, part in enumerate((far, nearest)):
+        dk_codes[i, :HD, :], dk_codes[i, HD:, :] = encode(part)
 
 
 def hop_kernel(kv_count, picks, last, *refs):
@@ -320,42 +322,41 @@
     )(queries, gain, keys)
 
 
-def far_scores(lo, queries, out_grad, gain, keys, stats):
+def far_scores(lo, queries, out_grad, gain, keys, stats, nearest):
     s = Shapes(queries, keys)
     return pl.pallas_call(
         functools.partial(far_kernel, s.group),
-        out_shape=[s.heads_array(), s.weight_array(), s.code_array()],
+        out_shape=[s.heads_array(), s.weight_array(), s.code_array(2)],
         grid_spec=pltpu.PrefetchScalarGridSpec(
             num_scalar_prefetch=1,
             grid=(s.kv_count,),
-            in_specs=[s.wide, s.wide, s.line, s.thin] + [s.stat] * len(stats),
-            out_specs=[s.heads, s.weight, s.code],
+            in_specs=[s.wide, s.wide, s.line, s.thin] + [s.stat] * len(stats) + [s.heads],
+            out_specs=[s.heads, s.weight, s.codes],
             scratch_shapes=[
-                pltpu.VMEM((s.rows, s.group * s.rows), jnp.bfloat16),
+                pltpu.VMEM((2 * s.rows, s.group * s.rows), jnp.bfloat16),
                 pltpu.VMEM((s.group * s.rows, HD), jnp.bfloat16),
             ],
         ),
         compiler_params=pltpu.CompilerParams(vmem_limit_bytes=16 * 2**20),
-        cost_estimate=s.cost(2, 1, 1),
+        cost_estimate=s.cost(3, 1, 1),
         name="far_scores",
-    )(lo, queries, out_grad, gain, keys, *stats)
+    )(lo, queries, out_grad, gain, keys, *stats, nearest)
 
 
 def near_values(queries, keys, out_grad, weights, heads):
     s = Shapes(queries, keys)
-    near = REACH - 1
     return pl.pallas_call(
         functools.partial(values_kernel, s.group),
-        out_shape=[s.part_array(), s.code_array(), s.part_array()],
+        out_shape=[s.part_array()] * 2,
         grid=(s.kv_count,),
-        in_specs=[s.wide, s.weight] + [s.heads] * near,
-        out_specs=[s.part, s.code, s.part],
+        in_specs=[s.wide, s.weight] + [s.heads] * 2,
+        out_specs=[s.part] * 2,
         scratch_shapes=[
-            pltpu.VMEM((near * s.rows, s.group * s.rows), jnp.bfloat16),
+            pltpu.VMEM((2 * s.rows, s.group * s.rows), jnp.bfloat16),
             pltpu.VMEM((s.group * s.rows, HD), jnp.bfloat16),
         ],
         compiler_params=pltpu.CompilerParams(vmem_limit_bytes=15 * 2**20),
-        cost_estimate=s.cost(1, near, 0),
+        cost_estimate=s.cost(1, 2, 0),
         name="near_values",
     )(out_grad, weights, *heads)
 
@@ -406,28 +407,27 @@
             near.insert(0, chunk_scores(q, gain, keys[0], False))
             values.insert(0, shifted(values[0], 1))
     values.insert(0, shifted(values[0], 1))
-    half = own_keys.shape[1] // HD // 2
+    most = own_keys.shape[1] // HD - 1
 
     stats = [stat for _, *pair in near for stat in pair]
-    far, weights, moved = far_scores(lo, q, do, gain, keys[0], stats)
+    far, weights, dv_codes = far_scores(lo, q, do, gain, keys[0], stats, near[1][0])
     heads = [far] + [e for e, *_ in near]
-    dv_far = shifted(moved, -1)
-    dv_middle, dv_near, dv_own = near_values(q, own_keys, do, weights, heads[1:])
-    dv_near = shifted(dv_near, -1)
-    early = attention_grads(0, half, [], q, do, gain, weights, heads, keys, values)
-    dv_middle = shifted(hop([(dv_far, 0)], dv_middle, False), -2)
+    dv_codes = shifted(dv_codes, -1)
+    dv_middle, dv_own = near_values(q, own_keys, do, weights, heads[1::2])
+    early = attention_grads(0, most, [], q, do, gain, weights, heads, keys, values)
+    dv_middle = shifted(hop([(dv_codes, 0)], dv_middle, False), -2)
     attn_out, query_grad, gain_term, dk_codes, dk_middle, dk_own = attention_grads(
-        half, half, early, q, do, gain, weights, heads, keys, values
+        most, 1, early, q, do, gain, weights, heads, keys, values
     )
     dk_codes = shifted(dk_codes, -1)
     count = lax.axis_size("ctx")
     columns = [[i + z for i in range(0, count, Z_CHIPS)] for z in range(Z_CHIPS)]
     total = gathered_sum(gain_term, "dp", lax.axis_size("dp"))
     total = gathered_sum(total, "ctx", count // Z_CHIPS, columns)
-    dk_codes, total = together((dk_codes, total))
-    dk_middle = shifted(hop([(dk_codes, 0)], dk_middle, False), -2)
+    dk_middle = hop([(dk_codes, 0)], dk_middle, False)
+    dk_middle = shifted(dk_middle, -2)
     gain_grad = ring_sum(total)
-    value_grad = hop([(dv_middle, 0), (dv_near, 0)], dv_own, True)
+    value_grad = hop([(dv_middle, 0), (dv_codes, 1)], dv_own, True)
     key_grad = hop([(dk_middle, 0), (dk_codes, 1)], dk_own, True)
     return (
         attn_out[None],

time: 147 us -> 148 us (level)
  waiting for transfers between devices: 30.9 us -> 34.5 us
  starting transfers between devices: 47.5 us -> 44.1 us
  blocking collectives: 22.4 us -> 19.6 us
  other arithmetic: 1.53 us -> 3.59 us
    ppermute x11 -> x10, starting transfers between devices: 35.1 us -> 29.3 us  [shifted(): return lax.ppermute(value, 'ctx', pairs)]
    all_to_all x2, blocking collectives: 22.4 us -> 19.6 us  [gathered_sum(): lax.all_to_all(copies, axis, 0, 0, tiled=True, axis_index_groups=groups)]
    ppermute x3, starting transfers between devices: 12.4 us -> 14.8 us  [ring_sum(): value = jnp.concatenate([value, lax.ppermute(value, 'ctx', pairs)], axis=0)]
    ppermute x3, waiting for transfers between devices: 0.01 us -> 2.22 us  [ring_sum(): value = jnp.concatenate([value, lax.ppermute(value, 'ctx', pairs)], axis=0)]
    concatenate x3, other arithmetic: 0.1 us -> 2.16 us  [ring_sum(): value = jnp.concatenate([value, lax.ppermute(value, 'ctx', pairs)], axis=0)]
    ppermute x11 -> x10, waiting for transfers between devices: 30.9 us -> 32.3 us  [shifted(): return lax.ppermute(value, 'ctx', pairs)]
  transfers between devices with their start and end apart: 14 -> 13, of which waited for: 6 -> 8; matrix products, arithmetic and copies ran while one was open for 2% -> 3% of each run, Pallas kernels for 12% -> 12%
where the time goes in v7:
time: 148 us
  starting transfers between devices  44.1 us (30%)
  waiting for transfers between devices  34.5 us (23%)
  Pallas kernels  32.6 us (22%)
  blocking collectives  19.6 us (13%)
  local copies, waits for them, and re-layouts  12.3 us (8%)
  other arithmetic  3.59 us (2%)
    ppermute x10, waiting for transfers between devices, shifted(): return lax.ppermute(value, 'ctx', pairs)  32.3 us
    ppermute x10, starting transfers between devices, shifted(): return lax.ppermute(value, 'ctx', pairs)  29.3 us
    all_to_all x2, blocking collectives, gathered_sum(): lax.all_to_all(copies, axis, 0, 0, tiled=True, axis_index_groups=groups)  19.6 us
    ppermute x3, starting transfers between devices, ring_sum(): value = jnp.concatenate([value, lax.ppermute(value, 'ctx', pairs)], axis=0)  14.8 us
    pallas_call x2, Pallas kernels, attention_grads(): pl.pallas_call(functools.partial(grads_kernel, s.group, s.rows, len(befor...  13.8 us
    unnamed x36, local copies, waits for them, and re-layouts  11.5 us
    pallas_call x3, Pallas kernels, chunk_scores(): pl.pallas_call(functools.partial(scores_kernel, s.group, own), out_shape=...  6.65 us
    pallas_call x1, Pallas kernels, far_scores(): pl.pallas_call(functools.partial(far_kernel, s.group), out_shape=[s.heads...  5.81 us
  transfers between devices with their start and end apart: 13, of which 8 were waited for; matrix products, arithmetic and copies ran while one was open for 3% of the time, Pallas kernels for 12%

profile of v7, /device:TPU:32, one launch (start us, length us, event | category | flops | bytes accessed | tf_op | source)
XLA Modules:
  0.0 147.7 jit_solution(2516557065623614232)
XLA Ops:
  0.6 3.8 %collective-permute-start = (bf16[256,512]{1,0:T(8,128)(2,1)}, bf16[256,512]{1,0:T(8,128)(2,1)S(1)}, u32[]{:S(2)}, u32[]{:S(2)}) collective-permute-start(bf16[256,512]{1,0:T(8,128)(2,1)} %bitcast.21), channel_id=1, source_target_pairs={{0,1},{1,2},{2,3},{3,4},{4,5},{5,6},{6,7},{7,8},{8,9},{9,10},{10,1... | collective-permute-start | bytes 786440 | tf_op jit(solution)/shard_map/ppermute | solution.py:27
  4.5 3.8 %collective-permute-start.3 = (bf16[256,512]{1,0:T(8,128)(2,1)}, bf16[256,512]{1,0:T(8,128)(2,1)S(1)}, u32[]{:S(2)}, u32[]{:S(2)}) collective-permute-start(bf16[256,512]{1,0:T(8,128)(2,1)} %bitcast.25), channel_id=1, source_target_pairs={{0,1},{1,2},{2,3},{3,4},{4,5},{5,6},{6,7},{7,8},{8,9},{9,10},{10,1... | collective-permute-start | bytes 786440 | tf_op jit(solution)/shard_map/ppermute | solution.py:27
  8.3 3.6 %collective-permute-done.k_ref.refs_6_ = bf16[256,512]{1,0:T(8,128)(2,1)S(1)} collective-permute-done((bf16[256,512]{1,0:T(8,128)(2,1)}, bf16[256,512]{1,0:T(8,128)(2,1)S(1)}, u32[]{:S(2)}, u32[]{:S(2)}) %collective-permute-start) | collective-permute-done | bytes 262176 | tf_op jit(solution)/shard_map/ppermute | solution.py:27
  11.9 3.8 %collective-permute-start.1 = (bf16[256,512]{1,0:T(8,128)(2,1)S(1)}, bf16[256,512]{1,0:T(8,128)(2,1)S(1)}, u32[]{:S(2)}, u32[]{:S(2)}) collective-permute-start(bf16[256,512]{1,0:T(8,128)(2,1)S(1)} %collective-permute-done.k_ref.refs_6_), channel_id=1, source_target_pairs={{0,1},{1,2},{2,3},{3,4},{4,5},{5,6},{6,7},{7,8},{8,9},{9,10},{10,1... | collective-permute-start | bytes 786440 | tf_op jit(solution)/shard_map/ppermute | solution.py:27
  17.5 3.8 %collective-permute-start.4 = (bf16[256,512]{1,0:T(8,128)(2,1)S(1)}, bf16[256,512]{1,0:T(8,128)(2,1)S(1)}, u32[]{:S(2)}, u32[]{:S(2)}) collective-permute-start(bf16[256,512]{1,0:T(8,128)(2,1)S(1)} %collective-permute-done.3.refs_10_), channel_id=1, source_target_pairs={{0,1},{1,2},{2,3},{3,4},{4,5},{5,6},{6,7},{7,8},{8,9},{9,10},{10,1... | collective-permute-start | bytes 786440 | tf_op jit(solution)/shard_map/ppermute | solution.py:27
  23.1 3.8 %collective-permute-start.2 = (bf16[256,512]{1,0:T(8,128)(2,1)S(1)}, bf16[256,512]{1,0:T(8,128)(2,1)S(1)}, u32[]{:S(2)}, u32[]{:S(2)}) collective-permute-start(bf16[256,512]{1,0:T(8,128)(2,1)S(1)} %collective-permute-done.1.k_ref.refs_5_), channel_id=1, source_target_pairs={{0,1},{1,2},{2,3},{3,4},{4,5},{5,6},{6,7},{7,8},{8,9},{9,10},{10,1... | collective-permute-start | bytes 786440 | tf_op jit(solution)/shard_map/ppermute | solution.py:27
  28.8 3.8 %collective-permute-start.5 = (bf16[256,512]{1,0:T(8,128)(2,1)S(1)}, bf16[256,512]{1,0:T(8,128)(2,1)S(1)}, u32[]{:S(2)}, u32[]{:S(2)}) collective-permute-start(bf16[256,512]{1,0:T(8,128)(2,1)S(1)} %collective-permute-done.4.refs_9_), channel_id=1, source_target_pairs={{0,1},{1,2},{2,3},{3,4},{4,5},{5,6},{6,7},{7,8},{8,9},{9,10},{10,1... | collective-permute-start | bytes 786440 | tf_op jit(solution)/shard_map/ppermute | solution.py:27
  36.2 2.3 %scores_own.1 = (f32[20,256,256]{2,1,0:T(8,128)S(1)}, f32[4,10,256]{2,1,0:T(8,128)S(1)}, f32[4,10,256]{2,1,0:T(8,128)S(1)}) custom-call(bf16[256,2560]{1,0:T(8,128)(2,1)S(1)} %bitcast.15, f32[1,2560]{1,0:T(1,128)S(1)} %broadcast_in_dim.29.gain_ref, bf16[256,512]{1,0:T(8,128)(2,1)S(1)} %bitcast.22), custom_call_target="tpu_custom_call" | custom-call | flops 335544320 | bytes 5242880 | tf_op jit(solution)/shard_map/scores_own/pallas_call | solution.py:313
  38.5 2.2 %scores.3 = (f32[20,256,256]{2,1,0:T(8,128)S(1)}, f32[4,10,256]{2,1,0:T(8,128)S(1)}, f32[4,10,256]{2,1,0:T(8,128)S(1)}) custom-call(bf16[256,2560]{1,0:T(8,128)(2,1)S(1)} %bitcast.16, f32[1,2560]{1,0:T(1,128)S(1)} %broadcast_in_dim.29.gain_ref, bf16[256,512]{1,0:T(8,128)(2,1)S(1)} %collective-permute-done.k_ref.refs_6_), custom_call_target="tpu_custom_call" | custom-call | flops 335544320 | bytes 5242880 | tf_op jit(solution)/shard_map/scores/pallas_call | solution.py:313
  40.7 2.2 %scores.2 = (f32[20,256,256]{2,1,0:T(8,128)S(1)}, f32[4,10,256]{2,1,0:T(8,128)S(1)}, f32[4,10,256]{2,1,0:T(8,128)S(1)}) custom-call(bf16[256,2560]{1,0:T(8,128)(2,1)S(1)} %bitcast.17, f32[1,2560]{1,0:T(1,128)S(1)} %broadcast_in_dim.29.gain_ref, bf16[256,512]{1,0:T(8,128)(2,1)S(1)} %collective-permute-done.1.k_ref.refs_5_), custom_call_target="tpu_custom_call" | custom-call | flops 335544320 | bytes 5242880 | tf_op jit(solution)/shard_map/scores/pallas_call | solution.py:313
  43.0 5.8 %far_scores.1 = (f32[20,256,256]{2,1,0:T(8,128)S(1)}, f32[4,40,256]{2,1,0:T(8,128)S(1)}, s16[2,576,256]{2,1,0:T(8,128)(2,1)S(1)}) custom-call(s32[2]{0:T(128)S(1)} %subtract_bitcast_fusion.lo, bf16[256,2560]{1,0:T(8,128)(2,1)S(1)} %bitcast.18, bf16[256,2560]{1,0:T(8,128)(2,1)S(1)} %bitcast.11, f32[1,2560]{1,0:T(1,128)S(1)} %broadcast_in_dim.29.gain_ref, ...), custom_call_target="tpu_custom_call" | custom-call | flops 1006632960 | bytes 5242880 | tf_op jit(solution)/shard_map/far_scores/pallas_call | solution.py:327
  49.6 10.2 %shard_map.101 = (bf16[256,2560]{1,0:T(8,128)(2,1)}, bf16[256,2560]{1,0:T(8,128)(2,1)}, f32[1,2560]{1,0:T(1,128)S(1)}, s16[2,576,256]{2,1,0:T(8,128)(2,1)S(1)}, ...) custom-call(bf16[256,2560]{1,0:T(8,128)(2,1)S(1)} %bitcast.19, bf16[256,2560]{1,0:T(8,128)(2,1)S(1)} %bitcast.12, ...), custom_call_target="tpu_custom_call" | custom-call | flops 4026531840 | bytes 15728640 | tf_op jit(solution)/shard_map/pallas_call | solution.py:368
  59.8 3.7 %shard_map.102 = (bf16[256,2560]{1,0:T(8,128)(2,1)}, bf16[256,2560]{1,0:T(8,128)(2,1)}, f32[1,2560]{1,0:T(1,128)S(1)}, s16[2,576,256]{2,1,0:T(8,128)(2,1)S(1)}, ...) custom-call(bf16[256,2560]{1,0:T(8,128)(2,1)S(1)} %bitcast.20, ...), custom_call_target="tpu_custom_call", output_to_operand_aliasing={{0}: (16, {}), {1}: (17, {}), {2}: (18, {}), {3}: (19, {}),... | custom-call | flops 1342177280 | bytes 5242880 | tf_op jit(solution)/shard_map/pallas_call | solution.py:368
  64.4 10.0 %all_to_all.10 = f32[8,1,2560]{2,1,0:T(1,128)S(1)} all-to-all(f32[8,1,2560]{2,1,0:T(1,128)S(1)} %broadcast_in_dim.35), channel_id=1, replica_groups=mesh['dp'=8,'ctx'=32] {'dp'}, dimensions={0} | all-to-all | bytes 163840 | tf_op jit(solution)/shard_map/all_to_all | solution.py:32
  74.5 9.6 %all_to_all.11 = f32[4,1,2560]{2,1,0:T(1,128)S(1)} all-to-all(f32[4,1,2560]{2,1,0:T(1,128)S(1)} %broadcast_in_dim.36), channel_id=1, replica_groups={{0,8,16,24},{1,9,17,25},{2,10,18,26},{3,11,19,27},{4,12,20,28},{5,13,21..., dimensions={0} | all-to-all | bytes 81920 | tf_op jit(solution)/shard_map/all_to_all | solution.py:32
  84.2 3.5 %collective-permute-start.10 = (f32[1,2560]{1,0:T(1,128)S(1)}, f32[1,2560]{1,0:T(1,128)S(1)}, u32[]{:S(2)}, u32[]{:S(2)}) collective-permute-start(f32[1,2560]{1,0:T(1,128)S(1)} %reduce_sum.22), channel_id=1, source_target_pairs={{0,1},{1,2},{2,3},{3,4},{4,5},{5,6},{6,7},{7,0},{8,9},{9,10},{10,1... | collective-permute-start | bytes 30728 | tf_op jit(solution)/shard_map/ppermute | solution.py:51
  92.7 5.1 %collective-permute-start.11 = (f32[2,2560]{1,0:T(2,128)}, f32[2,2560]{1,0:T(2,128)}, u32[]{:S(2)}, u32[]{:S(2)}) collective-permute-start(f32[2,2560]{1,0:T(2,128)} %pad_maximum_fusion.2), channel_id=1, source_target_pairs={{0,2},{1,3},{2,4},{3,5},{4,6},{5,7},{6,0},{7,1},{8,10},{9,11},{10,... | collective-permute-start | bytes 61448 | tf_op jit(solution)/shard_map/ppermute | solution.py:51
  97.9 2.2 %collective-permute-done.11 = f32[2,2560]{1,0:T(2,128)} collective-permute-done((f32[2,2560]{1,0:T(2,128)}, f32[2,2560]{1,0:T(2,128)}, u32[]{:S(2)}, u32[]{:S(2)}) %collective-permute-start.11) | collective-permute-done | bytes 20512 | tf_op jit(solution)/shard_map/ppermute | solution.py:51
  100.9 6.2 %collective-permute-start.12 = (f32[4,2560]{1,0:T(4,128)S(1)}, f32[4,2560]{1,0:T(4,128)S(1)}, u32[]{:S(2)}, u32[]{:S(2)}) collective-permute-start(f32[4,2560]{1,0:T(4,128)S(1)} %pad_maximum_fusion.1), channel_id=1, source_target_pairs={{0,4},{1,5},{2,6},{3,7},{4,0},{5,1},{6,2},{7,3},{8,12},{9,13},{10,... | collective-permute-start | bytes 122888 | tf_op jit(solution)/shard_map/ppermute | solution.py:51
  107.1 2.5 %copy-done.1 = f32[20,256,256]{2,1,0:T(8,128)S(1)} copy-done((f32[20,256,256]{2,1,0:T(8,128)S(1)}, f32[20,256,256]{2,1,0:T(8,128)}, u32[]{:S(2)}) %copy-start.1) | copy-done | bytes 5242904
  109.6 2.5 %copy-done.3 = f32[20,256,256]{2,1,0:T(8,128)S(1)} copy-done((f32[20,256,256]{2,1,0:T(8,128)S(1)}, f32[20,256,256]{2,1,0:T(8,128)}, u32[]{:S(2)}) %copy-start.3) | copy-done | bytes 5242904
  113.0 2.6 %near_values.1 = (f32[512,256]{1,0:T(8,128)S(1)}, f32[512,256]{1,0:T(8,128)S(1)}) custom-call(bf16[256,2560]{1,0:T(8,128)(2,1)S(1)} %bitcast.14, f32[4,40,256]{2,1,0:T(8,128)S(1)} %copy-done.8, f32[20,256,256]{2,1,0:T(8,128)S(1)} %copy-done.3, f32[20,256,256]{2,1,0:T(8,128)S(1)} %copy-done.1), custom_call_target="tpu_custom_call" | custom-call | flops 671088640 | bytes 10485760 | tf_op jit(solution)/shard_map/near_values/pallas_call | solution.py:348
  122.2 7.3 %collective-permute-done.9.refs_0_ = s16[1,576,256]{2,1,0:T(8,128)(2,1)S(1)} collective-permute-done((s16[1,576,256]{2,1,0:T(8,128)(2,1)}, s16[1,576,256]{2,1,0:T(8,128)(2,1)S(1)}, u32[]{:S(2)}, u32[]{:S(2)}) %collective-permute-start.9) | collective-permute-done | bytes 294944 | tf_op jit(solution)/shard_map/ppermute | solution.py:27
  131.5 15.2 %collective-permute-done.7.refs_0_ = s16[1,576,256]{2,1,0:T(8,128)(2,1)S(1)} collective-permute-done((s16[1,576,256]{2,1,0:T(8,128)(2,1)}, s16[1,576,256]{2,1,0:T(8,128)(2,1)S(1)}, u32[]{:S(2)}, u32[]{:S(2)}) %collective-permute-start.7) | collective-permute-done | bytes 294944 | tf_op jit(solution)/shard_map/ppermute | solution.py:27
  (64 shorter events, 27.1 us)
Async XLA Ops:
  0.6 11.3 %collective-permute-start = (bf16[256,512]{1,0:T(8,128)(2,1)}, bf16[256,512]{1,0:T(8,128)(2,1)S(1)}, u32[]{:S(2)}, u32[]{:S(2)}) collective-permute-start(bf16[256,512]{1,0:T(8,128)(2,1)} %bitcast.21), channel_id=1, source_target_pairs={{0,1},{1,2},{2,3},{3,4},{4,5},{5,6},{6,7},{7,8},{8,9},{9,10},{10,1... | collective-permute-start | bytes 786440 | tf_op jit(solution)/shard_map/ppermute | solution.py:27
  4.5 13.1 %collective-permute-start.3 = (bf16[256,512]{1,0:T(8,128)(2,1)}, bf16[256,512]{1,0:T(8,128)(2,1)S(1)}, u32[]{:S(2)}, u32[]{:S(2)}) collective-permute-start(bf16[256,512]{1,0:T(8,128)(2,1)} %bitcast.25), channel_id=1, source_target_pairs={{0,1},{1,2},{2,3},{3,4},{4,5},{5,6},{6,7},{7,8},{8,9},{9,10},{10,1... | collective-permute-start | bytes 786440 | tf_op jit(solution)/shard_map/ppermute | solution.py:27
  11.9 11.2 %collective-permute-start.1 = (bf16[256,512]{1,0:T(8,128)(2,1)S(1)}, bf16[256,512]{1,0:T(8,128)(2,1)S(1)}, u32[]{:S(2)}, u32[]{:S(2)}) collective-permute-start(bf16[256,512]{1,0:T(8,128)(2,1)S(1)} %collective-permute-done.k_ref.refs_6_), channel_id=1, source_target_pairs={{0,1},{1,2},{2,3},{3,4},{4,5},{5,6},{6,7},{7,8},{8,9},{9,10},{10,1... | collective-permute-start | bytes 786440 | tf_op jit(solution)/shard_map/ppermute | solution.py:27
  17.5 11.2 %collective-permute-start.4 = (bf16[256,512]{1,0:T(8,128)(2,1)S(1)}, bf16[256,512]{1,0:T(8,128)(2,1)S(1)}, u32[]{:S(2)}, u32[]{:S(2)}) collective-permute-start(bf16[256,512]{1,0:T(8,128)(2,1)S(1)} %collective-permute-done.3.refs_10_), channel_id=1, source_target_pairs={{0,1},{1,2},{2,3},{3,4},{4,5},{5,6},{6,7},{7,8},{8,9},{9,10},{10,1... | collective-permute-start | bytes 786440 | tf_op jit(solution)/shard_map/ppermute | solution.py:27
  23.1 19.8 %collective-permute-start.2 = (bf16[256,512]{1,0:T(8,128)(2,1)S(1)}, bf16[256,512]{1,0:T(8,128)(2,1)S(1)}, u32[]{:S(2)}, u32[]{:S(2)}) collective-permute-start(bf16[256,512]{1,0:T(8,128)(2,1)S(1)} %collective-permute-done.1.k_ref.refs_5_), channel_id=1, source_target_pairs={{0,1},{1,2},{2,3},{3,4},{4,5},{5,6},{6,7},{7,8},{8,9},{9,10},{10,1... | collective-permute-start | bytes 786440 | tf_op jit(solution)/shard_map/ppermute | solution.py:27
  28.8 20.9 %collective-permute-start.5 = (bf16[256,512]{1,0:T(8,128)(2,1)S(1)}, bf16[256,512]{1,0:T(8,128)(2,1)S(1)}, u32[]{:S(2)}, u32[]{:S(2)}) collective-permute-start(bf16[256,512]{1,0:T(8,128)(2,1)S(1)} %collective-permute-done.4.refs_9_), channel_id=1, source_target_pairs={{0,1},{1,2},{2,3},{3,4},{4,5},{5,6},{6,7},{7,8},{8,9},{9,10},{10,1... | collective-permute-start | bytes 786440 | tf_op jit(solution)/shard_map/ppermute | solution.py:27
  38.5 21.3 %copy-start = (f32[20,256,256]{2,1,0:T(8,128)}, f32[20,256,256]{2,1,0:T(8,128)S(1)}, u32[]{:S(2)}) copy-start(f32[20,256,256]{2,1,0:T(8,128)S(1)} %get-tuple-element.45.refs_3_.refs_1_) | copy-start | bytes 15728644
  38.5 4.4 %copy-start.6 = (bf16[1,256,2560]{2,1,0:T(8,128)(2,1)S(1)}, bf16[1,256,2560]{2,1,0:T(8,128)(2,1)}, u32[]{:S(2)}) copy-start(bf16[1,256,2560]{2,1,0:T(8,128)(2,1)} %param.6) | copy-start | bytes 3932164
  40.7 2.2 %copy-start.4 = (bf16[1,256,2560]{2,1,0:T(8,128)(2,1)S(1)}, bf16[1,256,2560]{2,1,0:T(8,128)(2,1)}, u32[]{:S(2)}) copy-start(bf16[1,256,2560]{2,1,0:T(8,128)(2,1)} %param.9) | copy-start | bytes 3932164
  42.9 16.9 %copy-start.2 = (f32[20,256,256]{2,1,0:T(8,128)}, f32[20,256,256]{2,1,0:T(8,128)S(1)}, u32[]{:S(2)}) copy-start(f32[20,256,256]{2,1,0:T(8,128)S(1)} %get-tuple-element.44.refs_1_.refs_0_) | copy-start | bytes 15728644
  43.0 6.7 %copy-start.10 = (bf16[1,256,512]{2,1,0:T(8,128)(2,1)S(1)}, bf16[1,256,512]{2,1,0:T(8,128)(2,1)}, u32[]{:S(2)}) copy-start(bf16[1,256,512]{2,1,0:T(8,128)(2,1)} %param.7) | copy-start | bytes 786436
  43.0 6.7 %copy-start.11 = (bf16[1,256,512]{2,1,0:T(8,128)(2,1)S(1)}, bf16[1,256,512]{2,1,0:T(8,128)(2,1)}, u32[]{:S(2)}) copy-start(bf16[1,256,512]{2,1,0:T(8,128)(2,1)} %param.8) | copy-start | bytes 786436
  49.6 10.2 %copy-start.7 = (f32[4,40,256]{2,1,0:T(8,128)}, f32[4,40,256]{2,1,0:T(8,128)S(1)}, u32[]{:S(2)}) copy-start(f32[4,40,256]{2,1,0:T(8,128)S(1)} %get-tuple-element.42.w_ref) | copy-start | bytes 491524
  84.2 7.3 %collective-permute-start.10 = (f32[1,2560]{1,0:T(1,128)S(1)}, f32[1,2560]{1,0:T(1,128)S(1)}, u32[]{:S(2)}, u32[]{:S(2)}) collective-permute-start(f32[1,2560]{1,0:T(1,128)S(1)} %reduce_sum.22), channel_id=1, source_target_pairs={{0,1},{1,2},{2,3},{3,4},{4,5},{5,6},{6,7},{7,0},{8,9},{9,10},{10,1... | collective-permute-start | bytes 30728 | tf_op jit(solution)/shard_map/ppermute | solution.py:51
  87.6 27.9 %collective-permute-start.8 = (s16[2,576,256]{2,1,0:T(8,128)(2,1)}, s16[2,576,256]{2,1,0:T(8,128)(2,1)S(1)}, u32[]{:S(2)}, u32[]{:S(2)}) collective-permute-start(s16[2,576,256]{2,1,0:T(8,128)(2,1)} %copy-done.15), channel_id=1, source_target_pairs={{1,0},{2,1},{3,2},{4,3},{5,4},{6,5},{7,6},{8,7},{9,8},{10,9},{11,1... | collective-permute-start | bytes 1769480 | tf_op jit(solution)/shard_map/ppermute | solution.py:27
  89.6 29.0 %collective-permute-start.6 = (s16[2,576,256]{2,1,0:T(8,128)(2,1)}, s16[2,576,256]{2,1,0:T(8,128)(2,1)S(1)}, u32[]{:S(2)}, u32[]{:S(2)}) collective-permute-start(s16[2,576,256]{2,1,0:T(8,128)(2,1)} %copy-done.12), channel_id=1, source_target_pairs={{1,0},{2,1},{3,2},{4,3},{5,4},{6,5},{7,6},{8,7},{9,8},{10,9},{11,1... | collective-permute-start | bytes 1769480 | tf_op jit(solution)/shard_map/ppermute | solution.py:27
  92.7 7.4 %collective-permute-start.11 = (f32[2,2560]{1,0:T(2,128)}, f32[2,2560]{1,0:T(2,128)}, u32[]{:S(2)}, u32[]{:S(2)}) collective-permute-start(f32[2,2560]{1,0:T(2,128)} %pad_maximum_fusion.2), channel_id=1, source_target_pairs={{0,2},{1,3},{2,4},{3,5},{4,6},{5,7},{6,0},{7,1},{8,10},{9,11},{10,... | collective-permute-start | bytes 61448 | tf_op jit(solution)/shard_map/ppermute | solution.py:51
  100.9 19.9 %collective-permute-start.12 = (f32[4,2560]{1,0:T(4,128)S(1)}, f32[4,2560]{1,0:T(4,128)S(1)}, u32[]{:S(2)}, u32[]{:S(2)}) collective-permute-start(f32[4,2560]{1,0:T(4,128)S(1)} %pad_maximum_fusion.1), channel_id=1, source_target_pairs={{0,4},{1,5},{2,6},{3,7},{4,0},{5,1},{6,2},{7,3},{8,12},{9,13},{10,... | collective-permute-start | bytes 122888 | tf_op jit(solution)/shard_map/ppermute | solution.py:51
  107.1 2.5 %copy-start.1 = (f32[20,256,256]{2,1,0:T(8,128)S(1)}, f32[20,256,256]{2,1,0:T(8,128)}, u32[]{:S(2)}) copy-start(f32[20,256,256]{2,1,0:T(8,128)} %copy-done) | copy-start | bytes 15728644
  109.5 2.5 %copy-start.3 = (f32[20,256,256]{2,1,0:T(8,128)S(1)}, f32[20,256,256]{2,1,0:T(8,128)}, u32[]{:S(2)}) copy-start(f32[20,256,256]{2,1,0:T(8,128)} %copy-done.2) | copy-start | bytes 15728644
  115.6 3.9 %copy-start.13 = (f32[512,256]{1,0:T(8,128)}, f32[512,256]{1,0:T(8,128)S(1)}, u32[]{:S(2)}) copy-start(f32[512,256]{1,0:T(8,128)S(1)} %get-tuple-element.59.refs_2_) | copy-start | bytes 1572868
  115.6 5.1 %copy-start.17 = (f32[1,2560]{1,0:T(1,128)S(1)}, f32[1,2560]{1,0:T(1,128)}, u32[]{:S(2)}) copy-start(f32[1,2560]{1,0:T(1,128)} %copy-done.16) | copy-start | bytes 30724
  116.5 13.0 %collective-permute-start.9 = (s16[1,576,256]{2,1,0:T(8,128)(2,1)}, s16[1,576,256]{2,1,0:T(8,128)(2,1)S(1)}, u32[]{:S(2)}, u32[]{:S(2)}) collective-permute-start(s16[1,576,256]{2,1,0:T(8,128)(2,1)} %hop.3), channel_id=1, source_target_pairs={{2,0},{3,1},{4,2},{5,3},{6,4},{7,5},{8,6},{9,7},{10,8},{11,9},{12,... | collective-permute-start | bytes 884744 | tf_op jit(solution)/shard_map/ppermute | solution.py:27
  119.4 27.3 %collective-permute-start.7 = (s16[1,576,256]{2,1,0:T(8,128)(2,1)}, s16[1,576,256]{2,1,0:T(8,128)(2,1)S(1)}, u32[]{:S(2)}, u32[]{:S(2)}) collective-permute-start(s16[1,576,256]{2,1,0:T(8,128)(2,1)} %hop.2), channel_id=1, source_target_pairs={{2,0},{3,1},{4,2},{5,3},{6,4},{7,5},{8,6},{9,7},{10,8},{11,9},{12,... | collective-permute-start | bytes 884744 | tf_op jit(solution)/shard_map/ppermute | solution.py:27
  (7 other events, 6.5 us)

commit v8 on v7

--- a/solution.py
+++ b/solution.py
@@ -48,7 +48,8 @@
         pairs = [
             (i, i - i % Z_CHIPS + (i + step) % Z_CHIPS) for i in range(count)
         ]
-        value = jnp.concatenate([value, lax.ppermute(value, "ctx", pairs)], axis=0)
+        moved = lax.ppermute(value, "ctx", pairs)
+        value = jnp.concatenate([value, moved], axis=0)
         step *= 2
     place = (lax.axis_index("ctx") % Z_CHIPS).reshape(1)
     return pl.pallas_call(
@@ -347,7 +348,7 @@
     s = Shapes(queries, keys)
     return pl.pallas_call(
         functools.partial(values_kernel, s.group),
-        out_shape=[s.part_array()] * 2,
+        out_shape=[s.part_array(), pltpu.HBM((s.kv_channels, s.rows), jnp.float32)],
         grid=(s.kv_count,),
         in_specs=[s.wide, s.weight] + [s.heads] * 2,
         out_specs=[s.part] * 2,

time: 148 us -> 149 us (level)
    unnamed x36 -> x34, local copies, waits for them, and re-layouts: 11.5 us -> 11.5 us
  transfers between devices with their start and end apart: 13 -> 13, of which waited for: 8 -> 7; matrix products, arithmetic and copies ran while one was open for 3% -> 3% of each run, Pallas kernels for 12% -> 13%
where the time goes in v8:
time: 149 us; the launch traced here: 148 us
  starting transfers between devices  44.1 us (30%)
  waiting for transfers between devices  34 us (23%)
  Pallas kernels  33.2 us (22%)
  blocking collectives  19.6 us (13%)
  local copies, waits for them, and re-layouts  12.3 us (8%)
  other arithmetic  3.59 us (2%)
    ppermute x10, waiting for transfers between devices, shifted(): return lax.ppermute(value, 'ctx', pairs)  31.7 us
    ppermute x10, starting transfers between devices, shifted(): return lax.ppermute(value, 'ctx', pairs)  29.3 us
    all_to_all x2, blocking collectives, gathered_sum(): lax.all_to_all(copies, axis, 0, 0, tiled=True, axis_index_groups=groups)  19.6 us
    ppermute x3, starting transfers between devices, ring_sum(): moved = lax.ppermute(value, 'ctx', pairs)  14.8 us
    pallas_call x2, Pallas kernels, attention_grads(): pl.pallas_call(functools.partial(grads_kernel, s.group, s.rows, len(befor...  13.8 us
    unnamed x34, local copies, waits for them, and re-layouts  11.5 us
    pallas_call x3, Pallas kernels, chunk_scores(): pl.pallas_call(functools.partial(scores_kernel, s.group, own), out_shape=...  6.65 us
    pallas_call x1, Pallas kernels, far_scores(): pl.pallas_call(functools.partial(far_kernel, s.group), out_shape=[s.heads...  5.81 us
  transfers between devices with their start and end apart: 13, of which 7 were waited for; matrix products, arithmetic and copies ran while one was open for 3% of the time, Pallas kernels for 13%

profile of v8, /device:TPU:32, one launch (start us, length us, event | category | flops | bytes accessed | tf_op | source)
XLA Modules:
  0.0 147.7 jit_solution(18186504445749705359)
XLA Ops:
  0.6 3.8 %collective-permute-start = (bf16[256,512]{1,0:T(8,128)(2,1)}, bf16[256,512]{1,0:T(8,128)(2,1)S(1)}, u32[]{:S(2)}, u32[]{:S(2)}) collective-permute-start(bf16[256,512]{1,0:T(8,128)(2,1)} %bitcast.21), channel_id=1, source_target_pairs={{0,1},{1,2},{2,3},{3,4},{4,5},{5,6},{6,7},{7,8},{8,9},{9,10},{10,1... | collective-permute-start | bytes 786440 | tf_op jit(solution)/shard_map/ppermute | solution.py:27
  4.5 3.8 %collective-permute-start.3 = (bf16[256,512]{1,0:T(8,128)(2,1)}, bf16[256,512]{1,0:T(8,128)(2,1)S(1)}, u32[]{:S(2)}, u32[]{:S(2)}) collective-permute-start(bf16[256,512]{1,0:T(8,128)(2,1)} %bitcast.25), channel_id=1, source_target_pairs={{0,1},{1,2},{2,3},{3,4},{4,5},{5,6},{6,7},{7,8},{8,9},{9,10},{10,1... | collective-permute-start | bytes 786440 | tf_op jit(solution)/shard_map/ppermute | solution.py:27
  8.3 3.6 %collective-permute-done.k_ref.refs_6_ = bf16[256,512]{1,0:T(8,128)(2,1)S(1)} collective-permute-done((bf16[256,512]{1,0:T(8,128)(2,1)}, bf16[256,512]{1,0:T(8,128)(2,1)S(1)}, u32[]{:S(2)}, u32[]{:S(2)}) %collective-permute-start) | collective-permute-done | bytes 262176 | tf_op jit(solution)/shard_map/ppermute | solution.py:27
  11.9 3.8 %collective-permute-start.1 = (bf16[256,512]{1,0:T(8,128)(2,1)S(1)}, bf16[256,512]{1,0:T(8,128)(2,1)S(1)}, u32[]{:S(2)}, u32[]{:S(2)}) collective-permute-start(bf16[256,512]{1,0:T(8,128)(2,1)S(1)} %collective-permute-done.k_ref.refs_6_), channel_id=1, source_target_pairs={{0,1},{1,2},{2,3},{3,4},{4,5},{5,6},{6,7},{7,8},{8,9},{9,10},{10,1... | collective-permute-start | bytes 786440 | tf_op jit(solution)/shard_map/ppermute | solution.py:27
  17.5 3.8 %collective-permute-start.4 = (bf16[256,512]{1,0:T(8,128)(2,1)S(1)}, bf16[256,512]{1,0:T(8,128)(2,1)S(1)}, u32[]{:S(2)}, u32[]{:S(2)}) collective-permute-start(bf16[256,512]{1,0:T(8,128)(2,1)S(1)} %collective-permute-done.3.refs_10_), channel_id=1, source_target_pairs={{0,1},{1,2},{2,3},{3,4},{4,5},{5,6},{6,7},{7,8},{8,9},{9,10},{10,1... | collective-permute-start | bytes 786440 | tf_op jit(solution)/shard_map/ppermute | solution.py:27
  23.1 3.8 %collective-permute-start.2 = (bf16[256,512]{1,0:T(8,128)(2,1)S(1)}, bf16[256,512]{1,0:T(8,128)(2,1)S(1)}, u32[]{:S(2)}, u32[]{:S(2)}) collective-permute-start(bf16[256,512]{1,0:T(8,128)(2,1)S(1)} %collective-permute-done.1.k_ref.refs_5_), channel_id=1, source_target_pairs={{0,1},{1,2},{2,3},{3,4},{4,5},{5,6},{6,7},{7,8},{8,9},{9,10},{10,1... | collective-permute-start | bytes 786440 | tf_op jit(solution)/shard_map/ppermute | solution.py:27
  28.8 3.8 %collective-permute-start.5 = (bf16[256,512]{1,0:T(8,128)(2,1)S(1)}, bf16[256,512]{1,0:T(8,128)(2,1)S(1)}, u32[]{:S(2)}, u32[]{:S(2)}) collective-permute-start(bf16[256,512]{1,0:T(8,128)(2,1)S(1)} %collective-permute-done.4.refs_9_), channel_id=1, source_target_pairs={{0,1},{1,2},{2,3},{3,4},{4,5},{5,6},{6,7},{7,8},{8,9},{9,10},{10,1... | collective-permute-start | bytes 786440 | tf_op jit(solution)/shard_map/ppermute | solution.py:27
  36.2 2.3 %scores_own.1 = (f32[20,256,256]{2,1,0:T(8,128)S(1)}, f32[4,10,256]{2,1,0:T(8,128)S(1)}, f32[4,10,256]{2,1,0:T(8,128)S(1)}) custom-call(bf16[256,2560]{1,0:T(8,128)(2,1)S(1)} %bitcast.15, f32[1,2560]{1,0:T(1,128)S(1)} %broadcast_in_dim.29.gain_ref, bf16[256,512]{1,0:T(8,128)(2,1)S(1)} %bitcast.22), custom_call_target="tpu_custom_call" | custom-call | flops 335544320 | bytes 5242880 | tf_op jit(solution)/shard_map/scores_own/pallas_call | solution.py:314
  38.5 2.2 %scores.3 = (f32[20,256,256]{2,1,0:T(8,128)S(1)}, f32[4,10,256]{2,1,0:T(8,128)S(1)}, f32[4,10,256]{2,1,0:T(8,128)S(1)}) custom-call(bf16[256,2560]{1,0:T(8,128)(2,1)S(1)} %bitcast.16, f32[1,2560]{1,0:T(1,128)S(1)} %broadcast_in_dim.29.gain_ref, bf16[256,512]{1,0:T(8,128)(2,1)S(1)} %collective-permute-done.k_ref.refs_6_), custom_call_target="tpu_custom_call" | custom-call | flops 335544320 | bytes 5242880 | tf_op jit(solution)/shard_map/scores/pallas_call | solution.py:314
  40.7 2.2 %scores.2 = (f32[20,256,256]{2,1,0:T(8,128)S(1)}, f32[4,10,256]{2,1,0:T(8,128)S(1)}, f32[4,10,256]{2,1,0:T(8,128)S(1)}) custom-call(bf16[256,2560]{1,0:T(8,128)(2,1)S(1)} %bitcast.17, f32[1,2560]{1,0:T(1,128)S(1)} %broadcast_in_dim.29.gain_ref, bf16[256,512]{1,0:T(8,128)(2,1)S(1)} %collective-permute-done.1.k_ref.refs_5_), custom_call_target="tpu_custom_call" | custom-call | flops 335544320 | bytes 5242880 | tf_op jit(solution)/shard_map/scores/pallas_call | solution.py:314
  43.0 5.8 %far_scores.1 = (f32[20,256,256]{2,1,0:T(8,128)S(1)}, f32[4,40,256]{2,1,0:T(8,128)S(1)}, s16[2,576,256]{2,1,0:T(8,128)(2,1)S(1)}) custom-call(s32[2]{0:T(128)S(1)} %subtract_bitcast_fusion.lo, bf16[256,2560]{1,0:T(8,128)(2,1)S(1)} %bitcast.18, bf16[256,2560]{1,0:T(8,128)(2,1)S(1)} %bitcast.11, f32[1,2560]{1,0:T(1,128)S(1)} %broadcast_in_dim.29.gain_ref, ...), custom_call_target="tpu_custom_call" | custom-call | flops 1006632960 | bytes 5242880 | tf_op jit(solution)/shard_map/far_scores/pallas_call | solution.py:328
  49.6 10.2 %shard_map.101 = (bf16[256,2560]{1,0:T(8,128)(2,1)}, bf16[256,2560]{1,0:T(8,128)(2,1)}, f32[1,2560]{1,0:T(1,128)S(1)}, s16[2,576,256]{2,1,0:T(8,128)(2,1)S(1)}, ...) custom-call(bf16[256,2560]{1,0:T(8,128)(2,1)S(1)} %bitcast.19, bf16[256,2560]{1,0:T(8,128)(2,1)S(1)} %bitcast.12, ...), custom_call_target="tpu_custom_call" | custom-call | flops 4026531840 | bytes 15728640 | tf_op jit(solution)/shard_map/pallas_call | solution.py:369
  59.8 3.7 %shard_map.102 = (bf16[256,2560]{1,0:T(8,128)(2,1)}, bf16[256,2560]{1,0:T(8,128)(2,1)}, f32[1,2560]{1,0:T(1,128)S(1)}, s16[2,576,256]{2,1,0:T(8,128)(2,1)S(1)}, ...) custom-call(bf16[256,2560]{1,0:T(8,128)(2,1)S(1)} %bitcast.20, ...), custom_call_target="tpu_custom_call", output_to_operand_aliasing={{0}: (16, {}), {1}: (17, {}), {2}: (18, {}), {3}: (19, {}),... | custom-call | flops 1342177280 | bytes 5242880 | tf_op jit(solution)/shard_map/pallas_call | solution.py:369
  64.4 10.0 %all_to_all.10 = f32[8,1,2560]{2,1,0:T(1,128)S(1)} all-to-all(f32[8,1,2560]{2,1,0:T(1,128)S(1)} %broadcast_in_dim.35), channel_id=1, replica_groups=mesh['dp'=8,'ctx'=32] {'dp'}, dimensions={0} | all-to-all | bytes 163840 | tf_op jit(solution)/shard_map/all_to_all | solution.py:32
  74.5 9.6 %all_to_all.11 = f32[4,1,2560]{2,1,0:T(1,128)S(1)} all-to-all(f32[4,1,2560]{2,1,0:T(1,128)S(1)} %broadcast_in_dim.36), channel_id=1, replica_groups={{0,8,16,24},{1,9,17,25},{2,10,18,26},{3,11,19,27},{4,12,20,28},{5,13,21..., dimensions={0} | all-to-all | bytes 81920 | tf_op jit(solution)/shard_map/all_to_all | solution.py:32
  84.2 3.5 %collective-permute-start.10 = (f32[1,2560]{1,0:T(1,128)S(1)}, f32[1,2560]{1,0:T(1,128)S(1)}, u32[]{:S(2)}, u32[]{:S(2)}) collective-permute-start(f32[1,2560]{1,0:T(1,128)S(1)} %reduce_sum.22), channel_id=1, source_target_pairs={{0,1},{1,2},{2,3},{3,4},{4,5},{5,6},{6,7},{7,0},{8,9},{9,10},{10,1... | collective-permute-start | bytes 30728 | tf_op jit(solution)/shard_map/ppermute | solution.py:51
  92.7 5.1 %collective-permute-start.11 = (f32[2,2560]{1,0:T(2,128)}, f32[2,2560]{1,0:T(2,128)}, u32[]{:S(2)}, u32[]{:S(2)}) collective-permute-start(f32[2,2560]{1,0:T(2,128)} %pad_maximum_fusion.2), channel_id=1, source_target_pairs={{0,2},{1,3},{2,4},{3,5},{4,6},{5,7},{6,0},{7,1},{8,10},{9,11},{10,... | collective-permute-start | bytes 61448 | tf_op jit(solution)/shard_map/ppermute | solution.py:51
  97.9 2.2 %collective-permute-done.11 = f32[2,2560]{1,0:T(2,128)} collective-permute-done((f32[2,2560]{1,0:T(2,128)}, f32[2,2560]{1,0:T(2,128)}, u32[]{:S(2)}, u32[]{:S(2)}) %collective-permute-start.11) | collective-permute-done | bytes 20512 | tf_op jit(solution)/shard_map/ppermute | solution.py:51
  100.9 6.2 %collective-permute-start.12 = (f32[4,2560]{1,0:T(4,128)S(1)}, f32[4,2560]{1,0:T(4,128)S(1)}, u32[]{:S(2)}, u32[]{:S(2)}) collective-permute-start(f32[4,2560]{1,0:T(4,128)S(1)} %pad_maximum_fusion.1), channel_id=1, source_target_pairs={{0,4},{1,5},{2,6},{3,7},{4,0},{5,1},{6,2},{7,3},{8,12},{9,13},{10,... | collective-permute-start | bytes 122888 | tf_op jit(solution)/shard_map/ppermute | solution.py:51
  107.1 2.5 %copy-done.1 = f32[20,256,256]{2,1,0:T(8,128)S(1)} copy-done((f32[20,256,256]{2,1,0:T(8,128)S(1)}, f32[20,256,256]{2,1,0:T(8,128)}, u32[]{:S(2)}) %copy-start.1) | copy-done | bytes 5242904
  109.5 2.5 %copy-done.3 = f32[20,256,256]{2,1,0:T(8,128)S(1)} copy-done((f32[20,256,256]{2,1,0:T(8,128)S(1)}, f32[20,256,256]{2,1,0:T(8,128)}, u32[]{:S(2)}) %copy-start.3) | copy-done | bytes 5242904
  112.9 3.3 %near_values.1 = (f32[512,256]{1,0:T(8,128)S(1)}, f32[512,256]{1,0:T(8,128)}) custom-call(bf16[256,2560]{1,0:T(8,128)(2,1)S(1)} %bitcast.14, f32[4,40,256]{2,1,0:T(8,128)S(1)} %copy-done.8, f32[20,256,256]{2,1,0:T(8,128)S(1)} %copy-done.3, f32[20,256,256]{2,1,0:T(8,128)S(1)} %copy-done.1), custom_call_target="tpu_custom_call" | custom-call | flops 671088640 | bytes 10485760 | tf_op jit(solution)/shard_map/near_values/pallas_call | solution.py:349
  122.1 8.0 %collective-permute-done.9.refs_0_ = s16[1,576,256]{2,1,0:T(8,128)(2,1)S(1)} collective-permute-done((s16[1,576,256]{2,1,0:T(8,128)(2,1)}, s16[1,576,256]{2,1,0:T(8,128)(2,1)S(1)}, u32[]{:S(2)}, u32[]{:S(2)}) %collective-permute-start.9) | collective-permute-done | bytes 294944 | tf_op jit(solution)/shard_map/ppermute | solution.py:27
  132.0 14.7 %collective-permute-done.7.refs_0_ = s16[1,576,256]{2,1,0:T(8,128)(2,1)S(1)} collective-permute-done((s16[1,576,256]{2,1,0:T(8,128)(2,1)}, s16[1,576,256]{2,1,0:T(8,128)(2,1)S(1)}, u32[]{:S(2)}, u32[]{:S(2)}) %collective-permute-start.7) | collective-permute-done | bytes 294944 | tf_op jit(solution)/shard_map/ppermute | solution.py:27
  (62 shorter events, 26.4 us)
Async XLA Ops:
  0.6 11.3 %collective-permute-start = (bf16[256,512]{1,0:T(8,128)(2,1)}, bf16[256,512]{1,0:T(8,128)(2,1)S(1)}, u32[]{:S(2)}, u32[]{:S(2)}) collective-permute-start(bf16[256,512]{1,0:T(8,128)(2,1)} %bitcast.21), channel_id=1, source_target_pairs={{0,1},{1,2},{2,3},{3,4},{4,5},{5,6},{6,7},{7,8},{8,9},{9,10},{10,1... | collective-permute-start | bytes 786440 | tf_op jit(solution)/shard_map/ppermute | solution.py:27
  4.5 13.1 %collective-permute-start.3 = (bf16[256,512]{1,0:T(8,128)(2,1)}, bf16[256,512]{1,0:T(8,128)(2,1)S(1)}, u32[]{:S(2)}, u32[]{:S(2)}) collective-permute-start(bf16[256,512]{1,0:T(8,128)(2,1)} %bitcast.25), channel_id=1, source_target_pairs={{0,1},{1,2},{2,3},{3,4},{4,5},{5,6},{6,7},{7,8},{8,9},{9,10},{10,1... | collective-permute-start | bytes 786440 | tf_op jit(solution)/shard_map/ppermute | solution.py:27
  11.9 11.2 %collective-permute-start.1 = (bf16[256,512]{1,0:T(8,128)(2,1)S(1)}, bf16[256,512]{1,0:T(8,128)(2,1)S(1)}, u32[]{:S(2)}, u32[]{:S(2)}) collective-permute-start(bf16[256,512]{1,0:T(8,128)(2,1)S(1)} %collective-permute-done.k_ref.refs_6_), channel_id=1, source_target_pairs={{0,1},{1,2},{2,3},{3,4},{4,5},{5,6},{6,7},{7,8},{8,9},{9,10},{10,1... | collective-permute-start | bytes 786440 | tf_op jit(solution)/shard_map/ppermute | solution.py:27
  17.5 11.2 %collective-permute-start.4 = (bf16[256,512]{1,0:T(8,128)(2,1)S(1)}, bf16[256,512]{1,0:T(8,128)(2,1)S(1)}, u32[]{:S(2)}, u32[]{:S(2)}) collective-permute-start(bf16[256,512]{1,0:T(8,128)(2,1)S(1)} %collective-permute-done.3.refs_10_), channel_id=1, source_target_pairs={{0,1},{1,2},{2,3},{3,4},{4,5},{5,6},{6,7},{7,8},{8,9},{9,10},{10,1... | collective-permute-start | bytes 786440 | tf_op jit(solution)/shard_map/ppermute | solution.py:27
  23.1 19.8 %collective-permute-start.2 = (bf16[256,512]{1,0:T(8,128)(2,1)S(1)}, bf16[256,512]{1,0:T(8,128)(2,1)S(1)}, u32[]{:S(2)}, u32[]{:S(2)}) collective-permute-start(bf16[256,512]{1,0:T(8,128)(2,1)S(1)} %collective-permute-done.1.k_ref.refs_5_), channel_id=1, source_target_pairs={{0,1},{1,2},{2,3},{3,4},{4,5},{5,6},{6,7},{7,8},{8,9},{9,10},{10,1... | collective-permute-start | bytes 786440 | tf_op jit(solution)/shard_map/ppermute | solution.py:27
  28.8 20.9 %collective-permute-start.5 = (bf16[256,512]{1,0:T(8,128)(2,1)S(1)}, bf16[256,512]{1,0:T(8,128)(2,1)S(1)}, u32[]{:S(2)}, u32[]{:S(2)}) collective-permute-start(bf16[256,512]{1,0:T(8,128)(2,1)S(1)} %collective-permute-done.4.refs_9_), channel_id=1, source_target_pairs={{0,1},{1,2},{2,3},{3,4},{4,5},{5,6},{6,7},{7,8},{8,9},{9,10},{10,1... | collective-permute-start | bytes 786440 | tf_op jit(solution)/shard_map/ppermute | solution.py:27
  34.0 1.3 copy-start.5
  38.5 21.3 %copy-start = (f32[20,256,256]{2,1,0:T(8,128)}, f32[20,256,256]{2,1,0:T(8,128)S(1)}, u32[]{:S(2)}) copy-start(f32[20,256,256]{2,1,0:T(8,128)S(1)} %get-tuple-element.45.refs_3_.refs_1_) | copy-start | bytes 15728644
  38.5 4.4 %copy-start.6 = (bf16[1,256,2560]{2,1,0:T(8,128)(2,1)S(1)}, bf16[1,256,2560]{2,1,0:T(8,128)(2,1)}, u32[]{:S(2)}) copy-start(bf16[1,256,2560]{2,1,0:T(8,128)(2,1)} %param.6) | copy-start | bytes 3932164
  40.7 2.2 %copy-start.4 = (bf16[1,256,2560]{2,1,0:T(8,128)(2,1)S(1)}, bf16[1,256,2560]{2,1,0:T(8,128)(2,1)}, u32[]{:S(2)}) copy-start(bf16[1,256,2560]{2,1,0:T(8,128)(2,1)} %param.9) | copy-start | bytes 3932164
  42.9 16.9 %copy-start.2 = (f32[20,256,256]{2,1,0:T(8,128)}, f32[20,256,256]{2,1,0:T(8,128)S(1)}, u32[]{:S(2)}) copy-start(f32[20,256,256]{2,1,0:T(8,128)S(1)} %get-tuple-element.44.refs_1_.refs_0_) | copy-start | bytes 15728644
  43.0 6.7 %copy-start.10 = (bf16[1,256,512]{2,1,0:T(8,128)(2,1)S(1)}, bf16[1,256,512]{2,1,0:T(8,128)(2,1)}, u32[]{:S(2)}) copy-start(bf16[1,256,512]{2,1,0:T(8,128)(2,1)} %param.7) | copy-start | bytes 786436
  43.0 6.6 %copy-start.11 = (bf16[1,256,512]{2,1,0:T(8,128)(2,1)S(1)}, bf16[1,256,512]{2,1,0:T(8,128)(2,1)}, u32[]{:S(2)}) copy-start(bf16[1,256,512]{2,1,0:T(8,128)(2,1)} %param.8) | copy-start | bytes 786436
  49.6 10.2 %copy-start.7 = (f32[4,40,256]{2,1,0:T(8,128)}, f32[4,40,256]{2,1,0:T(8,128)S(1)}, u32[]{:S(2)}) copy-start(f32[4,40,256]{2,1,0:T(8,128)S(1)} %get-tuple-element.42.w_ref) | copy-start | bytes 491524
  84.2 7.3 %collective-permute-start.10 = (f32[1,2560]{1,0:T(1,128)S(1)}, f32[1,2560]{1,0:T(1,128)S(1)}, u32[]{:S(2)}, u32[]{:S(2)}) collective-permute-start(f32[1,2560]{1,0:T(1,128)S(1)} %reduce_sum.22), channel_id=1, source_target_pairs={{0,1},{1,2},{2,3},{3,4},{4,5},{5,6},{6,7},{7,0},{8,9},{9,10},{10,1... | collective-permute-start | bytes 30728 | tf_op jit(solution)/shard_map/ppermute | solution.py:51
  87.6 28.6 %collective-permute-start.8 = (s16[2,576,256]{2,1,0:T(8,128)(2,1)}, s16[2,576,256]{2,1,0:T(8,128)(2,1)S(1)}, u32[]{:S(2)}, u32[]{:S(2)}) collective-permute-start(s16[2,576,256]{2,1,0:T(8,128)(2,1)} %copy-done.14), channel_id=1, source_target_pairs={{1,0},{2,1},{3,2},{4,3},{5,4},{6,5},{7,6},{8,7},{9,8},{10,9},{11,1... | collective-permute-start | bytes 1769480 | tf_op jit(solution)/shard_map/ppermute | solution.py:27
  89.6 28.9 %collective-permute-start.6 = (s16[2,576,256]{2,1,0:T(8,128)(2,1)}, s16[2,576,256]{2,1,0:T(8,128)(2,1)S(1)}, u32[]{:S(2)}, u32[]{:S(2)}) collective-permute-start(s16[2,576,256]{2,1,0:T(8,128)(2,1)} %copy-done.12), channel_id=1, source_target_pairs={{1,0},{2,1},{3,2},{4,3},{5,4},{6,5},{7,6},{8,7},{9,8},{10,9},{11,1... | collective-permute-start | bytes 1769480 | tf_op jit(solution)/shard_map/ppermute | solution.py:27
  92.7 7.4 %collective-permute-start.11 = (f32[2,2560]{1,0:T(2,128)}, f32[2,2560]{1,0:T(2,128)}, u32[]{:S(2)}, u32[]{:S(2)}) collective-permute-start(f32[2,2560]{1,0:T(2,128)} %pad_maximum_fusion.2), channel_id=1, source_target_pairs={{0,2},{1,3},{2,4},{3,5},{4,6},{5,7},{6,0},{7,1},{8,10},{9,11},{10,... | collective-permute-start | bytes 61448 | tf_op jit(solution)/shard_map/ppermute | solution.py:51
  100.9 19.8 %collective-permute-start.12 = (f32[4,2560]{1,0:T(4,128)S(1)}, f32[4,2560]{1,0:T(4,128)S(1)}, u32[]{:S(2)}, u32[]{:S(2)}) collective-permute-start(f32[4,2560]{1,0:T(4,128)S(1)} %pad_maximum_fusion.1), channel_id=1, source_target_pairs={{0,4},{1,5},{2,6},{3,7},{4,0},{5,1},{6,2},{7,3},{8,12},{9,13},{10,... | collective-permute-start | bytes 122888 | tf_op jit(solution)/shard_map/ppermute | solution.py:51
  107.1 2.5 %copy-start.1 = (f32[20,256,256]{2,1,0:T(8,128)S(1)}, f32[20,256,256]{2,1,0:T(8,128)}, u32[]{:S(2)}) copy-start(f32[20,256,256]{2,1,0:T(8,128)} %copy-done) | copy-start | bytes 15728644
  109.5 2.5 %copy-start.3 = (f32[20,256,256]{2,1,0:T(8,128)S(1)}, f32[20,256,256]{2,1,0:T(8,128)}, u32[]{:S(2)}) copy-start(f32[20,256,256]{2,1,0:T(8,128)} %copy-done.2) | copy-start | bytes 15728644
  116.2 4.4 %copy-start.16 = (f32[1,2560]{1,0:T(1,128)S(1)}, f32[1,2560]{1,0:T(1,128)}, u32[]{:S(2)}) copy-start(f32[1,2560]{1,0:T(1,128)} %copy-done.15) | copy-start | bytes 30724
  117.1 13.0 %collective-permute-start.9 = (s16[1,576,256]{2,1,0:T(8,128)(2,1)}, s16[1,576,256]{2,1,0:T(8,128)(2,1)S(1)}, u32[]{:S(2)}, u32[]{:S(2)}) collective-permute-start(s16[1,576,256]{2,1,0:T(8,128)(2,1)} %hop.3), channel_id=1, source_target_pairs={{2,0},{3,1},{4,2},{5,3},{6,4},{7,5},{8,6},{9,7},{10,8},{11,9},{12,... | collective-permute-start | bytes 884744 | tf_op jit(solution)/shard_map/ppermute | solution.py:27
  119.3 27.4 %collective-permute-start.7 = (s16[1,576,256]{2,1,0:T(8,128)(2,1)}, s16[1,576,256]{2,1,0:T(8,128)(2,1)S(1)}, u32[]{:S(2)}, u32[]{:S(2)}) collective-permute-start(s16[1,576,256]{2,1,0:T(8,128)(2,1)} %hop.2), channel_id=1, source_target_pairs={{2,0},{3,1},{4,2},{5,3},{6,4},{7,5},{8,6},{9,7},{10,8},{11,9},{12,... | collective-permute-start | bytes 884744 | tf_op jit(solution)/shard_map/ppermute | solution.py:27
  (6 other events, 5.2 us)
